TPU v7x, 256 devices: a whole 4x4x8 slice. The times are simulated.
256 devices in a mesh: bulk: 64 (over z, x, core), slab: 4 (over y).
Axes of the slice: x: 4, y: 4, z: 8, core: 2. Of those that a mesh axis runs over, the one named last changes fastest.
Arguments:
- pressure: float32 [1024, 256, 128], P('bulk', 'slab'), may hold values from -12 to 12
- rhs: float32 [1024, 256, 128], P('bulk', 'slab'), may hold values from -48 to 48
- kappa: float32 [1024, 256, 128], P('bulk', 'slab'), may hold values from 0.5 to 8
- owner: int32 [4, 64, 1024, 1], P('slab', 'bulk'), may hold values from 0 to 63; in each aligned block of 1024 rows (0 to 1023, 1024 to 2047, ..., all dimensions but the last counted through in order) at most 40 rows name the same one
- coarse_row: int32 [4, 64, 1024], P('slab', 'bulk'), may hold values from 0 to 127
- coarse_leak: float32 [4, 8192, 128], P('slab', 'bulk'), may hold values from 1 to 16
- coarse_link: float32 [4, 8192, 128], P('slab', 'bulk'), may hold values from 1 to 16
Outputs:
- pressure_out: float32 [1024, 256, 128], P('bulk', 'slab')
Inputs may be any that keep to these rules, and one draw needn't show every extreme that they name: Among the 1024 fine rows of one device, at most 40 name the same owner; in every draw some device gives exactly 40 rows to some owner.
All inputs are finite; a program needn't handle non-finite values.
Results may differ from a plain program's by a relative error of at most 0.00002.
Values sent between devices are 32-bit elements; how exact they have to be, the bound alone decides.
No kernel may reach another device: no remote copies, remote signals or barrier semaphores. Data moves between devices by JAX's collectives and lax.ppermute only.
A program may use at most 64 MiB of HBM per device.

v0:
```python
import jax
import jax.numpy as jnp
from jax import lax
from jax.sharding import PartitionSpec as P

SWEEPS = 2
COARSE_SWEEPS = 3


damping = 0.8


def extended(block, sides, width):
    for axis, dim in sides:
        count = lax.axis_size(axis)
        forward = [(i, i + 1) for i in range(count - 1)]
        backward = [(target, source) for source, target in forward]
        low = lax.ppermute(
            lax.slice_in_dim(block, block.shape[dim] - width, None, axis=dim), axis, forward
        )
        high = lax.ppermute(lax.slice_in_dim(block, 0, width, axis=dim), axis, backward)
        block = jnp.concatenate([low, block, high], axis=dim)
    return block


def shift_up(values):
    return jnp.concatenate([values[..., 1:], jnp.zeros_like(values[..., :1])], axis=-1)


def shift_down(values):
    return jnp.concatenate([jnp.zeros_like(values[..., :1]), values[..., :-1]], axis=-1)


def face_set(kappa, kappa_rims):
    west_face = 0.5 * (kappa + kappa_rims[:-2, 1:-1])
    east_face = 0.5 * (kappa + kappa_rims[2:, 1:-1])
    south_face = 0.5 * (kappa + kappa_rims[1:-1, :-2])
    north_face = 0.5 * (kappa + kappa_rims[1:-1, 2:])
    lower_face = 0.5 * (kappa + shift_down(kappa))
    upper_face = 0.5 * (kappa + shift_up(kappa))
    faces = (west_face, east_face, south_face, north_face, lower_face, upper_face)
    diagonal = west_face + east_face + south_face + north_face + lower_face + upper_face
    return (faces, diagonal)


def operate(field, faces):
    field_rims = extended(field, (("bulk", 0), ("slab", 1)), 1)
    west_face, east_face, south_face, north_face, lower_face, upper_face = faces
    result = west_face * (field - field_rims[:-2, 1:-1]) + east_face * (
        field - field_rims[2:, 1:-1]
    )
    result = (
        result
        + south_face * (field - field_rims[1:-1, :-2])
        + north_face * (field - field_rims[1:-1, 2:])
    )
    result = (
        result + lower_face * (field - shift_down(field)) + upper_face * (field - shift_up(field))
    )
    return result


def coarse_smooth(coarse_rhs, leak, link):
    link_below = shift_down(link)
    cdiag = leak + link + link_below
    correction = jnp.zeros_like(coarse_rhs)
    for sweep_index in range(COARSE_SWEEPS):
        applied = (
            leak * correction
            + link * (correction - shift_up(correction))
            + link_below * (correction - shift_down(correction))
        )
        correction = correction + damping * (coarse_rhs - applied) / cdiag
    return correction


def per_device(pressure, rhs, kappa, owner, coarse_row, coarse_leak, coarse_link):
    kappa_rims = extended(kappa, (("bulk", 0), ("slab", 1)), 1)
    faces, diagonal = face_set(kappa, kappa_rims)
    field = pressure
    for sweep_index in range(SWEEPS):
        field = field + damping * (rhs - operate(field, faces)) / diagonal
    residual = rhs - operate(field, faces)
    cells_x, cells_y, depth_cells = residual.shape
    row_total = cells_x * cells_y
    residual_rows = residual.reshape(row_total, depth_cells)
    owners = owner.reshape(row_total)
    targets = coarse_row.reshape(row_total)
    leak = coarse_leak[0]
    link = coarse_link[0]
    coarse_count = leak.shape[0]
    coarse_index = owners * coarse_count + targets
    first_row = jnp.int32(0)
    inside = (coarse_index >= first_row) & (
        coarse_index < first_row + coarse_count * lax.axis_size("bulk")
    )
    local_index = jnp.where(inside, coarse_index, coarse_count * lax.axis_size("bulk"))
    coarse_rhs = lax.psum_scatter(
        jax.ops.segment_sum(
            residual_rows, local_index, num_segments=coarse_count * lax.axis_size("bulk")
        ),
        "bulk",
        scatter_dimension=0,
        tiled=True,
    )
    correction = coarse_smooth(coarse_rhs, leak, link)
    all_corrections = lax.all_gather(correction, "bulk", axis=0, tiled=True)
    fine_correction = all_corrections[coarse_index]
    field = field + fine_correction.reshape(cells_x, cells_y, depth_cells)
    for sweep_index in range(SWEEPS):
        field = field + damping * (rhs - operate(field, faces)) / diagonal
    return field


def solution(mesh):
    return jax.shard_map(
        per_device,
        mesh=mesh,
        in_specs=(
            P("bulk", "slab", None),
            P("bulk", "slab", None),
            P("bulk", "slab", None),
            P("slab", "bulk", None, None),
            P("slab", "bulk", None),
            P("slab", "bulk", None),
            P("slab", "bulk", None),
        ),
        out_specs=P("bulk", "slab", None),
        check_vma=False,
    )
```

profile of v0, /device:TPU:103, one launch (start us, length us, event | category | flops | bytes accessed | tf_op | source)
XLA Modules:
  0.0 371.2 jit_solution(16211809709474440119)
XLA Ops:
  7.4 5.2 %collective-permute-start = (f32[1,64,128]{2,1,0:T(8,128)S(1)}, f32[1,64,128]{2,1,0:T(8,128)S(1)}, u32[]{:S(2)}, u32[]{:S(2)}) collective-permute-start(f32[1,64,128]{2,1,0:T(8,128)S(1)} %get-tuple-element.41), channel_id=1, source_target_pairs={{0,4},{4,8},{8,12},{12,16},{16,20},{20,24},{24,28},{28,32},{32,36}... | collective-permute-start | bytes 98312 | tf_op jit(solution)/shard_map/ppermute | solution.py:18
  15.4 7.0 %collective-permute-start.1 = (f32[1,64,128]{2,1,0:T(8,128)S(1)}, f32[1,64,128]{2,1,0:T(8,128)S(1)}, u32[]{:S(2)}, u32[]{:S(2)}) collective-permute-start(f32[1,64,128]{2,1,0:T(8,128)S(1)} %get-tuple-element.45), channel_id=1, source_target_pairs={{0,4},{4,8},{8,12},{12,16},{16,20},{20,24},{24,28},{28,32},{32,36}... | collective-permute-start | bytes 98312 | tf_op jit(solution)/shard_map/ppermute | solution.py:18
  25.4 5.5 %collective-permute-done.2 = f32[1,64,128]{2,1,0:T(8,128)S(1)} collective-permute-done((f32[1,64,128]{2,1,0:T(8,128)S(1)}, f32[1,64,128]{2,1,0:T(8,128)S(1)}, u32[]{:S(2)}, u32[]{:S(2)}) %collective-permute-start.2) | collective-permute-done | bytes 32800 | tf_op jit(solution)/shard_map/ppermute | solution.py:21
  32.2 4.0 %collective-permute-start.4 = (f32[18,1,128]{2,1,0:T(1,128)S(1)}, f32[18,1,128]{2,1,0:T(1,128)S(1)}, u32[]{:S(2)}, u32[]{:S(2)}) collective-permute-start(f32[18,1,128]{2,1,0:T(1,128)S(1)} %get-tuple-element.19), channel_id=1, source_target_pairs={{0,1},{1,2},{2,3},{4,5},{5,6},{6,7},{8,9},{9,10},{10,11},{12,13},{... | collective-permute-start | bytes 27656 | tf_op jit(solution)/shard_map/ppermute | solution.py:18
  37.4 3.2 collective-permute-start.5
  46.0 4.0 %collective-permute-start.8 = (f32[1,64,128]{2,1,0:T(8,128)S(1)}, f32[1,64,128]{2,1,0:T(8,128)S(1)}, u32[]{:S(2)}, u32[]{:S(2)}) collective-permute-start(f32[1,64,128]{2,1,0:T(8,128)S(1)} %get-tuple-element.36), channel_id=1, source_target_pairs={{0,4},{4,8},{8,12},{12,16},{16,20},{20,24},{24,28},{28,32},{32,36}... | collective-permute-start | bytes 98312 | tf_op jit(solution)/shard_map/ppermute | solution.py:18
  52.0 6.6 %collective-permute-done.9 = f32[1,64,128]{2,1,0:T(8,128)S(1)} collective-permute-done((f32[1,64,128]{2,1,0:T(8,128)S(1)}, f32[1,64,128]{2,1,0:T(8,128)S(1)}, u32[]{:S(2)}, u32[]{:S(2)}) %collective-permute-start.9) | collective-permute-done | bytes 32800 | tf_op jit(solution)/shard_map/ppermute | solution.py:21
  58.6 3.2 collective-permute-start.10
  63.4 2.9 collective-permute-done.11
  67.0 3.3 collective-permute-start.12
  72.3 6.6 %collective-permute-done.13 = f32[1,64,128]{2,1,0:T(8,128)S(1)} collective-permute-done((f32[1,64,128]{2,1,0:T(8,128)S(1)}, f32[1,64,128]{2,1,0:T(8,128)S(1)}, u32[]{:S(2)}, u32[]{:S(2)}) %collective-permute-start.13) | collective-permute-done | bytes 32800 | tf_op jit(solution)/shard_map/ppermute | solution.py:21
  82.5 2.9 collective-permute-done.15
  86.8 8.6 %scatter_custom_fusion = f32[8192,128]{1,0:T(8,128)} fusion(s32[1024]{0:T(1024)S(1)} %bitcast.63, f32[1024,128]{1,0:T(8,128)} %bitcast.61, f32[]{:T(128)} %constant.7.clone.1), kind=kCustom, calls=%fused_computation.2 | custom fusion | flops 131072 | bytes 4194816 | tf_op jit(solution)/shard_map/scatter-add | solution.py:99
  95.5 133.8 %reduce-scatter.2.cloned.1.call-done = f32[128,128]{1,0:T(8,128)} async-done(((f32[8192,128]{1,0:T(8,128)}), f32[128,128]{1,0:T(8,128)}) %reduce-scatter.2.cloned.1.call-update) | async-done | bytes 65552 | tf_op jit(solution)/shard_map/reduce_scatter | solution.py:98
  232.9 82.3 %all-gather.2.cloned.1.call-done = f32[8192,128]{1,0:T(8,128)} async-done(((f32[128,128]{1,0:T(8,128)}), f32[8192,128]{1,0:T(8,128)}) %all-gather.2.cloned.1.call-update) | async-done | bytes 4194320 | tf_op jit(solution)/shard_map/all_gather | solution.py:107
  315.2 6.2 %gather_fusion = f32[1024,128]{1,0:T(8,128)} fusion(f32[8192,128]{1,0:T(8,128)} %all-gather.2.cloned.1.call-done, s32[1024]{0:T(1024)S(1)} %broadcast_clamp_fusion), kind=kCustom, calls=%fused_computation | custom fusion | bytes 1052672 | tf_op jit(solution)/shard_map/gather | solution.py:108
  322.6 4.0 %collective-permute-start.16 = (f32[1,64,128]{2,1,0:T(8,128)S(1)}, f32[1,64,128]{2,1,0:T(8,128)S(1)}, u32[]{:S(2)}, u32[]{:S(2)}) collective-permute-start(f32[1,64,128]{2,1,0:T(8,128)S(1)} %get-tuple-element.28), channel_id=1, source_target_pairs={{0,4},{4,8},{8,12},{12,16},{16,20},{20,24},{24,28},{28,32},{32,36}... | collective-permute-start | bytes 98312 | tf_op jit(solution)/shard_map/ppermute | solution.py:18
  328.6 6.6 %collective-permute-done.17 = f32[1,64,128]{2,1,0:T(8,128)S(1)} collective-permute-done((f32[1,64,128]{2,1,0:T(8,128)S(1)}, f32[1,64,128]{2,1,0:T(8,128)S(1)}, u32[]{:S(2)}, u32[]{:S(2)}) %collective-permute-start.17) | collective-permute-done | bytes 32800 | tf_op jit(solution)/shard_map/ppermute | solution.py:21
  335.2 3.1 collective-permute-start.18
  339.9 2.9 collective-permute-done.19
  343.4 3.3 collective-permute-start.20
  348.7 6.6 %collective-permute-done.21 = f32[1,64,128]{2,1,0:T(8,128)S(1)} collective-permute-done((f32[1,64,128]{2,1,0:T(8,128)S(1)}, f32[1,64,128]{2,1,0:T(8,128)S(1)}, u32[]{:S(2)}, u32[]{:S(2)}) %collective-permute-start.21) | collective-permute-done | bytes 32800 | tf_op jit(solution)/shard_map/ppermute | solution.py:21
  355.4 3.1 collective-permute-start.22
  360.0 2.9 collective-permute-done.23
  (86 shorter events, 39.4 us)
Async XLA Ops:
  6.5 222.7 %reduce-scatter.2.cloned.1.call-start = ((), (), s32[]{:S(2)}) async-start(), calls=%async_computation.1 | async-start | bytes 4259840 | tf_op jit(solution)/shard_map/reduce_scatter | solution.py:98
  7.4 16.8 %collective-permute-start = (f32[1,64,128]{2,1,0:T(8,128)S(1)}, f32[1,64,128]{2,1,0:T(8,128)S(1)}, u32[]{:S(2)}, u32[]{:S(2)}) collective-permute-start(f32[1,64,128]{2,1,0:T(8,128)S(1)} %get-tuple-element.41), channel_id=1, source_target_pairs={{0,4},{4,8},{8,12},{12,16},{16,20},{20,24},{24,28},{28,32},{32,36}... | collective-permute-start | bytes 98312 | tf_op jit(solution)/shard_map/ppermute | solution.py:18
  13.5 23.9 %collective-permute-start.3 = (f32[1,64,128]{2,1,0:T(8,128)S(1)}, f32[1,64,128]{2,1,0:T(8,128)S(1)}, u32[]{:S(2)}, u32[]{:S(2)}) collective-permute-start(f32[1,64,128]{2,1,0:T(8,128)S(1)} %get-tuple-element.44), channel_id=1, source_target_pairs={{4,0},{8,4},{12,8},{16,12},{20,16},{24,20},{28,24},{32,28},{36,32}... | collective-permute-start | bytes 98312 | tf_op jit(solution)/shard_map/ppermute | solution.py:21
  15.4 20.8 %collective-permute-start.1 = (f32[1,64,128]{2,1,0:T(8,128)S(1)}, f32[1,64,128]{2,1,0:T(8,128)S(1)}, u32[]{:S(2)}, u32[]{:S(2)}) collective-permute-start(f32[1,64,128]{2,1,0:T(8,128)S(1)} %get-tuple-element.45), channel_id=1, source_target_pairs={{0,4},{4,8},{8,12},{12,16},{16,20},{20,24},{24,28},{28,32},{32,36}... | collective-permute-start | bytes 98312 | tf_op jit(solution)/shard_map/ppermute | solution.py:18
  22.3 8.6 %collective-permute-start.2 = (f32[1,64,128]{2,1,0:T(8,128)S(1)}, f32[1,64,128]{2,1,0:T(8,128)S(1)}, u32[]{:S(2)}, u32[]{:S(2)}) collective-permute-start(f32[1,64,128]{2,1,0:T(8,128)S(1)} %get-tuple-element.40), channel_id=1, source_target_pairs={{4,0},{8,4},{12,8},{16,12},{20,16},{24,20},{28,24},{32,28},{36,32}... | collective-permute-start | bytes 98312 | tf_op jit(solution)/shard_map/ppermute | solution.py:21
  30.9 12.9 %collective-permute-start.6 = (f32[18,1,128]{2,1,0:T(1,128)S(1)}, f32[18,1,128]{2,1,0:T(1,128)S(1)}, u32[]{:S(2)}, u32[]{:S(2)}) collective-permute-start(f32[18,1,128]{2,1,0:T(1,128)S(1)} %get-tuple-element.18), channel_id=1, source_target_pairs={{1,0},{2,1},{3,2},{5,4},{6,5},{7,6},{9,8},{10,9},{11,10},{13,12},{... | collective-permute-start | bytes 27656 | tf_op jit(solution)/shard_map/ppermute | solution.py:21
  32.2 11.6 %collective-permute-start.4 = (f32[18,1,128]{2,1,0:T(1,128)S(1)}, f32[18,1,128]{2,1,0:T(1,128)S(1)}, u32[]{:S(2)}, u32[]{:S(2)}) collective-permute-start(f32[18,1,128]{2,1,0:T(1,128)S(1)} %get-tuple-element.19), channel_id=1, source_target_pairs={{0,1},{1,2},{2,3},{4,5},{5,6},{6,7},{8,9},{9,10},{10,11},{12,13},{... | collective-permute-start | bytes 27656 | tf_op jit(solution)/shard_map/ppermute | solution.py:18
  37.4 6.5 %collective-permute-start.5 = (f32[18,1,128]{2,1,0:T(1,128)S(1)}, f32[18,1,128]{2,1,0:T(1,128)S(1)}, u32[]{:S(2)}, u32[]{:S(2)}) collective-permute-start(f32[18,1,128]{2,1,0:T(1,128)S(1)} %get-tuple-element.20), channel_id=1, source_target_pairs={{0,1},{1,2},{2,3},{4,5},{5,6},{6,7},{8,9},{9,10},{10,11},{12,13},{... | collective-permute-start | bytes 27656 | tf_op jit(solution)/shard_map/ppermute | solution.py:18
  40.6 4.4 %collective-permute-start.7 = (f32[18,1,128]{2,1,0:T(1,128)S(1)}, f32[18,1,128]{2,1,0:T(1,128)S(1)}, u32[]{:S(2)}, u32[]{:S(2)}) collective-permute-start(f32[18,1,128]{2,1,0:T(1,128)S(1)} %get-tuple-element.21), channel_id=1, source_target_pairs={{1,0},{2,1},{3,2},{5,4},{6,5},{7,6},{9,8},{10,9},{11,10},{13,12},{... | collective-permute-start | bytes 27656 | tf_op jit(solution)/shard_map/ppermute | solution.py:21
  46.0 6.0 %collective-permute-start.8 = (f32[1,64,128]{2,1,0:T(8,128)S(1)}, f32[1,64,128]{2,1,0:T(8,128)S(1)}, u32[]{:S(2)}, u32[]{:S(2)}) collective-permute-start(f32[1,64,128]{2,1,0:T(8,128)S(1)} %get-tuple-element.36), channel_id=1, source_target_pairs={{0,4},{4,8},{8,12},{12,16},{16,20},{20,24},{24,28},{28,32},{32,36}... | collective-permute-start | bytes 98312 | tf_op jit(solution)/shard_map/ppermute | solution.py:18
  50.1 8.6 %collective-permute-start.9 = (f32[1,64,128]{2,1,0:T(8,128)S(1)}, f32[1,64,128]{2,1,0:T(8,128)S(1)}, u32[]{:S(2)}, u32[]{:S(2)}) collective-permute-start(f32[1,64,128]{2,1,0:T(8,128)S(1)} %get-tuple-element.37), channel_id=1, source_target_pairs={{4,0},{8,4},{12,8},{16,12},{20,16},{24,20},{28,24},{32,28},{36,32}... | collective-permute-start | bytes 98312 | tf_op jit(solution)/shard_map/ppermute | solution.py:21
  58.6 4.7 %collective-permute-start.10 = (f32[18,1,128]{2,1,0:T(1,128)S(1)}, f32[18,1,128]{2,1,0:T(1,128)S(1)}, u32[]{:S(2)}, u32[]{:S(2)}) collective-permute-start(f32[18,1,128]{2,1,0:T(1,128)S(1)} %get-tuple-element.16), channel_id=1, source_target_pairs={{0,1},{1,2},{2,3},{4,5},{5,6},{6,7},{8,9},{9,10},{10,11},{12,13},{... | collective-permute-start | bytes 27656 | tf_op jit(solution)/shard_map/ppermute | solution.py:18
  61.9 4.4 %collective-permute-start.11 = (f32[18,1,128]{2,1,0:T(1,128)S(1)}, f32[18,1,128]{2,1,0:T(1,128)S(1)}, u32[]{:S(2)}, u32[]{:S(2)}) collective-permute-start(f32[18,1,128]{2,1,0:T(1,128)S(1)} %get-tuple-element.17), channel_id=1, source_target_pairs={{1,0},{2,1},{3,2},{5,4},{6,5},{7,6},{9,8},{10,9},{11,10},{13,12},{... | collective-permute-start | bytes 27656 | tf_op jit(solution)/shard_map/ppermute | solution.py:21
  67.0 5.3 %collective-permute-start.12 = (f32[1,64,128]{2,1,0:T(8,128)S(1)}, f32[1,64,128]{2,1,0:T(8,128)S(1)}, u32[]{:S(2)}, u32[]{:S(2)}) collective-permute-start(f32[1,64,128]{2,1,0:T(8,128)S(1)} %get-tuple-element.32), channel_id=1, source_target_pairs={{0,4},{4,8},{8,12},{12,16},{16,20},{20,24},{24,28},{28,32},{32,36}... | collective-permute-start | bytes 98312 | tf_op jit(solution)/shard_map/ppermute | solution.py:18
  70.3 8.6 %collective-permute-start.13 = (f32[1,64,128]{2,1,0:T(8,128)S(1)}, f32[1,64,128]{2,1,0:T(8,128)S(1)}, u32[]{:S(2)}, u32[]{:S(2)}) collective-permute-start(f32[1,64,128]{2,1,0:T(8,128)S(1)} %get-tuple-element.33), channel_id=1, source_target_pairs={{4,0},{8,4},{12,8},{16,12},{20,16},{24,20},{28,24},{32,28},{36,32}... | collective-permute-start | bytes 98312 | tf_op jit(solution)/shard_map/ppermute | solution.py:21
  95.4 219.8 %all-gather.2.cloned.1.call-start = ((), (), s32[]{:S(2)}) async-start(), calls=%async_computation.2 | async-start | bytes 4259840 | tf_op jit(solution)/shard_map/all_gather | solution.py:107
  322.6 6.0 %collective-permute-start.16 = (f32[1,64,128]{2,1,0:T(8,128)S(1)}, f32[1,64,128]{2,1,0:T(8,128)S(1)}, u32[]{:S(2)}, u32[]{:S(2)}) collective-permute-start(f32[1,64,128]{2,1,0:T(8,128)S(1)} %get-tuple-element.28), channel_id=1, source_target_pairs={{0,4},{4,8},{8,12},{12,16},{16,20},{20,24},{24,28},{28,32},{32,36}... | collective-permute-start | bytes 98312 | tf_op jit(solution)/shard_map/ppermute | solution.py:18
  326.7 8.6 %collective-permute-start.17 = (f32[1,64,128]{2,1,0:T(8,128)S(1)}, f32[1,64,128]{2,1,0:T(8,128)S(1)}, u32[]{:S(2)}, u32[]{:S(2)}) collective-permute-start(f32[1,64,128]{2,1,0:T(8,128)S(1)} %get-tuple-element.29), channel_id=1, source_target_pairs={{4,0},{8,4},{12,8},{16,12},{20,16},{24,20},{28,24},{32,28},{36,32}... | collective-permute-start | bytes 98312 | tf_op jit(solution)/shard_map/ppermute | solution.py:21
  335.2 4.6 %collective-permute-start.18 = (f32[18,1,128]{2,1,0:T(1,128)S(1)}, f32[18,1,128]{2,1,0:T(1,128)S(1)}, u32[]{:S(2)}, u32[]{:S(2)}) collective-permute-start(f32[18,1,128]{2,1,0:T(1,128)S(1)} %get-tuple-element.12), channel_id=1, source_target_pairs={{0,1},{1,2},{2,3},{4,5},{5,6},{6,7},{8,9},{9,10},{10,11},{12,13},{... | collective-permute-start | bytes 27656 | tf_op jit(solution)/shard_map/ppermute | solution.py:18
  338.4 4.4 %collective-permute-start.19 = (f32[18,1,128]{2,1,0:T(1,128)S(1)}, f32[18,1,128]{2,1,0:T(1,128)S(1)}, u32[]{:S(2)}, u32[]{:S(2)}) collective-permute-start(f32[18,1,128]{2,1,0:T(1,128)S(1)} %get-tuple-element.13), channel_id=1, source_target_pairs={{1,0},{2,1},{3,2},{5,4},{6,5},{7,6},{9,8},{10,9},{11,10},{13,12},{... | collective-permute-start | bytes 27656 | tf_op jit(solution)/shard_map/ppermute | solution.py:21
  343.4 5.3 %collective-permute-start.20 = (f32[1,64,128]{2,1,0:T(8,128)S(1)}, f32[1,64,128]{2,1,0:T(8,128)S(1)}, u32[]{:S(2)}, u32[]{:S(2)}) collective-permute-start(f32[1,64,128]{2,1,0:T(8,128)S(1)} %get-tuple-element.24), channel_id=1, source_target_pairs={{0,4},{4,8},{8,12},{12,16},{16,20},{20,24},{24,28},{28,32},{32,36}... | collective-permute-start | bytes 98312 | tf_op jit(solution)/shard_map/ppermute | solution.py:18
  346.8 8.6 %collective-permute-start.21 = (f32[1,64,128]{2,1,0:T(8,128)S(1)}, f32[1,64,128]{2,1,0:T(8,128)S(1)}, u32[]{:S(2)}, u32[]{:S(2)}) collective-permute-start(f32[1,64,128]{2,1,0:T(8,128)S(1)} %get-tuple-element.25), channel_id=1, source_target_pairs={{4,0},{8,4},{12,8},{16,12},{20,16},{24,20},{28,24},{32,28},{36,32}... | collective-permute-start | bytes 98312 | tf_op jit(solution)/shard_map/ppermute | solution.py:21
  355.4 4.6 %collective-permute-start.22 = (f32[18,1,128]{2,1,0:T(1,128)S(1)}, f32[18,1,128]{2,1,0:T(1,128)S(1)}, u32[]{:S(2)}, u32[]{:S(2)}) collective-permute-start(f32[18,1,128]{2,1,0:T(1,128)S(1)} %get-tuple-element.10), channel_id=1, source_target_pairs={{0,1},{1,2},{2,3},{4,5},{5,6},{6,7},{8,9},{9,10},{10,11},{12,13},{... | collective-permute-start | bytes 27656 | tf_op jit(solution)/shard_map/ppermute | solution.py:18
  358.5 4.4 %collective-permute-start.23 = (f32[18,1,128]{2,1,0:T(1,128)S(1)}, f32[18,1,128]{2,1,0:T(1,128)S(1)}, u32[]{:S(2)}, u32[]{:S(2)}) collective-permute-start(f32[18,1,128]{2,1,0:T(1,128)S(1)} %get-tuple-element.11), channel_id=1, source_target_pairs={{1,0},{2,1},{3,2},{5,4},{6,5},{7,6},{9,8},{10,9},{11,10},{13,12},{... | collective-permute-start | bytes 27656 | tf_op jit(solution)/shard_map/ppermute | solution.py:21
  (11 other events, 521.5 us)
Sparse Core Ops, SparseCore 0:
  95.6 133.6 reduce-scatter.1
  233.1 82.1 all-gather.1
where the time goes:
time: 372 us; the launch traced here: 371 us
  waiting for transfers between devices  261 us (70%)
  starting transfers between devices  64.9 us (17%)
  other arithmetic  18.6 us (5%)
  between operations  13.9 us (4%)
  local copies, waits for them, and re-layouts  13.1 us (4%)
    reduce_scatter x1, waiting for transfers between devices, per_device(): lax.psum_scatter(jax.ops.segment_sum(residual_rows, local_index, num_segm...  134 us
    all_gather x1, waiting for transfers between devices, per_device(): all_corrections = lax.all_gather(correction, 'bulk', axis=0, tiled=True)  82.3 us
    ppermute x12, starting transfers between devices, extended(): lax.ppermute(lax.slice_in_dim(block, block.shape[dim] - width, None, axis...  45.6 us
    ppermute x12, waiting for transfers between devices, extended(): lax.ppermute(lax.slice_in_dim(block, 0, width, axis=dim), axis, backward)  44.6 us
    ppermute x12, starting transfers between devices, extended(): lax.ppermute(lax.slice_in_dim(block, 0, width, axis=dim), axis, backward)  19.3 us
    scatter-add x1, other arithmetic, per_device(): jax.ops.segment_sum(residual_rows, local_index, num_segments=coarse_count...  8.62 us
  transfers between devices with their start and end apart: 26, of which 12 were waited for; matrix products, arithmetic and copies ran while one was open for 2% of the time, Pallas kernels for 0%

commit v1 on v0

v1 whole, which is shorter than its diff:
```python
import jax
import jax.numpy as jnp
from jax import lax
from jax.experimental import pallas as pl
from jax.experimental.pallas import tpu as pltpu
from jax.sharding import PartitionSpec as P

DAMPING = 0.8
CX, CY, NZ = 16, 64, 128
CR = 128
CAP = 40
BLOCK = CAP + 1
TRIO = 3 * BLOCK
W = 3
TOP = 8
EX, EY = CX + 2 * W, CY + 2 * TOP
F32, BF16, I32 = jnp.float32, jnp.bfloat16, jnp.int32

VMEM = pl.BlockSpec(memory_space=pltpu.VMEM)
SMEM = pl.BlockSpec(memory_space=pltpu.SMEM)


def iota(shape, dim):
    return lax.broadcasted_iota(I32, shape, dim)


def call(kernel, outs, args, in_specs=None, scratch=(), mib=16, aliases=None, out_specs=None):
    return pl.pallas_call(
        kernel,
        out_shape=[jax.ShapeDtypeStruct(s, d) for s, d in outs],
        in_specs=in_specs or [VMEM] * len(args),
        out_specs=out_specs or [VMEM] * len(outs),
        scratch_shapes=list(scratch),
        input_output_aliases=aliases or {},
        compiler_params=pltpu.CompilerParams(vmem_limit_bytes=mib << 20),
    )(*args)


def slot_kernel(owners, own_ref, row_ref, slot_ref, buf_ref):
    shift = lax.rem(lax.axis_index("bulk"), 3) * BLOCK
    before = (iota((128, 128), 0) < iota((128, 128), 1)).astype(BF16)
    owner_of = iota((owners, 128), 0)
    lane_of = iota((128, 128), 0)
    seen = jnp.zeros((owners, 1), F32)
    numbers = jnp.zeros((owners, 128), F32)
    for b in range(own_ref.shape[0]):
        own = own_ref[b : b + 1, :]
        mine = owner_of == own
        mine_f = mine.astype(F32)
        count = jnp.dot(mine_f.astype(BF16), before, preferred_element_type=F32) + seen
        rank = jnp.sum(jnp.where(mine, count, 0.0), axis=0, keepdims=True).astype(I32)
        seen = seen + jnp.sum(mine_f, axis=1, keepdims=True)
        slot_ref[b : b + 1, :] = own * BLOCK + rank
        named = jnp.where(lane_of == rank + shift, (row_ref[b : b + 1, :] + 1).astype(F32), 0.0)
        numbers = numbers + lax.dot_general(
            mine_f.astype(BF16), named.astype(BF16), (((1,), (1,)), ((), ())), preferred_element_type=F32
        )
    buf_ref[...] = jnp.zeros_like(buf_ref)
    for o in range(owners):
        buf_ref[o * BLOCK + CAP : o * BLOCK + BLOCK, :] = numbers[o : o + 1, :]


def inside_rows(low, high):
    y = iota((EY, NZ), 0)
    return ((y >= TOP) | low) & ((y < TOP + CY) | high)


def edges():
    b, s = lax.axis_index("bulk"), lax.axis_index("slab")
    return b > 0, b < lax.axis_size("bulk") - 1, s > 0, s < lax.axis_size("slab") - 1


def prepare(k_ref, wx, wy, wz, q, first, last):
    xl, xh, yl, yh = edges()
    z = iota((EY, NZ), 1)
    rows_in = inside_rows(yl, yh)

    def body(x, carry):
        k = k_ref[x]
        wxl, wxh = k + k_ref[x - 1], k + k_ref[x + 1]
        wyl, wyh = k + pltpu.roll(k, 1, 0), k + pltpu.roll(k, EY - 1, 0)
        ks = jnp.where(z == 0, 0.0, pltpu.roll(k, 1, 1))
        kn = jnp.where(z == NZ - 1, 0.0, pltpu.roll(k, NZ - 1, 1))
        diagonal = (wxl + wxh) + (wyl + wyh) + ((k + ks) + (k + kn))
        ok = rows_in & ((x >= W) | xl) & ((x < W + CX) | xh) & (diagonal > 0.0)
        q[x] = jnp.where(ok, DAMPING / jnp.where(ok, diagonal, 1.0), 0.0)
        wx[x] = wxl
        wy[x] = wyl
        wz[x] = jnp.where(z == 0, 0.0, k + ks)
        return carry

    lax.fori_loop(first, last, body, 0)
    wx[last] = k_ref[last] + k_ref[last - 1]


def neighbours(x, v_ref, wx, wy, wz):
    v = v_ref[x]
    wyl, wzl = wy[x], wz[x]
    total = wx[x] * v_ref[x - 1] + wx[x + 1] * v_ref[x + 1]
    total = total + wyl * pltpu.roll(v, 1, 0) + pltpu.roll(wyl * v, EY - 1, 0)
    total = total + wzl * pltpu.roll(v, 1, 1) + pltpu.roll(wzl * v, NZ - 1, 1)
    return v, total


def sweep(old, new, r2, wx, wy, wz, q, first, last):
    def body(x, carry):
        v, total = neighbours(x, old, wx, wy, wz)
        new[x] = (1.0 - DAMPING) * v + q[x] * (r2[x] + total)
        return carry

    lax.fori_loop(first, last, body, 0)


def pre_kernel(
    slot, p_ref, r_ref, k_ref, bl, bh, sl, sh, buf_in, vout, buf, kx, rx, va, vb, wx, wy, wz, q, res
):
    del buf_in
    xl, xh, yl, yh = edges()
    zero = jnp.zeros((EY, NZ), F32)

    def fill(dst, own, a, scale):
        for x in range(EX):
            dst[x, 0:TOP, :] = zero[0:TOP]
            dst[x, TOP + CY :, :] = zero[0:TOP]
            if x < W:
                mid, ok = bl[a * W + x], xl
            elif x < W + CX:
                mid, ok = own[x - W], None
            else:
                mid, ok = bh[a * W + x - W - CX], xh
            lo, hi = sl[a * EX + x], sh[a * EX + x]
            oky, okz = (yl, yh) if ok is None else (yl & ok, yh & ok)
            if ok is not None:
                mid = jnp.where(ok, mid, 0.0)
            dst[x, TOP : TOP + CY, :] = mid * scale if scale != 1 else mid
            dst[x, TOP - W : TOP, :] = jnp.where(oky, lo, 0.0) * scale
            dst[x, TOP + CY : TOP + CY + W, :] = jnp.where(okz, hi, 0.0) * scale

    fill(va, p_ref, 0, 1.0)
    fill(rx, r_ref, 1, 2.0)
    fill(kx, k_ref, 2, 1.0)
    prepare(kx, wx, wy, wz, q, 1, EX - 1)
    sweep(va, vb, rx, wx, wy, wz, q, 1, EX - 1)
    sweep(vb, va, rx, wx, wy, wz, q, 2, EX - 2)
    for x in range(CX):
        vout[x] = va[x + W, TOP : TOP + CY, :]

    def residual(x, carry):
        v, total = neighbours(x + W, va, wx, wy, wz)
        d = DAMPING / jnp.where(q[x + W] == 0.0, 1.0, q[x + W])
        out = 0.5 * ((rx[x + W] + total) - d * v)
        res[pl.ds(pl.multiple_of(x * CY, CY), CY), :] = out[TOP : TOP + CY]
        return carry

    lax.fori_loop(0, CX, residual, 0)

    def put(i, carry):
        for u in range(16):
            r = i * 16 + u
            buf[pl.ds(slot[r], 1), :] = res[pl.ds(r, 1), :]
        return carry

    lax.fori_loop(0, CX * CY // 16, put, 0)


def parts_of(x):
    a = x.astype(BF16)
    rest = x - a.astype(F32)
    b = rest.astype(BF16)
    return a, b, (rest - b.astype(F32)).astype(BF16)


def coarse_kernel(owners, data, leak_ref, link_ref, back, hot):
    rows = owners * BLOCK
    groups = -(-owners // 3)
    number = (iota((CR, 128), 0) + 1).astype(F32)
    total = jnp.zeros((CR, NZ), F32)
    bases = []
    for g in range(groups):
        base = g * TRIO
        names = [data[base + t * BLOCK + CAP : base + (t + 1) * BLOCK, :] for t in range(min(3, owners - 3 * g))]
        name = names[0]
        for more in names[1:]:
            name = name + more
        if base + 128 > rows:
            name = pltpu.roll(jnp.broadcast_to(name, (8, 128)), base - (rows - 128), 1)[0:1]
            base = rows - 128
        bases.append(base)
        one_hot = jnp.where(number == name, 1.0, 0.0).astype(BF16)
        hot[g] = one_hot
        for part in parts_of(data[base : base + 128, :]):
            total = total + jnp.dot(one_hot, part, preferred_element_type=F32)

    z = iota((CR, NZ), 1)
    link = link_ref[...]
    inner = jnp.where(z == NZ - 1, 0.0, link)
    below = pltpu.roll(inner, 1, 1)
    w = DAMPING / (leak_ref[...] + link + below)
    u = w * total
    for _ in range(2):
        u = (1.0 - DAMPING) * u + w * (total + inner * pltpu.roll(u, NZ - 1, 1) + pltpu.roll(inner * u, 1, 1))
    pieces = parts_of(u)
    for g in range(groups - 1, -1, -1):
        out = jnp.zeros((128, NZ), F32)
        for part in pieces:
            out = out + lax.dot_general(hot[g], part, (((0,), (0,)), ((), ())), preferred_element_type=F32)
        if g == groups - 1:
            back[bases[g] : bases[g] + 128, :] = out
        else:
            back[bases[g] : bases[g] + TRIO, :] = out[0:TRIO]


def correct_kernel(slot, back, v_ref, out):
    def take(i, carry):
        for u in range(16):
            r = i * 16 + u
            out[pl.ds(r, 1), :] = back[pl.ds(slot[r], 1), :]
        return carry

    lax.fori_loop(0, CX * CY // 16, take, 0)
    out[...] = out[...] + v_ref[...]


def post_kernel(v_ref, bl, bh, sl, sh, kx, rx, out, va, vb, wx, wy, wz, q):
    xl, xh, yl, yh = edges()
    zero = jnp.zeros((EY, NZ), F32)
    for e in range(1, EX - 1):
        va[e] = zero
        if e < W:
            mid, ok = bl[e - 1], xl
        elif e < W + CX:
            mid, ok = v_ref[e - W], None
        else:
            mid, ok = bh[e - W - CX], xh
        va[e, TOP : TOP + CY, :] = mid if ok is None else jnp.where(ok, mid, 0.0)
        if 2 <= e < EX - 2:
            oky, okz = (yl, yh) if ok is None else (yl & ok, yh & ok)
            va[e, TOP - 2 : TOP, :] = jnp.where(oky, sl[e - 2], 0.0)
            va[e, TOP + CY : TOP + CY + 2, :] = jnp.where(okz, sh[e - 2], 0.0)
    prepare(kx, wx, wy, wz, q, 2, EX - 2)
    sweep(va, vb, rx, wx, wy, wz, q, 2, EX - 2)

    def body(x, carry):
        v, total = neighbours(x + W, vb, wx, wy, wz)
        new = (1.0 - DAMPING) * v + q[x + W] * (rx[x + W] + total)
        out[x] = new[TOP : TOP + CY]
        return carry

    lax.fori_loop(0, CX, body, 0)


def ring(axis, step):
    n = lax.axis_size(axis)
    return [(i, (i + step) % n) for i in range(n)]


def from_both(axis, to_high, to_low):
    return lax.ppermute(to_high, axis, ring(axis, 1)), lax.ppermute(to_low, axis, ring(axis, -1))


def per_device(pressure, rhs, kappa, owner, coarse_row, coarse_leak, coarse_link):
    owners = lax.axis_size("bulk")
    slots = owners * BLOCK
    fields = (pressure, rhs, kappa)
    bl, bh = from_both(
        "bulk",
        jnp.concatenate([f[CX - W :] for f in fields], axis=0),
        jnp.concatenate([f[:W] for f in fields], axis=0),
    )

    def side(lo, hi):
        return jnp.concatenate(
            [
                t
                for a, f in enumerate(fields)
                for t in (bl[a * W : a * W + W, lo:hi], f[:, lo:hi], bh[a * W : a * W + W, lo:hi])
            ],
            axis=0,
        )

    sl, sh = from_both("slab", side(CY - W, CY), side(0, W))
    slot, buf = call(
        lambda *refs: slot_kernel(owners, *refs),
        [((8, 128), I32), ((slots, NZ), F32)],
        (owner.reshape(8, 128), coarse_row.reshape(8, 128)),
    )
    slot = slot.reshape(CX * CY)
    ext = pltpu.VMEM((EX, EY, NZ), F32)
    v, buf, kx, rx = call(
        pre_kernel,
        [((CX, CY, NZ), F32), ((slots, NZ), F32), ((EX, EY, NZ), F32), ((EX, EY, NZ), F32)],
        (slot, pressure, rhs, kappa, bl, bh, sl, sh, buf),
        in_specs=[SMEM] + [VMEM] * 8,
        scratch=[ext] * 6 + [pltpu.VMEM((CX * CY, NZ), F32)],
        aliases={8: 1},
        mib=24,
    )
    sent = lax.all_to_all(buf.reshape(owners, BLOCK, 1, NZ), "bulk", 0, 0)
    (back,) = call(
        lambda *refs: coarse_kernel(owners, *refs),
        [((slots, NZ), F32)],
        (sent.reshape(slots, NZ), coarse_leak[0], coarse_link[0]),
        scratch=[pltpu.VMEM((-(-owners // 3), CR, 128), BF16)],
    )
    got = lax.all_to_all(back.reshape(owners, BLOCK, 1, NZ), "bulk", 0, 0)
    (v,) = call(
        correct_kernel,
        [((CX * CY, NZ), F32)],
        (slot, got.reshape(slots, NZ), v.reshape(CX * CY, NZ)),
        in_specs=[SMEM, VMEM, VMEM],
    )
    v = v.reshape(CX, CY, NZ)
    bl, bh = from_both("bulk", v[CX - 2 :], v[:2])

    def rim(lo, hi):
        return jnp.concatenate([bl[1:, lo:hi], v[:, lo:hi], bh[:1, lo:hi]], axis=0)

    sl, sh = from_both("slab", rim(CY - 2, CY), rim(0, 2))
    (out,) = call(
        post_kernel,
        [((CX, CY, NZ), F32)],
        (v, bl, bh, sl, sh, kx, rx),
        scratch=[ext] * 6,
        mib=24,
    )
    return out


def solution(mesh):
    return jax.shard_map(
        per_device,
        mesh=mesh,
        in_specs=(
            P("bulk", "slab", None),
            P("bulk", "slab", None),
            P("bulk", "slab", None),
            P("slab", "bulk", None, None),
            P("slab", "bulk", None),
            P("slab", "bulk", None),
            P("slab", "bulk", None),
        ),
        out_specs=P("bulk", "slab", None),
        check_vma=False,
    )
```

time: 372 us -> 140 us (0.38)
  the two profiles are of different devices: /device:TPU:103 before, /device:TPU:24 now
where the time goes in v1:
time: 140 us; the launch traced here: 139 us
  blocking collectives  83.9 us (60%)
  Pallas kernels  20.2 us (14%)
  starting transfers between devices  19.3 us (14%)
  waiting for transfers between devices  13.4 us (10%)
  local copies, waits for them, and re-layouts  2.35 us (2%)
    all_to_all x1, blocking collectives, per_device(): sent = lax.all_to_all(buf.reshape(owners, BLOCK, 1, NZ), 'bulk', 0, 0)  43.4 us
    all_to_all x1, blocking collectives, per_device(): got = lax.all_to_all(back.reshape(owners, BLOCK, 1, NZ), 'bulk', 0, 0)  40.4 us
    pallas_call x5, Pallas kernels, call(): pl.pallas_call(kernel, out_shape=[jax.ShapeDtypeStruct(s, d) for s, d in...  20.2 us
    ppermute x4, starting transfers between devices, from_both(): lax.ppermute(to_low, axis, ring(axis, -1))  13.6 us
    ppermute x4, waiting for transfers between devices, from_both(): lax.ppermute(to_high, axis, ring(axis, 1))  7.5 us
    ppermute x4, waiting for transfers between devices, from_both(): lax.ppermute(to_low, axis, ring(axis, -1))  5.86 us
    ppermute x4, starting transfers between devices, from_both(): lax.ppermute(to_high, axis, ring(axis, 1))  5.69 us
  transfers between devices with their start and end apart: 8, of which 5 were waited for; matrix products, arithmetic and copies ran while one was open for 0% of the time, Pallas kernels for 1%

profile of v1, /device:TPU:24, one launch (start us, length us, event | category | flops | bytes accessed | tf_op | source)
XLA Modules:
  0.0 139.3 jit_solution(6875430545298418298)
XLA Ops:
  0.0 1.1 fusion.4
  1.1 0.0 copy-start.5
  1.1 1.1 fusion.2
  2.2 0.1 collective-permute-start
  2.3 7.6 %collective-permute-start.1 = (f32[9,64,128]{2,1,0:T(8,128)S(1)}, f32[9,64,128]{2,1,0:T(8,128)S(1)}, u32[]{:S(2)}, u32[]{:S(2)}) collective-permute-start(f32[9,64,128]{2,1,0:T(8,128)S(1)} %pad_maximum_fusion.1), channel_id=1, source_target_pairs={{0,252},{4,0},{8,4},{12,8},{16,12},{20,16},{24,20},{28,24},{32,28}... | collective-permute-start | bytes 884744 | tf_op jit(solution)/shard_map/ppermute | solution.py:258
  9.9 4.3 %collective-permute-done.bl = f32[9,64,128]{2,1,0:T(8,128)S(1)} collective-permute-done((f32[9,64,128]{2,1,0:T(8,128)S(1)}, f32[9,64,128]{2,1,0:T(8,128)S(1)}, u32[]{:S(2)}, u32[]{:S(2)}) %collective-permute-start) | collective-permute-done | bytes 294944 | tf_op jit(solution)/shard_map/ppermute | solution.py:258
  14.4 0.8 collective-permute-start.3
  15.2 2.5 %collective-permute-start.2 = (f32[66,3,128]{2,1,0:T(4,128)S(1)}, f32[66,3,128]{2,1,0:T(4,128)S(1)}, u32[]{:S(2)}, u32[]{:S(2)}) collective-permute-start(f32[66,3,128]{2,1,0:T(4,128)S(1)} %get-tuple-element.34), channel_id=1, source_target_pairs={{0,1},{1,2},{2,3},{3,0},{4,5},{5,6},{6,7},{7,4},{8,9},{9,10},{10,1... | collective-permute-start | bytes 304136 | tf_op jit(solution)/shard_map/ppermute | solution.py:258
  17.7 0.8 shard_map.73
  18.5 2.2 %collective-permute-done.3.sh = f32[66,3,128]{2,1,0:T(4,128)S(1)} collective-permute-done((f32[66,3,128]{2,1,0:T(4,128)S(1)}, f32[66,3,128]{2,1,0:T(4,128)S(1)}, u32[]{:S(2)}, u32[]{:S(2)}) %collective-permute-start.3) | collective-permute-done | bytes 101408 | tf_op jit(solution)/shard_map/ppermute | solution.py:258
  20.7 9.1 %shard_map.74 = (f32[16,64,128]{2,1,0:T(8,128)S(1)}, f32[2624,128]{1,0:T(8,128)S(1)}, f32[22,80,128]{2,1,0:T(8,128)S(1)}, f32[22,80,128]{2,1,0:T(8,128)S(1)}) custom-call(s32[1024]{0:T(1024)S(1)} %bitcast.22, f32[16,64,128]{2,1,0:T(8,128)S(1)} %copy-done.1, f32[16,64,128]{2,1,0:T(8,128)S(1)} %copy-done.2, ...), custom_call_target="tpu_custom_call", output_to_operand_aliasing={{1}: (8, {})} | custom-call | tf_op jit(solution)/shard_map/pallas_call | solution.py:28
  29.8 43.4 %all_to_all.10 = f32[64,41,1,128]{3,2,1,0:T(1,128)S(1)} all-to-all(f32[64,41,1,128]{3,2,1,0:T(1,128)S(1)} %bitcast.13), channel_id=1, replica_groups=mesh['bulk'=64,'slab'=4] {'bulk'}, dimensions={0} | all-to-all | bytes 2686976 | tf_op jit(solution)/shard_map/all_to_all | solution.py:298
  73.3 2.7 %shard_map.75 = f32[2624,128]{1,0:T(8,128)S(1)} custom-call(f32[2624,128]{1,0:T(8,128)S(1)} %bitcast.15, f32[128,128]{1,0:T(8,128)S(1)} %bitcast.20, f32[128,128]{1,0:T(8,128)S(1)} %bitcast.21), custom_call_target="tpu_custom_call" | custom-call | tf_op jit(solution)/shard_map/pallas_call | solution.py:28
  75.9 40.4 %all_to_all.11 = f32[64,41,1,128]{3,2,1,0:T(1,128)S(1)} all-to-all(f32[64,41,1,128]{3,2,1,0:T(1,128)S(1)} %bitcast.16), channel_id=1, replica_groups=mesh['bulk'=64,'slab'=4] {'bulk'}, dimensions={0} | all-to-all | bytes 2686976 | tf_op jit(solution)/shard_map/all_to_all | solution.py:305
  116.4 1.7 %shard_map.76 = f32[1024,128]{1,0:T(8,128)S(1)} custom-call(s32[1024]{0:T(1024)S(1)} %bitcast.23, f32[2624,128]{1,0:T(8,128)S(1)} %bitcast.14, f32[1024,128]{1,0:T(8,128)S(1)} %bitcast.19), custom_call_target="tpu_custom_call" | custom-call | tf_op jit(solution)/shard_map/pallas_call | solution.py:28
  118.1 0.1 collective-permute-start.4
  118.3 5.1 %collective-permute-start.5 = (f32[2,64,128]{2,1,0:T(8,128)S(1)}, f32[2,64,128]{2,1,0:T(8,128)S(1)}, u32[]{:S(2)}, u32[]{:S(2)}) collective-permute-start(f32[2,64,128]{2,1,0:T(8,128)S(1)} %bitcast.26), channel_id=1, source_target_pairs={{0,252},{4,0},{8,4},{12,8},{16,12},{20,16},{24,20},{28,24},{32,28}... | collective-permute-start | bytes 196616 | tf_op jit(solution)/shard_map/ppermute | solution.py:258
  123.4 1.9 %collective-permute-done.4.bl = f32[2,64,128]{2,1,0:T(8,128)S(1)} collective-permute-done((f32[2,64,128]{2,1,0:T(8,128)S(1)}, f32[2,64,128]{2,1,0:T(8,128)S(1)}, u32[]{:S(2)}, u32[]{:S(2)}) %collective-permute-start.4) | collective-permute-done | bytes 65568 | tf_op jit(solution)/shard_map/ppermute | solution.py:258
  125.2 0.0 collective-permute-done.5.bh
  125.3 3.0 %collective-permute-start.6 = (f32[18,2,128]{2,1,0:T(2,128)S(1)}, f32[18,2,128]{2,1,0:T(2,128)S(1)}, u32[]{:S(2)}, u32[]{:S(2)}) collective-permute-start(f32[18,2,128]{2,1,0:T(2,128)S(1)} %pad_maximum_fusion.2), channel_id=1, source_target_pairs={{0,1},{1,2},{2,3},{3,0},{4,5},{5,6},{6,7},{7,4},{8,9},{9,10},{10,1... | collective-permute-start | bytes 55304 | tf_op jit(solution)/shard_map/ppermute | solution.py:258
  128.3 0.1 collective-permute-start.7
  128.4 1.4 collective-permute-done.6.sl
  129.8 3.6 %collective-permute-done.7.sh = f32[18,2,128]{2,1,0:T(2,128)S(1)} collective-permute-done((f32[18,2,128]{2,1,0:T(2,128)S(1)}, f32[18,2,128]{2,1,0:T(2,128)S(1)}, u32[]{:S(2)}, u32[]{:S(2)}) %collective-permute-start.7) | collective-permute-done | bytes 18464 | tf_op jit(solution)/shard_map/ppermute | solution.py:258
  133.4 5.9 %shard_map.77 = f32[16,64,128]{2,1,0:T(8,128)} custom-call(f32[16,64,128]{2,1,0:T(8,128)S(1)} %bitcast.18, f32[2,64,128]{2,1,0:T(8,128)S(1)} %collective-permute-done.4.bl, f32[2,64,128]{2,1,0:T(8,128)S(1)} %collective-permute-done.5.bh, f32[18,2,128]{2,1,0:T(2,128)S(1)} %collective-permute-done.6.sl, f32[18,2,128]{2,1,0:T(2,128)S(1)} %collective-permute-done.7.sh, ...), custom_call_target="tpu_custom_call" | custom-call | tf_op jit(solution)/shard_map/pallas_call | solution.py:28
  (32 shorter events, 0.3 us)
Async XLA Ops:
  0.0 14.3 %copy-start = (f32[16,64,128]{2,1,0:T(8,128)S(1)}, f32[16,64,128]{2,1,0:T(8,128)}, u32[]{:S(2)}) copy-start(f32[16,64,128]{2,1,0:T(8,128)} %k_ref.1) | copy-start | bytes 1572868
  0.0 14.3 %copy-start.2 = (f32[16,64,128]{2,1,0:T(8,128)S(1)}, f32[16,64,128]{2,1,0:T(8,128)}, u32[]{:S(2)}) copy-start(f32[16,64,128]{2,1,0:T(8,128)} %r_ref.1) | copy-start | bytes 1572868
  0.0 14.2 %copy-start.1 = (f32[16,64,128]{2,1,0:T(8,128)S(1)}, f32[16,64,128]{2,1,0:T(8,128)}, u32[]{:S(2)}) copy-start(f32[16,64,128]{2,1,0:T(8,128)} %p_ref.1) | copy-start | bytes 1572868
  1.1 16.6 %copy-start.5 = (s32[1,1,1024,1]{2,3,1,0:T(1,128)S(1)}, s32[1,1,1024,1]{2,3,1,0:T(1,128)}, u32[]{:S(2)}) copy-start(s32[1,1,1024,1]{2,3,1,0:T(1,128)} %param.10) | copy-start | bytes 12292
  1.1 16.6 %copy-start.6 = (s32[1,1,1024]{2,1,0:T(1,128)S(1)}, s32[1,1,1024]{2,1,0:T(1,128)}, u32[]{:S(2)}) copy-start(s32[1,1,1024]{2,1,0:T(1,128)} %param.11) | copy-start | bytes 12292
  2.2 12.0 %collective-permute-start = (f32[9,64,128]{2,1,0:T(8,128)S(1)}, f32[9,64,128]{2,1,0:T(8,128)S(1)}, u32[]{:S(2)}, u32[]{:S(2)}) collective-permute-start(f32[9,64,128]{2,1,0:T(8,128)S(1)} %pad_maximum_fusion), channel_id=1, source_target_pairs={{0,4},{4,8},{8,12},{12,16},{16,20},{20,24},{24,28},{28,32},{32,36}... | collective-permute-start | bytes 884744 | tf_op jit(solution)/shard_map/ppermute | solution.py:258
  2.3 11.9 %collective-permute-start.1 = (f32[9,64,128]{2,1,0:T(8,128)S(1)}, f32[9,64,128]{2,1,0:T(8,128)S(1)}, u32[]{:S(2)}, u32[]{:S(2)}) collective-permute-start(f32[9,64,128]{2,1,0:T(8,128)S(1)} %pad_maximum_fusion.1), channel_id=1, source_target_pairs={{0,252},{4,0},{8,4},{12,8},{16,12},{20,16},{24,20},{28,24},{32,28}... | collective-permute-start | bytes 884744 | tf_op jit(solution)/shard_map/ppermute | solution.py:258
  14.4 6.3 %collective-permute-start.3 = (f32[66,3,128]{2,1,0:T(4,128)S(1)}, f32[66,3,128]{2,1,0:T(4,128)S(1)}, u32[]{:S(2)}, u32[]{:S(2)}) collective-permute-start(f32[66,3,128]{2,1,0:T(4,128)S(1)} %get-tuple-element.33), channel_id=1, source_target_pairs={{0,3},{1,0},{2,1},{3,2},{4,7},{5,4},{6,5},{7,6},{8,11},{9,8},{10,9... | collective-permute-start | bytes 304136 | tf_op jit(solution)/shard_map/ppermute | solution.py:258
  15.2 5.5 %collective-permute-start.2 = (f32[66,3,128]{2,1,0:T(4,128)S(1)}, f32[66,3,128]{2,1,0:T(4,128)S(1)}, u32[]{:S(2)}, u32[]{:S(2)}) collective-permute-start(f32[66,3,128]{2,1,0:T(4,128)S(1)} %get-tuple-element.34), channel_id=1, source_target_pairs={{0,1},{1,2},{2,3},{3,0},{4,5},{5,6},{6,7},{7,4},{8,9},{9,10},{10,1... | collective-permute-start | bytes 304136 | tf_op jit(solution)/shard_map/ppermute | solution.py:258
  29.8 43.5 %copy-start.3 = (f32[1,128,128]{2,1,0:T(8,128)S(1)}, f32[1,128,128]{2,1,0:T(8,128)}, u32[]{:S(2)}) copy-start(f32[1,128,128]{2,1,0:T(8,128)} %param.12) | copy-start | bytes 196612
  29.8 43.5 %copy-start.4 = (f32[1,128,128]{2,1,0:T(8,128)S(1)}, f32[1,128,128]{2,1,0:T(8,128)}, u32[]{:S(2)}) copy-start(f32[1,128,128]{2,1,0:T(8,128)} %param.13) | copy-start | bytes 196612
  118.1 7.1 %collective-permute-start.4 = (f32[2,64,128]{2,1,0:T(8,128)S(1)}, f32[2,64,128]{2,1,0:T(8,128)S(1)}, u32[]{:S(2)}, u32[]{:S(2)}) collective-permute-start(f32[2,64,128]{2,1,0:T(8,128)S(1)} %bitcast.27), channel_id=1, source_target_pairs={{0,4},{4,8},{8,12},{12,16},{16,20},{20,24},{24,28},{28,32},{32,36}... | collective-permute-start | bytes 196616 | tf_op jit(solution)/shard_map/ppermute | solution.py:258
  118.3 7.0 %collective-permute-start.5 = (f32[2,64,128]{2,1,0:T(8,128)S(1)}, f32[2,64,128]{2,1,0:T(8,128)S(1)}, u32[]{:S(2)}, u32[]{:S(2)}) collective-permute-start(f32[2,64,128]{2,1,0:T(8,128)S(1)} %bitcast.26), channel_id=1, source_target_pairs={{0,252},{4,0},{8,4},{12,8},{16,12},{20,16},{24,20},{28,24},{32,28}... | collective-permute-start | bytes 196616 | tf_op jit(solution)/shard_map/ppermute | solution.py:258
  125.3 4.5 %collective-permute-start.6 = (f32[18,2,128]{2,1,0:T(2,128)S(1)}, f32[18,2,128]{2,1,0:T(2,128)S(1)}, u32[]{:S(2)}, u32[]{:S(2)}) collective-permute-start(f32[18,2,128]{2,1,0:T(2,128)S(1)} %pad_maximum_fusion.2), channel_id=1, source_target_pairs={{0,1},{1,2},{2,3},{3,0},{4,5},{5,6},{6,7},{7,4},{8,9},{9,10},{10,1... | collective-permute-start | bytes 55304 | tf_op jit(solution)/shard_map/ppermute | solution.py:258
  128.3 5.0 %collective-permute-start.7 = (f32[18,2,128]{2,1,0:T(2,128)S(1)}, f32[18,2,128]{2,1,0:T(2,128)S(1)}, u32[]{:S(2)}, u32[]{:S(2)}) collective-permute-start(f32[18,2,128]{2,1,0:T(2,128)S(1)} %pad_maximum_fusion.3), channel_id=1, source_target_pairs={{0,3},{1,0},{2,1},{3,2},{4,7},{5,4},{6,5},{7,6},{8,11},{9,8},{10,9... | collective-permute-start | bytes 55304 | tf_op jit(solution)/shard_map/ppermute | solution.py:258

commit v2 on v1

v2 whole, which is shorter than its diff:
```python
import jax
import jax.numpy as jnp
from jax import lax
from jax.experimental import pallas as pl
from jax.experimental.pallas import tpu as pltpu
from jax.sharding import PartitionSpec as P

DAMPING = 0.8
CX, CY, NZ = 16, 64, 128
CR = 128
CAP = 40
BLOCK = CAP + 1
TRIO = 3 * BLOCK
W = 3
TOP = 8
EX, EY = CX + 2 * W, CY + 2 * TOP
F32, BF16, I32 = jnp.float32, jnp.bfloat16, jnp.int32

VMEM = pl.BlockSpec(memory_space=pltpu.VMEM)
SMEM = pl.BlockSpec(memory_space=pltpu.SMEM)


def iota(shape, dim):
    return lax.broadcasted_iota(I32, shape, dim)


def call(kernel, outs, args, in_specs=None, scratch=(), mib=16, aliases=None, out_specs=None):
    return pl.pallas_call(
        kernel,
        out_shape=[jax.ShapeDtypeStruct(s, d) for s, d in outs],
        in_specs=in_specs or [VMEM] * len(args),
        out_specs=out_specs or [VMEM] * len(outs),
        scratch_shapes=list(scratch),
        input_output_aliases=aliases or {},
        compiler_params=pltpu.CompilerParams(vmem_limit_bytes=mib << 20),
    )(*args)


def slot_kernel(owners, own_ref, row_ref, slot_ref, buf_ref):
    shift = lax.rem(lax.axis_index("bulk"), 3) * BLOCK
    before = (iota((128, 128), 0) < iota((128, 128), 1)).astype(BF16)
    owner_of = iota((owners, 128), 0)
    lane_of = iota((128, 128), 0)
    seen = jnp.zeros((owners, 1), F32)
    numbers = jnp.zeros((owners, 128), F32)
    for b in range(own_ref.shape[0]):
        own = own_ref[b : b + 1, :]
        mine = owner_of == own
        mine_f = mine.astype(F32)
        count = jnp.dot(mine_f.astype(BF16), before, preferred_element_type=F32) + seen
        rank = jnp.sum(jnp.where(mine, count, 0.0), axis=0, keepdims=True).astype(I32)
        seen = seen + jnp.sum(mine_f, axis=1, keepdims=True)
        slot_ref[b : b + 1, :] = own * BLOCK + rank
        named = jnp.where(lane_of == rank + shift, (row_ref[b : b + 1, :] + 1).astype(F32), 0.0)
        numbers = numbers + lax.dot_general(
            mine_f.astype(BF16), named.astype(BF16), (((1,), (1,)), ((), ())), preferred_element_type=F32
        )
    buf_ref[...] = jnp.zeros_like(buf_ref)
    for o in range(owners):
        buf_ref[o * BLOCK + CAP : o * BLOCK + BLOCK, :] = numbers[o : o + 1, :]


def edges():
    b, s = lax.axis_index("bulk"), lax.axis_index("slab")
    return b > 0, b < lax.axis_size("bulk") - 1, s > 0, s < lax.axis_size("slab") - 1


def zero_index():
    return jnp.minimum(lax.axis_index("bulk"), 0)


def keep(ok, values):
    return values if ok is None else jnp.where(ok, values, 0.0)


def plane_ok(e, xl, xh):
    return xl if e < W else (None if e < W + CX else xh)


def send_kernel(p_ref, k_ref, r_ref, to_high, to_low):
    at = 0
    for ref, n in ((p_ref, W), (k_ref, W), (r_ref, W - 1)):
        to_high[at : at + n] = ref[CX - n : CX]
        to_low[at : at + n] = ref[0:n]
        at += n


def halo_plane(refs, a, e):
    own, bl, bh = refs[a], refs[3], refs[4]
    if W <= e < W + CX:
        return own, e - W
    at = W * a
    if e < W:
        return bl, at + e - (1 if a == 2 else 0)
    return bh, at + e - W - CX


def side_kernel(p_ref, k_ref, r_ref, bl, bh, slot, to_high, to_low):
    del slot
    refs = (p_ref, k_ref, r_ref, bl, bh)
    for e in range(1, EX - 1):
        at = 0
        for a, n in ((0, W), (1, W), (2, W - 1)):
            ref, i = halo_plane(refs, a, e)
            to_high[e - 1, at : at + n, :] = ref[i, CY - n : CY, :]
            to_low[e - 1, at : at + n, :] = ref[i, 0:n, :]
            at += n


def prepare_rows(x, k_ref, wx, wy, wz, q, start, n, wy_start, ok, z):
    rows = pl.ds(start, n)
    k = k_ref[x, rows, :]
    low, high = k_ref[x, pl.ds(start - 1, n), :], k_ref[x, pl.ds(start + 1, n), :]
    wxl = k + k_ref[x - 1, rows, :]
    ks = jnp.where(z == 0, 0.0, pltpu.roll(k, 1, 1))
    kn = jnp.where(z == NZ - 1, 0.0, pltpu.roll(k, NZ - 1, 1))
    wzl = k + ks
    diagonal = (wxl + (k + k_ref[x + 1, rows, :])) + ((k + low) + (k + high)) + (wzl + (k + kn))
    ok = ok & (diagonal > 0.0)
    q[x, rows, :] = jnp.where(ok, DAMPING / jnp.where(ok, diagonal, 1.0), 0.0)
    wx[x, rows, :] = wxl
    wz[x, rows, :] = jnp.where(z == 0, 0.0, wzl)
    if wy_start is None:
        wy[x, rows, :] = k + low
    else:
        wy[x, pl.ds(wy_start, n), :] = k_ref[x, pl.ds(wy_start, n), :] + k_ref[x, pl.ds(wy_start - 1, n), :]


def neighbours(x, v_ref, wx, wy, wz, start, n, off):
    rows, below, above = pl.ds(start, n), pl.ds(off + (start - 1), n), pl.ds(off + (start + 1), n)
    v = v_ref[x, rows, :]
    wzl = wz[x, rows, :]
    total = wx[x, rows, :] * v_ref[x - 1, rows, :] + wx[x + 1, rows, :] * v_ref[x + 1, rows, :]
    total = total + (wy[x, rows, :] * v_ref[x, below, :] + wy[x, above, :] * v_ref[x, above, :])
    return v, total + (wzl * pltpu.roll(v, 1, 1) + pltpu.roll(wzl * v, NZ - 1, 1))


def sweep_rows(x, old, r2, wx, wy, wz, q, start, n, off):
    v, total = neighbours(x, old, wx, wy, wz, start, n, off)
    rows = pl.ds(start, n)
    return (1.0 - DAMPING) * v + q[x, rows, :] * (r2[x, rows, :] + total)


def residual_rows(x, old, r2, wx, wy, wz, q, start, n, off):
    v, total = neighbours(x, old, wx, wy, wz, start, n, off)
    rows = pl.ds(start, n)
    damped = q[x, rows, :]
    diagonal = DAMPING / jnp.where(damped == 0.0, 1.0, damped)
    return 0.5 * ((r2[x, rows, :] + total) - diagonal * v)


def put_rows(slot, buf, res, rows):
    for r in rows:
        buf[pl.ds(slot[r], 1), :] = res[r : r + 1, :]


def inner_kernel(slot, p_ref, k_ref, r_ref, bl, bh, buf_in, buf, kx, rx, va, vb, vc, wx, wy, wz, q, res):
    del buf_in
    xl, xh, _, _ = edges()
    off = zero_index()
    refs = (p_ref, k_ref, r_ref, bl, bh)
    for a, dst in ((0, va), (1, kx), (2, rx)):
        for e in range(EX) if a < 2 else range(1, EX - 1):
            ref, i = halo_plane(refs, a, e)
            values = keep(plane_ok(e, xl, xh), ref[i])
            dst[e, TOP : TOP + CY, :] = values * 2.0 if a == 2 else values
    z = iota((CY, NZ), 1)

    def prep(x, carry):
        ok = ((x >= W) | xl) & ((x < W + CX) | xh)
        prepare_rows(x, kx, wx, wy, wz, q, TOP, CY, None, ok, z)
        return carry

    lax.fori_loop(1, EX - 1, prep, 0, unroll=2)
    own = pl.ds(TOP, CY)
    wx[EX - 1, own, :] = kx[EX - 1, own, :] + kx[EX - 2, own, :]

    def first(x, carry):
        vb[x, own, :] = sweep_rows(x, va, rx, wx, wy, wz, q, TOP, CY, off)
        return carry

    def second(x, carry):
        vc[x, own, :] = sweep_rows(x, vb, rx, wx, wy, wz, q, TOP, CY, off)
        return carry

    def third(x, carry):
        e = x + W
        res[pl.ds(pl.multiple_of(x * CY, CY), CY), :] = residual_rows(e, vc, rx, wx, wy, wz, q, TOP, CY, off)
        return carry

    lax.fori_loop(1, EX - 1, first, 0, unroll=2)
    lax.fori_loop(2, EX - 2, second, 0, unroll=2)
    lax.fori_loop(0, CX, third, 0, unroll=2)

    def put(i, carry):
        for u in range(48):
            r = i * CY + TOP + u
            buf[pl.ds(slot[r], 1), :] = res[pl.ds(r, 1), :]
        return carry

    lax.fori_loop(0, CX, put, 0)


def rim_kernel(
    slot, sl, sh, kx_in, rx_in, va_in, vb_in, vc_in, wx_in, wy_in, wz_in, q_in, res, buf_in,
    kx, rx, va, vb, vc, wx, wy, wz, q, buf,
):
    del kx_in, rx_in, va_in, vb_in, vc_in, wx_in, wy_in, wz_in, q_in, buf_in
    xl, xh, yl, yh = edges()
    off = zero_index()
    end = TOP + CY
    for e in range(1, EX - 1):
        ok = plane_ok(e, xl, xh)
        low_ok, high_ok = (yl, yh) if ok is None else (yl & ok, yh & ok)
        for i, (dst, n, scale) in enumerate(((va, W, 1.0), (kx, W, 1.0), (rx, W - 1, 2.0))):
            at = W * i
            dst[e, TOP - n : TOP, :] = jnp.where(low_ok, sl[e - 1, at : at + n, :], 0.0) * scale
            dst[e, end : end + n, :] = jnp.where(high_ok, sh[e - 1, at : at + n, :], 0.0) * scale
    for e in (0, EX - 1):
        kx[e, TOP - W : TOP, :] = jnp.zeros((W, NZ), F32)
        kx[e, end : end + W, :] = jnp.zeros((W, NZ), F32)
        va[e, TOP - W : TOP, :] = jnp.zeros((W, NZ), F32)
        va[e, end : end + W, :] = jnp.zeros((W, NZ), F32)
    z, y = iota((8, NZ), 1), iota((8, NZ), 0)
    low_rows = (y >= 2) | yl
    high_rows = (y < 6) | yh

    def prep(x, carry):
        ok = ((x >= W) | xl) & ((x < W + CX) | xh)
        prepare_rows(x, kx, wx, wy, wz, q, off + (TOP - 2), 8, None, low_rows & ok, z)
        prepare_rows(x, kx, wx, wy, wz, q, off + (end - 6), 8, off + (end - 5), high_rows & ok, z)
        return carry

    lax.fori_loop(1, EX - 1, prep, 0, unroll=4)
    for start in (TOP - 2, end - 6):
        rows = pl.ds(off + start, 8)
        wx[EX - 1, rows, :] = kx[EX - 1, rows, :] + kx[EX - 2, rows, :]

    def first(x, carry):
        for start in (TOP - 2, end - 6):
            vb[x, pl.ds(off + start, 8), :] = sweep_rows(x, va, rx, wx, wy, wz, q, off + start, 8, 0)
        return carry

    def second(x, carry):
        for start in (TOP - 1, end - 7):
            vc[x, pl.ds(off + start, 8), :] = sweep_rows(x, vb, rx, wx, wy, wz, q, off + start, 8, 0)
        return carry

    lax.fori_loop(1, EX - 1, first, 0, unroll=4)
    lax.fori_loop(2, EX - 2, second, 0, unroll=3)
    for x in range(CX):
        for start in (TOP, end - 8):
            out = residual_rows(x + W, vc, rx, wx, wy, wz, q, start, 8, off)
            for u in range(8):
                buf[pl.ds(slot[x * CY + start - TOP + u], 1), :] = out[u : u + 1]


def parts_of(x):
    a = x.astype(BF16)
    rest = x - a.astype(F32)
    b = rest.astype(BF16)
    return a, b, (rest - b.astype(F32)).astype(BF16)


def coarse_kernel(owners, data, leak_ref, link_ref, back, hot):
    rows = owners * BLOCK
    groups = -(-owners // 3)
    number = (iota((CR, 128), 0) + 1).astype(F32)
    total = jnp.zeros((CR, NZ), F32)
    bases = []
    for g in range(groups):
        base = g * TRIO
        names = [data[base + t * BLOCK + CAP : base + (t + 1) * BLOCK, :] for t in range(min(3, owners - 3 * g))]
        name = names[0]
        for more in names[1:]:
            name = name + more
        if base + 128 > rows:
            name = pltpu.roll(jnp.broadcast_to(name, (8, 128)), base - (rows - 128), 1)[0:1]
            base = rows - 128
        bases.append(base)
        one_hot = jnp.where(number == name, 1.0, 0.0).astype(BF16)
        hot[g] = one_hot
        for part in parts_of(data[base : base + 128, :]):
            total = total + jnp.dot(one_hot, part, preferred_element_type=F32)

    z = iota((CR, NZ), 1)
    link = link_ref[...]
    inner = jnp.where(z == NZ - 1, 0.0, link)
    below = pltpu.roll(inner, 1, 1)
    w = DAMPING / (leak_ref[...] + link + below)
    u = w * total
    for _ in range(2):
        u = (1.0 - DAMPING) * u + w * (total + inner * pltpu.roll(u, NZ - 1, 1) + pltpu.roll(inner * u, 1, 1))
    pieces = parts_of(u)
    for g in range(groups - 1, -1, -1):
        out = jnp.zeros((128, NZ), F32)
        for part in pieces:
            out = out + lax.dot_general(hot[g], part, (((0,), (0,)), ((), ())), preferred_element_type=F32)
        if g == groups - 1:
            back[bases[g] : bases[g] + 128, :] = out
        else:
            back[bases[g] : bases[g] + TRIO, :] = out[0:TRIO]


EDGE = (0, 1, CX - 2, CX - 1)


def edge_kernel(slot, back, vc, to_high, to_low):
    for i, x in enumerate(EDGE):
        dst = to_low if i < 2 else to_high
        for y in range(CY):
            dst[i % 2, y : y + 1, :] = back[pl.ds(slot[x * CY + y], 1), :] + vc[x + W, TOP + y : TOP + y + 1, :]


def body_kernel(slot, back, vc, to_high, to_low, vd):
    for i, x in enumerate(EDGE):
        vd[x + W, TOP : TOP + CY, :] = (to_low if i < 2 else to_high)[i % 2]

    def plane(x, carry):
        for y in range(CY):
            row = back[pl.ds(slot[x * CY + y], 1), :] + vc[x + W, TOP + y : TOP + y + 1, :]
            vd[x + W, TOP + y : TOP + y + 1, :] = row
        return carry

    lax.fori_loop(2, CX - 2, plane, 0)


def last_inner_kernel(vd_in, bl, bh, rx, wx, wy, wz, q, vd, ve, out):
    del vd_in
    xl, xh, _, _ = edges()
    off = zero_index()
    own = pl.ds(TOP, CY)
    for e in (1, 2):
        vd[e, own, :] = keep(xl, bl[e - 1])
        vd[e + CX + 2, own, :] = keep(xh, bh[e - 1])

    def first(x, carry):
        ve[x, own, :] = sweep_rows(x, vd, rx, wx, wy, wz, q, TOP, CY, off)
        return carry

    def second(x, carry):
        out[x] = sweep_rows(x + W, ve, rx, wx, wy, wz, q, TOP, CY, off)
        return carry

    lax.fori_loop(2, EX - 2, first, 0, unroll=2)
    lax.fori_loop(0, CX, second, 0, unroll=2)


def last_rim_kernel(sl, sh, vd_in, ve_in, inner, rx, wx, wy, wz, q, vd, ve, out):
    del vd_in, ve_in
    xl, xh, yl, yh = edges()
    off = zero_index()
    end = TOP + CY
    for e in range(1, EX - 1):
        if 2 <= e < EX - 2:
            ok = plane_ok(e, xl, xh)
            low_ok, high_ok = (yl, yh) if ok is None else (yl & ok, yh & ok)
            vd[e, TOP - 2 : TOP, :] = jnp.where(low_ok, sl[e - 2], 0.0)
            vd[e, end : end + 2, :] = jnp.where(high_ok, sh[e - 2], 0.0)
        else:
            vd[e, TOP - 2 : TOP, :] = jnp.zeros((2, NZ), F32)
            vd[e, end : end + 2, :] = jnp.zeros((2, NZ), F32)

    def first(x, carry):
        for start in (TOP - 1, end - 7):
            ve[x, pl.ds(off + start, 8), :] = sweep_rows(x, vd, rx, wx, wy, wz, q, off + start, 8, 0)
        return carry

    lax.fori_loop(2, EX - 2, first, 0, unroll=3)

    def second(x, carry):
        out[x, 8 : CY - 8, :] = inner[x, 8 : CY - 8, :]
        for start in (TOP, end - 8):
            out[x, start - TOP : start - TOP + 8, :] = sweep_rows(x + W, ve, rx, wx, wy, wz, q, start, 8, off)
        return carry

    lax.fori_loop(0, CX, second, 0, unroll=4)


def ring(axis, step):
    n = lax.axis_size(axis)
    return [(i, (i + step) % n) for i in range(n)]


def from_both(axis, to_high, to_low):
    return lax.ppermute(to_high, axis, ring(axis, 1)), lax.ppermute(to_low, axis, ring(axis, -1))


EXT = ((EX, EY, NZ), F32)


def per_device(pressure, rhs, kappa, owner, coarse_row, coarse_leak, coarse_link):
    owners = lax.axis_size("bulk")
    slots = owners * BLOCK
    sent = ((2 * W + W - 1, CY, NZ), F32)
    side = ((EX - 2, 8, NZ), F32)
    to_high, to_low = call(
        send_kernel,
        [sent, sent],
        (pressure, kappa, rhs),
        mib=2,
    )
    bl, bh = from_both("bulk", to_high, to_low)
    slot, buf = call(
        lambda *refs: slot_kernel(owners, *refs),
        [((8, 128), I32), ((slots, NZ), F32)],
        (owner.reshape(8, 128), coarse_row.reshape(8, 128)),
    )
    to_high, to_low = call(side_kernel, [side, side], (pressure, kappa, rhs, bl, bh, slot))
    slot = slot.reshape(CX * CY)
    sl, sh = from_both("slab", to_high, to_low)
    buf, *ext, res = call(
        inner_kernel,
        [((slots, NZ), F32)] + [EXT] * 9 + [((CX * CY, NZ), F32)],
        (slot, pressure, kappa, rhs, bl, bh, buf),
        in_specs=[SMEM] + [VMEM] * 6,
        aliases={6: 0},
        mib=20,
    )
    *ext, buf = call(
        rim_kernel,
        [EXT] * 9 + [((slots, NZ), F32)],
        (slot, sl, sh, *ext, res, buf),
        in_specs=[SMEM] + [VMEM] * 13,
        aliases={**{3 + i: i for i in range(9)}, 13: 9},
        mib=20,
    )
    _, rx, _, _, vc, wx, wy, wz, q = ext
    got = lax.all_to_all(buf.reshape(owners, BLOCK, 1, NZ), "bulk", 0, 0)
    (back,) = call(
        lambda *refs: coarse_kernel(owners, *refs),
        [((slots, NZ), F32)],
        (got.reshape(slots, NZ), coarse_leak[0], coarse_link[0]),
        scratch=[pltpu.VMEM((-(-owners // 3), CR, 128), BF16)],
    )
    back = lax.all_to_all(back.reshape(owners, BLOCK, 1, NZ), "bulk", 0, 0).reshape(slots, NZ)
    to_high, to_low = call(
        edge_kernel, [((2, CY, NZ), F32)] * 2, (slot, back, vc), in_specs=[SMEM, VMEM, VMEM]
    )
    bl, bh = from_both("bulk", to_high, to_low)
    (vd,) = call(
        body_kernel, [EXT], (slot, back, vc, to_high, to_low), in_specs=[SMEM] + [VMEM] * 4
    )

    def rim(lo, hi):
        return jnp.concatenate([bl[1:, lo:hi], vd[W : W + CX, TOP + lo : TOP + hi], bh[:1, lo:hi]], axis=0)

    sl, sh = from_both("slab", rim(CY - 2, CY), rim(0, 2))
    vd, ve, inner = call(
        last_inner_kernel,
        [EXT, EXT, ((CX, CY, NZ), F32)],
        (vd, bl, bh, rx, wx, wy, wz, q),
        aliases={0: 0},
        mib=20,
    )
    _, _, out = call(
        last_rim_kernel,
        [EXT, EXT, ((CX, CY, NZ), F32)],
        (sl, sh, vd, ve, inner, rx, wx, wy, wz, q),
        aliases={2: 0, 3: 1},
        mib=20,
    )
    return out


def solution(mesh):
    return jax.shard_map(
        per_device,
        mesh=mesh,
        in_specs=(
            P("bulk", "slab", None),
            P("bulk", "slab", None),
            P("bulk", "slab", None),
            P("slab", "bulk", None, None),
            P("slab", "bulk", None),
            P("slab", "bulk", None),
            P("slab", "bulk", None),
        ),
        out_specs=P("bulk", "slab", None),
        check_vma=False,
    )
```

time: 140 us -> 130 us (0.929)
  waiting for transfers between devices: 13.4 us -> 6.96 us
  Pallas kernels: 20.2 us -> 17.1 us
  starting transfers between devices: 19.3 us -> 17.1 us
  local copies, waits for them, and re-layouts: 2.35 us -> 3.86 us
    ppermute x4, waiting for transfers between devices: 7.5 us -> 3.08 us  [from_both(): lax.ppermute(to_high, axis, ring(axis, 1))]
    unnamed x22 -> x20, local copies, waits for them, and re-layouts: 0.16 us -> 3.84 us
    ppermute x4, starting transfers between devices: 5.69 us -> 2.12 us  [from_both(): lax.ppermute(to_high, axis, ring(axis, 1))]
    pallas_call x5 -> x10, Pallas kernels: 20.2 us -> 17.1 us  [call(): pl.pallas_call(kernel, out_shape=[jax.ShapeDtypeStruct(s, d) for s, d in...]
    slice x6 -> x3, local copies, waits for them, and re-layouts: 2.18 us -> 0.02 us  [the longest x1 0.01 us: rim(): vd[W:W + CX, TOP + lo:TOP + hi]]
    ppermute x4, waiting for transfers between devices: 5.86 us -> 3.89 us  [from_both(): lax.ppermute(to_low, axis, ring(axis, -1))]
    ppermute x4, starting transfers between devices: 13.6 us -> 15 us  [from_both(): lax.ppermute(to_low, axis, ring(axis, -1))]
  transfers between devices with their start and end apart: 8 -> 8, of which waited for: 5 -> 4; matrix products, arithmetic and copies ran while one was open for 0% -> 0% of each run, Pallas kernels for 1% -> 7%
where the time goes in v2:
time: 130 us
  blocking collectives  84.4 us (65%)
  Pallas kernels  17.1 us (13%)
  starting transfers between devices  17.1 us (13%)
  waiting for transfers between devices  6.96 us (5%)
  local copies, waits for them, and re-layouts  3.86 us (3%)
    all_to_all x1, blocking collectives, per_device(): got = lax.all_to_all(buf.reshape(owners, BLOCK, 1, NZ), 'bulk', 0, 0)  44 us
    all_to_all x1, blocking collectives, per_device(): lax.all_to_all(back.reshape(owners, BLOCK, 1, NZ), 'bulk', 0, 0)  40.4 us
    pallas_call x10, Pallas kernels, call(): pl.pallas_call(kernel, out_shape=[jax.ShapeDtypeStruct(s, d) for s, d in...  17.1 us
    ppermute x4, starting transfers between devices, from_both(): lax.ppermute(to_low, axis, ring(axis, -1))  15 us
    ppermute x4, waiting for transfers between devices, from_both(): lax.ppermute(to_low, axis, ring(axis, -1))  3.89 us
    unnamed x20, local copies, waits for them, and re-layouts  3.84 us
    ppermute x4, waiting for transfers between devices, from_both(): lax.ppermute(to_high, axis, ring(axis, 1))  3.08 us
  transfers between devices with their start and end apart: 8, of which 4 were waited for; matrix products, arithmetic and copies ran while one was open for 0% of the time, Pallas kernels for 7%

profile of v2, /device:TPU:24, one launch (start us, length us, event | category | flops | bytes accessed | tf_op | source)
XLA Modules:
  0.0 129.6 jit_solution(4527824556950378165)
XLA Ops:
  0.0 1.0 copy-done
  1.0 1.0 copy-done.2
  2.1 1.0 copy-done.4
  3.3 7.6 %collective-permute-start.1 = (f32[8,64,128]{2,1,0:T(8,128)S(1)}, f32[8,64,128]{2,1,0:T(8,128)S(1)}, u32[]{:S(2)}, u32[]{:S(2)}) collective-permute-start(f32[8,64,128]{2,1,0:T(8,128)S(1)} %get-tuple-element.37), channel_id=1, source_target_pairs={{0,252},{4,0},{8,4},{12,8},{16,12},{20,16},{24,20},{28,24},{32,28}... | collective-permute-start | bytes 786440 | tf_op jit(solution)/shard_map/ppermute | solution.py:386
  10.8 0.7 copy-done.9
  11.5 0.8 shard_map.73
  12.3 2.5 %collective-permute-done.bl = f32[8,64,128]{2,1,0:T(8,128)S(1)} collective-permute-done((f32[8,64,128]{2,1,0:T(8,128)S(1)}, f32[8,64,128]{2,1,0:T(8,128)S(1)}, u32[]{:S(2)}, u32[]{:S(2)}) %collective-permute-start) | collective-permute-done | bytes 262176 | tf_op jit(solution)/shard_map/ppermute | solution.py:386
  14.9 0.3 collective-permute-start.2
  15.2 1.8 %collective-permute-start.3 = (f32[20,8,128]{2,1,0:T(8,128)S(1)}, f32[20,8,128]{2,1,0:T(8,128)S(1)}, u32[]{:S(2)}, u32[]{:S(2)}) collective-permute-start(f32[20,8,128]{2,1,0:T(8,128)S(1)} %get-tuple-element.39), channel_id=1, source_target_pairs={{0,3},{1,0},{2,1},{3,2},{4,7},{5,4},{6,5},{7,6},{8,11},{9,8},{10,9... | collective-permute-start | bytes 245768 | tf_op jit(solution)/shard_map/ppermute | solution.py:386
  17.0 5.5 %shard_map.76 = (f32[2624,128]{1,0:T(8,128)S(1)}, f32[22,80,128]{2,1,0:T(8,128)S(1)}, f32[22,80,128]{2,1,0:T(8,128)S(1)}, f32[22,80,128]{2,1,0:T(8,128)S(1)}, f3...) custom-call(s32[1024]{0:T(1024)S(1)} %bitcast.14, ...), custom_call_target="tpu_custom_call", output_to_operand_aliasing={{0}: (6, {})} | custom-call | tf_op jit(solution)/shard_map/pallas_call | solution.py:28
  22.5 2.3 %shard_map.77 = (f32[22,80,128]{2,1,0:T(8,128)S(1)}, f32[22,80,128]{2,1,0:T(8,128)S(1)}, f32[22,80,128]{2,1,0:T(8,128)S(1)}, f32[22,80,128]{2,1,0:T(8,128)S(1)},...) custom-call(s32[1024]{0:T(1024)S(1)} %bitcast.15, ...), custom_call_target="tpu_custom_call", output_to_operand_aliasing={{0}: (3, {}), {1}: (4, {}), {2}: (5, {}), {3}: (6, {}), {4}... | custom-call | tf_op jit(solution)/shard_map/pallas_call | solution.py:28
  24.9 44.0 %all_to_all.10 = f32[64,41,1,128]{3,2,1,0:T(1,128)S(1)} all-to-all(f32[64,41,1,128]{3,2,1,0:T(1,128)S(1)} %bitcast.9), channel_id=1, replica_groups=mesh['bulk'=64,'slab'=4] {'bulk'}, dimensions={0} | all-to-all | bytes 2686976 | tf_op jit(solution)/shard_map/all_to_all | solution.py:429
  68.9 2.7 %shard_map.78 = f32[2624,128]{1,0:T(8,128)S(1)} custom-call(f32[2624,128]{1,0:T(8,128)S(1)} %bitcast.12, f32[128,128]{1,0:T(8,128)S(1)} %bitcast.18, f32[128,128]{1,0:T(8,128)S(1)} %bitcast.19), custom_call_target="tpu_custom_call" | custom-call | tf_op jit(solution)/shard_map/pallas_call | solution.py:28
  71.5 40.4 %all_to_all.11 = f32[64,41,1,128]{3,2,1,0:T(1,128)S(1)} all-to-all(f32[64,41,1,128]{3,2,1,0:T(1,128)S(1)} %bitcast.13), channel_id=1, replica_groups=mesh['bulk'=64,'slab'=4] {'bulk'}, dimensions={0} | all-to-all | bytes 2686976 | tf_op jit(solution)/shard_map/all_to_all | solution.py:436
  112.0 0.8 shard_map.79
  112.8 1.3 shard_map.80.vd_in
  114.1 5.1 %collective-permute-start.5 = (f32[2,64,128]{2,1,0:T(8,128)S(1)}, f32[2,64,128]{2,1,0:T(8,128)S(1)}, u32[]{:S(2)}, u32[]{:S(2)}) collective-permute-start(f32[2,64,128]{2,1,0:T(8,128)S(1)} %get-tuple-element.55.to_low), channel_id=1, source_target_pairs={{0,252},{4,0},{8,4},{12,8},{16,12},{20,16},{24,20},{28,24},{32,28}... | collective-permute-start | bytes 196616 | tf_op jit(solution)/shard_map/ppermute | solution.py:386
  119.3 0.6 collective-permute-done.4.bl
  119.8 1.3 %collective-permute-done.5.bh = f32[2,64,128]{2,1,0:T(8,128)S(1)} collective-permute-done((f32[2,64,128]{2,1,0:T(8,128)S(1)}, f32[2,64,128]{2,1,0:T(8,128)S(1)}, u32[]{:S(2)}, u32[]{:S(2)}) %collective-permute-start.5) | collective-permute-done | bytes 65568 | tf_op jit(solution)/shard_map/ppermute | solution.py:386
  121.2 1.7 %collective-permute-start.6 = (f32[18,2,128]{2,1,0:T(2,128)S(1)}, f32[18,2,128]{2,1,0:T(2,128)S(1)}, u32[]{:S(2)}, u32[]{:S(2)}) collective-permute-start(f32[18,2,128]{2,1,0:T(2,128)S(1)} %pad_maximum_fusion), channel_id=1, source_target_pairs={{0,1},{1,2},{2,3},{3,0},{4,5},{5,6},{6,7},{7,4},{8,9},{9,10},{10,1... | collective-permute-start | bytes 55304 | tf_op jit(solution)/shard_map/ppermute | solution.py:386
  122.8 0.5 collective-permute-start.7
  123.4 1.9 %shard_map.81 = (f32[22,80,128]{2,1,0:T(8,128)S(1)}, f32[22,80,128]{2,1,0:T(8,128)S(1)}, f32[16,64,128]{2,1,0:T(8,128)S(1)}) custom-call(f32[22,80,128]{2,1,0:T(8,128)S(1)} %shard_map.80.vd_in, f32[2,64,128]{2,1,0:T(8,128)S(1)} %collective-permute-done.4.bl, f32[2,64,128]{2,1,0:T(8,128)S(1)} %collective-permute-done.5.bh, ...), custom_call_target="tpu_custom_call", output_to_operand_aliasing={{0}: (0, {})} | custom-call | tf_op jit(solution)/shard_map/pallas_call | solution.py:28
  125.3 2.6 %collective-permute-done.7.sh = f32[18,2,128]{2,1,0:T(2,128)S(1)} collective-permute-done((f32[18,2,128]{2,1,0:T(2,128)S(1)}, f32[18,2,128]{2,1,0:T(2,128)S(1)}, u32[]{:S(2)}, u32[]{:S(2)}) %collective-permute-start.7) | collective-permute-done | bytes 18464 | tf_op jit(solution)/shard_map/ppermute | solution.py:386
  127.9 1.7 %shard_map.82 = (f32[22,80,128]{2,1,0:T(8,128)S(1)}, f32[22,80,128]{2,1,0:T(8,128)S(1)}, f32[16,64,128]{2,1,0:T(8,128)}) custom-call(f32[18,2,128]{2,1,0:T(2,128)S(1)} %collective-permute-done.6.sl, f32[18,2,128]{2,1,0:T(2,128)S(1)} %collective-permute-done.7.sh, ...), custom_call_target="tpu_custom_call", output_to_operand_aliasing={{0}: (2, {}), {1}: (3, {})} | custom-call | tf_op jit(solution)/shard_map/pallas_call | solution.py:28
  (29 shorter events, 0.3 us)
Async XLA Ops:
  0.0 1.0 copy-start
  1.0 1.0 copy-start.2
  2.1 1.0 copy-start.4
  3.1 7.7 %copy-start.8 = (s32[1,1,1024,1]{2,3,1,0:T(1,128)S(1)}, s32[1,1,1024,1]{2,3,1,0:T(1,128)}, u32[]{:S(2)}) copy-start(s32[1,1,1024,1]{2,3,1,0:T(1,128)} %param.10) | copy-start | bytes 12292
  3.1 11.7 %copy-start.1 = (f32[16,64,128]{2,1,0:T(8,128)S(1)}, f32[16,64,128]{2,1,0:T(8,128)}, u32[]{:S(2)}) copy-start(f32[16,64,128]{2,1,0:T(8,128)} %p_ref.5) | copy-start | bytes 1572868
  3.1 11.7 %copy-start.3 = (f32[16,64,128]{2,1,0:T(8,128)S(1)}, f32[16,64,128]{2,1,0:T(8,128)}, u32[]{:S(2)}) copy-start(f32[16,64,128]{2,1,0:T(8,128)} %k_ref.5) | copy-start | bytes 1572868
  3.1 11.7 %copy-start.5 = (f32[16,64,128]{2,1,0:T(8,128)S(1)}, f32[16,64,128]{2,1,0:T(8,128)}, u32[]{:S(2)}) copy-start(f32[16,64,128]{2,1,0:T(8,128)} %r_ref.5) | copy-start | bytes 1572868
  3.2 11.6 %collective-permute-start = (f32[8,64,128]{2,1,0:T(8,128)S(1)}, f32[8,64,128]{2,1,0:T(8,128)S(1)}, u32[]{:S(2)}, u32[]{:S(2)}) collective-permute-start(f32[8,64,128]{2,1,0:T(8,128)S(1)} %get-tuple-element.36), channel_id=1, source_target_pairs={{0,4},{4,8},{8,12},{12,16},{16,20},{20,24},{24,28},{28,32},{32,36}... | collective-permute-start | bytes 786440 | tf_op jit(solution)/shard_map/ppermute | solution.py:386
  3.3 11.5 %collective-permute-start.1 = (f32[8,64,128]{2,1,0:T(8,128)S(1)}, f32[8,64,128]{2,1,0:T(8,128)S(1)}, u32[]{:S(2)}, u32[]{:S(2)}) collective-permute-start(f32[8,64,128]{2,1,0:T(8,128)S(1)} %get-tuple-element.37), channel_id=1, source_target_pairs={{0,252},{4,0},{8,4},{12,8},{16,12},{20,16},{24,20},{28,24},{32,28}... | collective-permute-start | bytes 786440 | tf_op jit(solution)/shard_map/ppermute | solution.py:386
  10.8 0.7 copy-start.9
  14.9 7.6 %collective-permute-start.2 = (f32[20,8,128]{2,1,0:T(8,128)S(1)}, f32[20,8,128]{2,1,0:T(8,128)S(1)}, u32[]{:S(2)}, u32[]{:S(2)}) collective-permute-start(f32[20,8,128]{2,1,0:T(8,128)S(1)} %get-tuple-element.38), channel_id=1, source_target_pairs={{0,1},{1,2},{2,3},{3,0},{4,5},{5,6},{6,7},{7,4},{8,9},{9,10},{10,1... | collective-permute-start | bytes 245768 | tf_op jit(solution)/shard_map/ppermute | solution.py:386
  15.2 7.3 %collective-permute-start.3 = (f32[20,8,128]{2,1,0:T(8,128)S(1)}, f32[20,8,128]{2,1,0:T(8,128)S(1)}, u32[]{:S(2)}, u32[]{:S(2)}) collective-permute-start(f32[20,8,128]{2,1,0:T(8,128)S(1)} %get-tuple-element.39), channel_id=1, source_target_pairs={{0,3},{1,0},{2,1},{3,2},{4,7},{5,4},{6,5},{7,6},{8,11},{9,8},{10,9... | collective-permute-start | bytes 245768 | tf_op jit(solution)/shard_map/ppermute | solution.py:386
  24.9 44.0 %copy-start.6 = (f32[1,128,128]{2,1,0:T(8,128)S(1)}, f32[1,128,128]{2,1,0:T(8,128)}, u32[]{:S(2)}) copy-start(f32[1,128,128]{2,1,0:T(8,128)} %param.12) | copy-start | bytes 196612
  24.9 44.0 %copy-start.7 = (f32[1,128,128]{2,1,0:T(8,128)S(1)}, f32[1,128,128]{2,1,0:T(8,128)}, u32[]{:S(2)}) copy-start(f32[1,128,128]{2,1,0:T(8,128)} %param.13) | copy-start | bytes 196612
  112.8 7.1 %collective-permute-start.4 = (f32[2,64,128]{2,1,0:T(8,128)S(1)}, f32[2,64,128]{2,1,0:T(8,128)S(1)}, u32[]{:S(2)}, u32[]{:S(2)}) collective-permute-start(f32[2,64,128]{2,1,0:T(8,128)S(1)} %get-tuple-element.54.to_high), channel_id=1, source_target_pairs={{0,4},{4,8},{8,12},{12,16},{16,20},{20,24},{24,28},{28,32},{32,36}... | collective-permute-start | bytes 196616 | tf_op jit(solution)/shard_map/ppermute | solution.py:386
  114.1 7.0 %collective-permute-start.5 = (f32[2,64,128]{2,1,0:T(8,128)S(1)}, f32[2,64,128]{2,1,0:T(8,128)S(1)}, u32[]{:S(2)}, u32[]{:S(2)}) collective-permute-start(f32[2,64,128]{2,1,0:T(8,128)S(1)} %get-tuple-element.55.to_low), channel_id=1, source_target_pairs={{0,252},{4,0},{8,4},{12,8},{16,12},{20,16},{24,20},{28,24},{32,28}... | collective-permute-start | bytes 196616 | tf_op jit(solution)/shard_map/ppermute | solution.py:386
  121.2 4.1 %collective-permute-start.6 = (f32[18,2,128]{2,1,0:T(2,128)S(1)}, f32[18,2,128]{2,1,0:T(2,128)S(1)}, u32[]{:S(2)}, u32[]{:S(2)}) collective-permute-start(f32[18,2,128]{2,1,0:T(2,128)S(1)} %pad_maximum_fusion), channel_id=1, source_target_pairs={{0,1},{1,2},{2,3},{3,0},{4,5},{5,6},{6,7},{7,4},{8,9},{9,10},{10,1... | collective-permute-start | bytes 55304 | tf_op jit(solution)/shard_map/ppermute | solution.py:386
  122.8 5.0 %collective-permute-start.7 = (f32[18,2,128]{2,1,0:T(2,128)S(1)}, f32[18,2,128]{2,1,0:T(2,128)S(1)}, u32[]{:S(2)}, u32[]{:S(2)}) collective-permute-start(f32[18,2,128]{2,1,0:T(2,128)S(1)} %pad_maximum_fusion.1), channel_id=1, source_target_pairs={{0,3},{1,0},{2,1},{3,2},{4,7},{5,4},{6,5},{7,6},{8,11},{9,8},{10,9... | collective-permute-start | bytes 55304 | tf_op jit(solution)/shard_map/ppermute | solution.py:386

commit v3 on v2

--- a/solution.py
+++ b/solution.py
@@ -4,6 +4,7 @@
 from jax.experimental import pallas as pl
 from jax.experimental.pallas import tpu as pltpu
 from jax.sharding import PartitionSpec as P
+
 
 DAMPING = 0.8
 CX, CY, NZ = 16, 64, 128
@@ -77,12 +78,17 @@
     return xl if e < W else (None if e < W + CX else xh)
 
 
-def send_kernel(p_ref, k_ref, r_ref, to_high, to_low):
+def send_kernel(p_ref, k_ref, r_ref, to_high, to_low, sems):
+    copies = []
     at = 0
     for ref, n in ((p_ref, W), (k_ref, W), (r_ref, W - 1)):
-        to_high[at : at + n] = ref[CX - n : CX]
-        to_low[at : at + n] = ref[0:n]
+        for src, dst in ((ref.at[pl.ds(CX - n, n)], to_high.at[pl.ds(at, n)]), (ref.at[pl.ds(0, n)], to_low.at[pl.ds(at, n)])):
+            copies.append(pltpu.make_async_copy(src, dst, sems.at[len(copies)]))
         at += n
+    for copy in copies:
+        copy.start()
+    for copy in copies:
+        copy.wait()
 
 
 def halo_plane(refs, a, e):
@@ -95,8 +101,8 @@
     return bh, at + e - W - CX
 
 
-def side_kernel(p_ref, k_ref, r_ref, bl, bh, slot, to_high, to_low):
-    del slot
+def side_kernel(p_ref, k_ref, r_ref, bl, bh, done, to_high, to_low):
+    del done
     refs = (p_ref, k_ref, r_ref, bl, bh)
     for e in range(1, EX - 1):
         at = 0
@@ -126,86 +132,119 @@
         wy[x, pl.ds(wy_start, n), :] = k_ref[x, pl.ds(wy_start, n), :] + k_ref[x, pl.ds(wy_start - 1, n), :]
 
 
-def neighbours(x, v_ref, wx, wy, wz, start, n, off):
+def turned(x, v_ref, wz, start, n):
+    v = v_ref[x, pl.ds(start, n), :]
+    return pltpu.roll(v, 1, 1), pltpu.roll(wz[x, pl.ds(start, n), :] * v, NZ - 1, 1)
+
+
+def neighbours(x, v_ref, wx, wy, wz, start, n, off, turn):
     rows, below, above = pl.ds(start, n), pl.ds(off + (start - 1), n), pl.ds(off + (start + 1), n)
-    v = v_ref[x, rows, :]
-    wzl = wz[x, rows, :]
     total = wx[x, rows, :] * v_ref[x - 1, rows, :] + wx[x + 1, rows, :] * v_ref[x + 1, rows, :]
     total = total + (wy[x, rows, :] * v_ref[x, below, :] + wy[x, above, :] * v_ref[x, above, :])
-    return v, total + (wzl * pltpu.roll(v, 1, 1) + pltpu.roll(wzl * v, NZ - 1, 1))
-
-
-def sweep_rows(x, old, r2, wx, wy, wz, q, start, n, off):
-    v, total = neighbours(x, old, wx, wy, wz, start, n, off)
+    return v_ref[x, rows, :], total + (wz[x, rows, :] * turn[0] + turn[1])
+
+
+def sweep_rows(x, old, r2, wx, wy, wz, q, start, n, off, turn=None):
+    turn = turn or turned(x, old, wz, start, n)
+    v, total = neighbours(x, old, wx, wy, wz, start, n, off, turn)
     rows = pl.ds(start, n)
     return (1.0 - DAMPING) * v + q[x, rows, :] * (r2[x, rows, :] + total)
 
 
-def residual_rows(x, old, r2, wx, wy, wz, q, start, n, off):
-    v, total = neighbours(x, old, wx, wy, wz, start, n, off)
+def residual_rows(x, old, r2, wx, wy, wz, q, start, n, off, turn=None):
+    turn = turn or turned(x, old, wz, start, n)
+    v, total = neighbours(x, old, wx, wy, wz, start, n, off, turn)
     rows = pl.ds(start, n)
     damped = q[x, rows, :]
     diagonal = DAMPING / jnp.where(damped == 0.0, 1.0, damped)
     return 0.5 * ((r2[x, rows, :] + total) - diagonal * v)
 
 
-def put_rows(slot, buf, res, rows):
-    for r in rows:
-        buf[pl.ds(slot[r], 1), :] = res[r : r + 1, :]
-
-
-def inner_kernel(slot, p_ref, k_ref, r_ref, bl, bh, buf_in, buf, kx, rx, va, vb, vc, wx, wy, wz, q, res):
-    del buf_in
-    xl, xh, _, _ = edges()
-    off = zero_index()
-    refs = (p_ref, k_ref, r_ref, bl, bh)
-    for a, dst in ((0, va), (1, kx), (2, rx)):
-        for e in range(EX) if a < 2 else range(1, EX - 1):
+def planes(first, last, old, wz, body):
+    def step(x, turn):
+        ahead = turned(x + 1, old, wz, TOP, CY)
+        body(x, turn)
+        return ahead
+
+    lax.fori_loop(first, last, step, turned(first, old, wz, TOP, CY))
+
+
+def fill(refs, fields, some, xl, xh):
+    for a, dst in enumerate(fields):
+        for e in some:
+            if a == 2 and e in (0, EX - 1):
+                continue
             ref, i = halo_plane(refs, a, e)
             values = keep(plane_ok(e, xl, xh), ref[i])
             dst[e, TOP : TOP + CY, :] = values * 2.0 if a == 2 else values
+
+
+def inner_steps(ranges, slot, buf, kx, rx, va, vb, vc, wx, wy, wz, q, res, xl, xh):
+    off = zero_index()
     z = iota((CY, NZ), 1)
+    own = pl.ds(TOP, CY)
+    field = (rx, wx, wy, wz, q, TOP, CY, off)
 
     def prep(x, carry):
         ok = ((x >= W) | xl) & ((x < W + CX) | xh)
         prepare_rows(x, kx, wx, wy, wz, q, TOP, CY, None, ok, z)
         return carry
 
-    lax.fori_loop(1, EX - 1, prep, 0, unroll=2)
-    own = pl.ds(TOP, CY)
-    wx[EX - 1, own, :] = kx[EX - 1, own, :] + kx[EX - 2, own, :]
-
-    def first(x, carry):
-        vb[x, own, :] = sweep_rows(x, va, rx, wx, wy, wz, q, TOP, CY, off)
-        return carry
-
-    def second(x, carry):
-        vc[x, own, :] = sweep_rows(x, vb, rx, wx, wy, wz, q, TOP, CY, off)
-        return carry
-
-    def third(x, carry):
-        e = x + W
-        res[pl.ds(pl.multiple_of(x * CY, CY), CY), :] = residual_rows(e, vc, rx, wx, wy, wz, q, TOP, CY, off)
-        return carry
-
-    lax.fori_loop(1, EX - 1, first, 0, unroll=2)
-    lax.fori_loop(2, EX - 2, second, 0, unroll=2)
-    lax.fori_loop(0, CX, third, 0, unroll=2)
-
-    def put(i, carry):
-        for u in range(48):
-            r = i * CY + TOP + u
+    def first(x, turn):
+        vb[x, own, :] = sweep_rows(x, va, *field, turn)
+
+    def second(x, turn):
+        vc[x, own, :] = sweep_rows(x, vb, *field, turn)
+
+    def third(x, turn):
+        rows = pl.ds(pl.multiple_of((x - W) * CY, CY), CY)
+        res[rows, :] = residual_rows(x, vc, *field, turn)
+
+    def put(x, carry):
+        for u in range(CY - 16):
+            r = (x - W) * CY + TOP + u
             buf[pl.ds(slot[r], 1), :] = res[pl.ds(r, 1), :]
         return carry
 
-    lax.fori_loop(0, CX, put, 0)
+    for lo, hi in ranges[0]:
+        lax.fori_loop(lo, hi, prep, 0)
+        wx[hi, own, :] = kx[hi, own, :] + kx[hi - 1, own, :]
+    for lo, hi in ranges[0]:
+        planes(lo, hi, va, wz, first)
+    for lo, hi in ranges[1]:
+        planes(lo, hi, vb, wz, second)
+    for lo, hi in ranges[2]:
+        planes(lo, hi, vc, wz, third)
+    for lo, hi in ranges[2]:
+        lax.fori_loop(lo, hi, put, 0)
+
+
+def core_kernel(slot, p_ref, k_ref, r_ref, buf_in, buf, kx, rx, va, vb, vc, wx, wy, wz, q, res, done):
+    del buf_in
+    fill((p_ref, k_ref, r_ref, None, None), (va, kx, rx), range(W, W + CX), None, None)
+    a, b = W + 1, W + CX - 1
+    ranges = (((a, b),), ((a + 1, b - 1),), ((a + 2, b - 2),))
+    inner_steps(ranges, slot, buf, kx, rx, va, vb, vc, wx, wy, wz, q, res, True, True)
+    done[...] = jnp.zeros_like(done)
+
+
+def mid_kernel(slot, bl, bh, *refs):
+    buf, kx, rx, va, vb, vc, wx, wy, wz, q, res = refs[11:]
+    xl, xh, _, _ = edges()
+    halo = [*range(W), *range(W + CX, EX)]
+    fill((None, None, None, bl, bh), (va, kx, rx), halo, xl, xh)
+    a, b = W + 1, W + CX - 1
+    ranges = tuple(((1 + i, a + i), (b - i, EX - 1 - i)) for i in range(3))
+    inner_steps(ranges, slot, buf, kx, rx, va, vb, vc, wx, wy, wz, q, res, xl, xh)
 
 
 def rim_kernel(
-    slot, sl, sh, kx_in, rx_in, va_in, vb_in, vc_in, wx_in, wy_in, wz_in, q_in, res, buf_in,
-    kx, rx, va, vb, vc, wx, wy, wz, q, buf,
+    slot_ref, sl, sh, kx_in, rx_in, va_in, vb_in, vc_in, wx_in, wy_in, wz_in, q_in, res, buf_in,
+    kx, rx, va, vb, vc, wx, wy, wz, q, buf, slot, sem,
 ):
-    del kx_in, rx_in, va_in, vb_in, vc_in, wx_in, wy_in, wz_in, q_in, buf_in
+    del kx_in, rx_in, va_in, vb_in, vc_in, wx_in, wy_in, wz_in, q_in, buf_in, res
+    table = pltpu.make_async_copy(slot_ref, slot, sem)
+    table.start()
     xl, xh, yl, yh = edges()
     off = zero_index()
     end = TOP + CY
@@ -224,33 +263,25 @@
     z, y = iota((8, NZ), 1), iota((8, NZ), 0)
     low_rows = (y >= 2) | yl
     high_rows = (y < 6) | yh
-
-    def prep(x, carry):
-        ok = ((x >= W) | xl) & ((x < W + CX) | xh)
+    field = (rx, wx, wy, wz, q)
+    for x in range(1, EX - 1):
+        ok = plane_ok(x, xl, xh)
+        ok = True if ok is None else ok
         prepare_rows(x, kx, wx, wy, wz, q, off + (TOP - 2), 8, None, low_rows & ok, z)
         prepare_rows(x, kx, wx, wy, wz, q, off + (end - 6), 8, off + (end - 5), high_rows & ok, z)
-        return carry
-
-    lax.fori_loop(1, EX - 1, prep, 0, unroll=4)
     for start in (TOP - 2, end - 6):
         rows = pl.ds(off + start, 8)
         wx[EX - 1, rows, :] = kx[EX - 1, rows, :] + kx[EX - 2, rows, :]
-
-    def first(x, carry):
+    for x in range(1, EX - 1):
         for start in (TOP - 2, end - 6):
-            vb[x, pl.ds(off + start, 8), :] = sweep_rows(x, va, rx, wx, wy, wz, q, off + start, 8, 0)
-        return carry
-
-    def second(x, carry):
+            vb[x, pl.ds(off + start, 8), :] = sweep_rows(x, va, *field, off + start, 8, 0)
+    for x in range(2, EX - 2):
         for start in (TOP - 1, end - 7):
-            vc[x, pl.ds(off + start, 8), :] = sweep_rows(x, vb, rx, wx, wy, wz, q, off + start, 8, 0)
-        return carry
-
-    lax.fori_loop(1, EX - 1, first, 0, unroll=4)
-    lax.fori_loop(2, EX - 2, second, 0, unroll=3)
+            vc[x, pl.ds(off + start, 8), :] = sweep_rows(x, vb, *field, off + start, 8, 0)
+    table.wait()
     for x in range(CX):
         for start in (TOP, end - 8):
-            out = residual_rows(x + W, vc, rx, wx, wy, wz, q, start, 8, off)
+            out = residual_rows(x + W, vc, *field, start, 8, off)
             for u in range(8):
                 buf[pl.ds(slot[x * CY + start - TOP + u], 1), :] = out[u : u + 1]
 
@@ -334,16 +365,16 @@
         vd[e, own, :] = keep(xl, bl[e - 1])
         vd[e + CX + 2, own, :] = keep(xh, bh[e - 1])
 
-    def first(x, carry):
-        ve[x, own, :] = sweep_rows(x, vd, rx, wx, wy, wz, q, TOP, CY, off)
-        return carry
-
-    def second(x, carry):
-        out[x] = sweep_rows(x + W, ve, rx, wx, wy, wz, q, TOP, CY, off)
-        return carry
-
-    lax.fori_loop(2, EX - 2, first, 0, unroll=2)
-    lax.fori_loop(0, CX, second, 0, unroll=2)
+    field = (rx, wx, wy, wz, q, TOP, CY, off)
+
+    def first(x, turn):
+        ve[x, own, :] = sweep_rows(x, vd, *field, turn)
+
+    def second(x, turn):
+        out[x - W] = sweep_rows(x, ve, *field, turn)
+
+    planes(2, EX - 2, vd, wz, first)
+    planes(W, W + CX, ve, wz, second)
 
 
 def last_rim_kernel(sl, sh, vd_in, ve_in, inner, rx, wx, wy, wz, q, vd, ve, out):
@@ -383,13 +414,15 @@
 
 
 def from_both(axis, to_high, to_low):
-    return lax.ppermute(to_high, axis, ring(axis, 1)), lax.ppermute(to_low, axis, ring(axis, -1))
+    low = lax.ppermute(to_high, axis, ring(axis, 1))
+    high = lax.ppermute(to_low, axis, ring(axis, -1))
+    return low, high
 
 
 EXT = ((EX, EY, NZ), F32)
 
 
-def per_device(pressure, rhs, kappa, owner, coarse_row, coarse_leak, coarse_link):
+def cycle(pressure, rhs, kappa, owner, coarse_row, coarse_leak, coarse_link):
     owners = lax.axis_size("bulk")
     slots = owners * BLOCK
     sent = ((2 * W + W - 1, CY, NZ), F32)
@@ -397,7 +430,9 @@
     to_high, to_low = call(
         send_kernel,
         [sent, sent],
-        (pressure, kappa, rhs),
+        [pltpu.with_memory_space_constraint(f, pltpu.MemorySpace.HBM) for f in (pressure, kappa, rhs)],
+        in_specs=[pl.BlockSpec(memory_space=pltpu.MemorySpace.HBM)] * 3,
+        scratch=[pltpu.SemaphoreType.DMA((6,))],
         mib=2,
     )
     bl, bh = from_both("bulk", to_high, to_low)
@@ -406,23 +441,32 @@
         [((8, 128), I32), ((slots, NZ), F32)],
         (owner.reshape(8, 128), coarse_row.reshape(8, 128)),
     )
-    to_high, to_low = call(side_kernel, [side, side], (pressure, kappa, rhs, bl, bh, slot))
-    slot = slot.reshape(CX * CY)
+    table = slot.reshape(CX * CY)
+    work = [((slots, NZ), F32)] + [EXT] * 9 + [((CX * CY, NZ), F32)]
+    *core, done = call(
+        core_kernel,
+        work + [((8, NZ), F32)],
+        (table, pressure, kappa, rhs, buf),
+        in_specs=[SMEM] + [VMEM] * 4,
+        aliases={4: 0},
+        mib=20,
+    )
+    to_high, to_low = call(side_kernel, [side, side], (pressure, kappa, rhs, bl, bh, done))
     sl, sh = from_both("slab", to_high, to_low)
     buf, *ext, res = call(
-        inner_kernel,
-        [((slots, NZ), F32)] + [EXT] * 9 + [((CX * CY, NZ), F32)],
-        (slot, pressure, kappa, rhs, bl, bh, buf),
-        in_specs=[SMEM] + [VMEM] * 6,
-        aliases={6: 0},
+        mid_kernel,
+        work,
+        (table, bl, bh, *core),
+        in_specs=[SMEM] + [VMEM] * 13,
+        aliases={3 + i: i for i in range(11)},
         mib=20,
     )
     *ext, buf = call(
         rim_kernel,
         [EXT] * 9 + [((slots, NZ), F32)],
-        (slot, sl, sh, *ext, res, buf),
-        in_specs=[SMEM] + [VMEM] * 13,
+        (table, sl, sh, *ext, res, buf),
         aliases={**{3 + i: i for i in range(9)}, 13: 9},
+        scratch=[pltpu.SMEM((CX * CY,), I32), pltpu.SemaphoreType.DMA],
         mib=20,
     )
     _, rx, _, _, vc, wx, wy, wz, q = ext
@@ -435,12 +479,10 @@
     )
     back = lax.all_to_all(back.reshape(owners, BLOCK, 1, NZ), "bulk", 0, 0).reshape(slots, NZ)
     to_high, to_low = call(
-        edge_kernel, [((2, CY, NZ), F32)] * 2, (slot, back, vc), in_specs=[SMEM, VMEM, VMEM]
+        edge_kernel, [((2, CY, NZ), F32)] * 2, (table, back, vc), in_specs=[SMEM, VMEM, VMEM]
     )
     bl, bh = from_both("bulk", to_high, to_low)
-    (vd,) = call(
-        body_kernel, [EXT], (slot, back, vc, to_high, to_low), in_specs=[SMEM] + [VMEM] * 4
-    )
+    (vd,) = call(body_kernel, [EXT], (table, back, vc, to_high, to_low), in_specs=[SMEM] + [VMEM] * 4)
 
     def rim(lo, hi):
         return jnp.concatenate([bl[1:, lo:hi], vd[W : W + CX, TOP + lo : TOP + hi], bh[:1, lo:hi]], axis=0)
@@ -465,7 +507,7 @@
 
 def solution(mesh):
     return jax.shard_map(
-        per_device,
+        cycle,
         mesh=mesh,
         in_specs=(
             P("bulk", "slab", None),

time: 130 us -> 127 us (0.977)
  Pallas kernels: 17.1 us -> 23.1 us
  waiting for transfers between devices: 6.96 us -> 1.97 us
  local copies, waits for them, and re-layouts: 3.86 us -> 0.74 us
  blocking collectives: 84.4 us -> 82.5 us
    pallas_call x10 -> x11, Pallas kernels: 17.1 us -> 23.1 us  [call(): pl.pallas_call(kernel, out_shape=[jax.ShapeDtypeStruct(s, d) for s, d in...]
    ppermute x8, waiting for transfers between devices: 6.96 us -> 1.97 us  [the longest x4 1.39 us: from_both(): high = lax.ppermute(to_low, axis, ring(axis, -1))]
    unnamed x20 -> x14, local copies, waits for them, and re-layouts: 3.84 us -> 0.71 us
    all_to_all x2, blocking collectives: 84.4 us -> 82.5 us  [the longest x1 42.1 us: cycle(): got = lax.all_to_all(buf.reshape(owners, BLOCK, 1, NZ), 'bulk', 0, 0)]
  transfers between devices with their start and end apart: 8 -> 8, of which waited for: 4 -> 2; matrix products, arithmetic and copies ran while one was open for 0% -> 0% of each run, Pallas kernels for 7% -> 12%
where the time goes in v3:
time: 127 us
  blocking collectives  82.5 us (65%)
  Pallas kernels  23.1 us (18%)
  starting transfers between devices  18.4 us (14%)
  waiting for transfers between devices  1.97 us (2%)
    all_to_all x1, blocking collectives, cycle(): got = lax.all_to_all(buf.reshape(owners, BLOCK, 1, NZ), 'bulk', 0, 0)  42.1 us
    all_to_all x1, blocking collectives, cycle(): lax.all_to_all(back.reshape(owners, BLOCK, 1, NZ), 'bulk', 0, 0)  40.4 us
    pallas_call x11, Pallas kernels, call(): pl.pallas_call(kernel, out_shape=[jax.ShapeDtypeStruct(s, d) for s, d in...  23.1 us
    ppermute x4, starting transfers between devices, from_both(): high = lax.ppermute(to_low, axis, ring(axis, -1))  15.3 us
    ppermute x4, starting transfers between devices, from_both(): low = lax.ppermute(to_high, axis, ring(axis, 1))  3.05 us
  transfers between devices with their start and end apart: 8, of which 2 were waited for; matrix products, arithmetic and copies ran while one was open for 0% of the time, Pallas kernels for 12%

profile of v3, /device:TPU:24, one launch (start us, length us, event | category | flops | bytes accessed | tf_op | source)
XLA Modules:
  0.0 126.9 jit_solution(5494681087618675839)
XLA Ops:
  0.0 1.2 shard_map.74
  1.3 0.1 collective-permute-start
  1.4 7.6 %collective-permute-start.1 = (f32[8,64,128]{2,1,0:T(8,128)S(1)}, f32[8,64,128]{2,1,0:T(8,128)S(1)}, u32[]{:S(2)}, u32[]{:S(2)}) collective-permute-start(f32[8,64,128]{2,1,0:T(8,128)S(1)} %get-tuple-element.49), channel_id=1, source_target_pairs={{0,252},{4,0},{8,4},{12,8},{16,12},{20,16},{24,20},{28,24},{32,28}... | collective-permute-start | bytes 786440 | tf_op jit(solution)/shard_map/ppermute | solution.py:418
  8.9 0.7 copy-done.6
  9.6 0.8 shard_map.73
  10.4 6.4 %shard_map.75 = (f32[2624,128]{1,0:T(8,128)S(1)}, f32[22,80,128]{2,1,0:T(8,128)S(1)}, f32[22,80,128]{2,1,0:T(8,128)S(1)}, f32[22,80,128]{2,1,0:T(8,128)S(1)}, f3...) custom-call(s32[1024]{0:T(1024)S(1)} %bitcast.14, ...), custom_call_target="tpu_custom_call", output_to_operand_aliasing={{0}: (4, {})} | custom-call | tf_op jit(solution)/shard_map/pallas_call | solution.py:29
  16.9 0.3 collective-permute-start.2
  17.2 1.8 %collective-permute-start.3 = (f32[20,8,128]{2,1,0:T(8,128)S(1)}, f32[20,8,128]{2,1,0:T(8,128)S(1)}, u32[]{:S(2)}, u32[]{:S(2)}) collective-permute-start(f32[20,8,128]{2,1,0:T(8,128)S(1)} %get-tuple-element.53), channel_id=1, source_target_pairs={{0,3},{1,0},{2,1},{3,2},{4,7},{5,4},{6,5},{7,6},{8,11},{9,8},{10,9... | collective-permute-start | bytes 245768 | tf_op jit(solution)/shard_map/ppermute | solution.py:418
  19.0 3.8 %shard_map.77 = (f32[2624,128]{1,0:T(8,128)S(1)}, f32[22,80,128]{2,1,0:T(8,128)S(1)}, f32[22,80,128]{2,1,0:T(8,128)S(1)}, f32[22,80,128]{2,1,0:T(8,128)S(1)}, f3...) custom-call(s32[1024]{0:T(1024)S(1)} %bitcast.15, ...), custom_call_target="tpu_custom_call", output_to_operand_aliasing={{0}: (3, {}), {1}: (4, {}), {2}: (5, {}), {3}: (6, {}), {4}... | custom-call | tf_op jit(solution)/shard_map/pallas_call | solution.py:29
  22.8 0.9 shard_map.78
  23.8 42.1 %all_to_all.10 = f32[64,41,1,128]{3,2,1,0:T(1,128)S(1)} all-to-all(f32[64,41,1,128]{3,2,1,0:T(1,128)S(1)} %bitcast.9), channel_id=1, replica_groups=mesh['bulk'=64,'slab'=4] {'bulk'}, dimensions={0} | all-to-all | bytes 2686976 | tf_op jit(solution)/shard_map/all_to_all | solution.py:473
  65.8 2.7 %shard_map.79 = f32[2624,128]{1,0:T(8,128)S(1)} custom-call(f32[2624,128]{1,0:T(8,128)S(1)} %bitcast.12, f32[128,128]{1,0:T(8,128)S(1)} %bitcast.19, f32[128,128]{1,0:T(8,128)S(1)} %bitcast.20), custom_call_target="tpu_custom_call" | custom-call | tf_op jit(solution)/shard_map/pallas_call | solution.py:29
  68.5 40.4 %all_to_all.11 = f32[64,41,1,128]{3,2,1,0:T(1,128)S(1)} all-to-all(f32[64,41,1,128]{3,2,1,0:T(1,128)S(1)} %bitcast.13), channel_id=1, replica_groups=mesh['bulk'=64,'slab'=4] {'bulk'}, dimensions={0} | all-to-all | bytes 2686976 | tf_op jit(solution)/shard_map/all_to_all | solution.py:480
  108.9 0.8 shard_map.80
  109.7 0.1 collective-permute-start.4
  109.8 1.3 %shard_map.81.vd_in = f32[22,80,128]{2,1,0:T(8,128)S(1)} custom-call(s32[1024]{0:T(1024)S(1)} %bitcast.18, f32[2624,128]{1,0:T(8,128)S(1)} %bitcast.11, f32[22,80,128]{2,1,0:T(8,128)S(1)} %get-tuple-element.77.vc, f32[2,64,128]{2,1,0:T(8,128)S(1)} %get-tuple-element.78.to_high, f32[2,64,128]{2,1,0:T(8,128)S(1)} %get-tuple-element.79.to_low), custom_call_target="tpu_custom_call" | custom-call | tf_op jit(solution)/shard_map/pallas_call | solution.py:29
  111.1 5.1 %collective-permute-start.5 = (f32[2,64,128]{2,1,0:T(8,128)S(1)}, f32[2,64,128]{2,1,0:T(8,128)S(1)}, u32[]{:S(2)}, u32[]{:S(2)}) collective-permute-start(f32[2,64,128]{2,1,0:T(8,128)S(1)} %get-tuple-element.79.to_low), channel_id=1, source_target_pairs={{0,252},{4,0},{8,4},{12,8},{16,12},{20,16},{24,20},{28,24},{32,28}... | collective-permute-start | bytes 196616 | tf_op jit(solution)/shard_map/ppermute | solution.py:418
  116.2 0.6 collective-permute-done.4.bl
  116.8 1.3 %collective-permute-done.5.bh = f32[2,64,128]{2,1,0:T(8,128)S(1)} collective-permute-done((f32[2,64,128]{2,1,0:T(8,128)S(1)}, f32[2,64,128]{2,1,0:T(8,128)S(1)}, u32[]{:S(2)}, u32[]{:S(2)}) %collective-permute-start.5) | collective-permute-done | bytes 65568 | tf_op jit(solution)/shard_map/ppermute | solution.py:418
  118.1 0.8 collective-permute-start.7
  118.9 2.6 %collective-permute-start.6 = (f32[18,2,128]{2,1,0:T(2,128)S(1)}, f32[18,2,128]{2,1,0:T(2,128)S(1)}, u32[]{:S(2)}, u32[]{:S(2)}) collective-permute-start(f32[18,2,128]{2,1,0:T(2,128)S(1)} %pad_maximum_fusion), channel_id=1, source_target_pairs={{0,1},{1,2},{2,3},{3,0},{4,5},{5,6},{6,7},{7,4},{8,9},{9,10},{10,1... | collective-permute-start | bytes 55304 | tf_op jit(solution)/shard_map/ppermute | solution.py:417
  121.5 3.5 %shard_map.82 = (f32[22,80,128]{2,1,0:T(8,128)S(1)}, f32[22,80,128]{2,1,0:T(8,128)S(1)}, f32[16,64,128]{2,1,0:T(8,128)S(1)}) custom-call(f32[22,80,128]{2,1,0:T(8,128)S(1)} %shard_map.81.vd_in, f32[2,64,128]{2,1,0:T(8,128)S(1)} %collective-permute-done.4.bl, f32[2,64,128]{2,1,0:T(8,128)S(1)} %collective-permute-done.5.bh, ...), custom_call_target="tpu_custom_call", output_to_operand_aliasing={{0}: (0, {})} | custom-call | tf_op jit(solution)/shard_map/pallas_call | solution.py:29
  125.1 0.0 collective-permute-done.7.sh
  125.1 1.8 %shard_map.83 = (f32[22,80,128]{2,1,0:T(8,128)S(1)}, f32[22,80,128]{2,1,0:T(8,128)S(1)}, f32[16,64,128]{2,1,0:T(8,128)}) custom-call(f32[18,2,128]{2,1,0:T(2,128)S(1)} %collective-permute-done.6.sl, f32[18,2,128]{2,1,0:T(2,128)S(1)} %collective-permute-done.7.sh, ...), custom_call_target="tpu_custom_call", output_to_operand_aliasing={{0}: (2, {}), {1}: (3, {})} | custom-call | tf_op jit(solution)/shard_map/pallas_call | solution.py:29
  (24 shorter events, 0.2 us)
Async XLA Ops:
  0.0 10.4 %copy-start = (f32[16,64,128]{2,1,0:T(8,128)S(1)}, f32[16,64,128]{2,1,0:T(8,128)}, u32[]{:S(2)}) copy-start(f32[16,64,128]{2,1,0:T(8,128)} %p_ref.5) | copy-start | bytes 1572868
  0.0 10.4 %copy-start.2 = (f32[16,64,128]{2,1,0:T(8,128)S(1)}, f32[16,64,128]{2,1,0:T(8,128)}, u32[]{:S(2)}) copy-start(f32[16,64,128]{2,1,0:T(8,128)} %r_ref.5) | copy-start | bytes 1572868
  0.0 10.4 %copy-start.1 = (f32[16,64,128]{2,1,0:T(8,128)S(1)}, f32[16,64,128]{2,1,0:T(8,128)}, u32[]{:S(2)}) copy-start(f32[16,64,128]{2,1,0:T(8,128)} %k_ref.5) | copy-start | bytes 1572868
  0.0 8.9 %copy-start.5 = (s32[1,1,1024,1]{2,3,1,0:T(1,128)S(1)}, s32[1,1,1024,1]{2,3,1,0:T(1,128)}, u32[]{:S(2)}) copy-start(s32[1,1,1024,1]{2,3,1,0:T(1,128)} %param.10) | copy-start | bytes 12292
  1.3 15.5 %collective-permute-start = (f32[8,64,128]{2,1,0:T(8,128)S(1)}, f32[8,64,128]{2,1,0:T(8,128)S(1)}, u32[]{:S(2)}, u32[]{:S(2)}) collective-permute-start(f32[8,64,128]{2,1,0:T(8,128)S(1)} %get-tuple-element.48), channel_id=1, source_target_pairs={{0,4},{4,8},{8,12},{12,16},{16,20},{20,24},{24,28},{28,32},{32,36}... | collective-permute-start | bytes 786440 | tf_op jit(solution)/shard_map/ppermute | solution.py:417
  1.4 15.5 %collective-permute-start.1 = (f32[8,64,128]{2,1,0:T(8,128)S(1)}, f32[8,64,128]{2,1,0:T(8,128)S(1)}, u32[]{:S(2)}, u32[]{:S(2)}) collective-permute-start(f32[8,64,128]{2,1,0:T(8,128)S(1)} %get-tuple-element.49), channel_id=1, source_target_pairs={{0,252},{4,0},{8,4},{12,8},{16,12},{20,16},{24,20},{28,24},{32,28}... | collective-permute-start | bytes 786440 | tf_op jit(solution)/shard_map/ppermute | solution.py:418
  8.9 0.7 copy-start.6
  16.9 5.9 %collective-permute-start.2 = (f32[20,8,128]{2,1,0:T(8,128)S(1)}, f32[20,8,128]{2,1,0:T(8,128)S(1)}, u32[]{:S(2)}, u32[]{:S(2)}) collective-permute-start(f32[20,8,128]{2,1,0:T(8,128)S(1)} %get-tuple-element.52), channel_id=1, source_target_pairs={{0,1},{1,2},{2,3},{3,0},{4,5},{5,6},{6,7},{7,4},{8,9},{9,10},{10,1... | collective-permute-start | bytes 245768 | tf_op jit(solution)/shard_map/ppermute | solution.py:417
  17.2 5.7 %collective-permute-start.3 = (f32[20,8,128]{2,1,0:T(8,128)S(1)}, f32[20,8,128]{2,1,0:T(8,128)S(1)}, u32[]{:S(2)}, u32[]{:S(2)}) collective-permute-start(f32[20,8,128]{2,1,0:T(8,128)S(1)} %get-tuple-element.53), channel_id=1, source_target_pairs={{0,3},{1,0},{2,1},{3,2},{4,7},{5,4},{6,5},{7,6},{8,11},{9,8},{10,9... | collective-permute-start | bytes 245768 | tf_op jit(solution)/shard_map/ppermute | solution.py:418
  23.7 42.1 %copy-start.3 = (f32[1,128,128]{2,1,0:T(8,128)S(1)}, f32[1,128,128]{2,1,0:T(8,128)}, u32[]{:S(2)}) copy-start(f32[1,128,128]{2,1,0:T(8,128)} %param.12) | copy-start | bytes 196612
  23.7 42.1 %copy-start.4 = (f32[1,128,128]{2,1,0:T(8,128)S(1)}, f32[1,128,128]{2,1,0:T(8,128)}, u32[]{:S(2)}) copy-start(f32[1,128,128]{2,1,0:T(8,128)} %param.13) | copy-start | bytes 196612
  109.7 7.1 %collective-permute-start.4 = (f32[2,64,128]{2,1,0:T(8,128)S(1)}, f32[2,64,128]{2,1,0:T(8,128)S(1)}, u32[]{:S(2)}, u32[]{:S(2)}) collective-permute-start(f32[2,64,128]{2,1,0:T(8,128)S(1)} %get-tuple-element.78.to_high), channel_id=1, source_target_pairs={{0,4},{4,8},{8,12},{12,16},{16,20},{20,24},{24,28},{28,32},{32,36}... | collective-permute-start | bytes 196616 | tf_op jit(solution)/shard_map/ppermute | solution.py:417
  111.1 7.0 %collective-permute-start.5 = (f32[2,64,128]{2,1,0:T(8,128)S(1)}, f32[2,64,128]{2,1,0:T(8,128)S(1)}, u32[]{:S(2)}, u32[]{:S(2)}) collective-permute-start(f32[2,64,128]{2,1,0:T(8,128)S(1)} %get-tuple-element.79.to_low), channel_id=1, source_target_pairs={{0,252},{4,0},{8,4},{12,8},{16,12},{20,16},{24,20},{28,24},{32,28}... | collective-permute-start | bytes 196616 | tf_op jit(solution)/shard_map/ppermute | solution.py:418
  118.1 7.0 %collective-permute-start.7 = (f32[18,2,128]{2,1,0:T(2,128)S(1)}, f32[18,2,128]{2,1,0:T(2,128)S(1)}, u32[]{:S(2)}, u32[]{:S(2)}) collective-permute-start(f32[18,2,128]{2,1,0:T(2,128)S(1)} %pad_maximum_fusion.1), channel_id=1, source_target_pairs={{0,3},{1,0},{2,1},{3,2},{4,7},{5,4},{6,5},{7,6},{8,11},{9,8},{10,9... | collective-permute-start | bytes 55304 | tf_op jit(solution)/shard_map/ppermute | solution.py:418
  118.9 6.2 %collective-permute-start.6 = (f32[18,2,128]{2,1,0:T(2,128)S(1)}, f32[18,2,128]{2,1,0:T(2,128)S(1)}, u32[]{:S(2)}, u32[]{:S(2)}) collective-permute-start(f32[18,2,128]{2,1,0:T(2,128)S(1)} %pad_maximum_fusion), channel_id=1, source_target_pairs={{0,1},{1,2},{2,3},{3,0},{4,5},{5,6},{6,7},{7,4},{8,9},{9,10},{10,1... | collective-permute-start | bytes 55304 | tf_op jit(solution)/shard_map/ppermute | solution.py:417

commit v4 on v3

--- a/solution.py
+++ b/solution.py
@@ -132,41 +132,27 @@
         wy[x, pl.ds(wy_start, n), :] = k_ref[x, pl.ds(wy_start, n), :] + k_ref[x, pl.ds(wy_start - 1, n), :]
 
 
-def turned(x, v_ref, wz, start, n):
-    v = v_ref[x, pl.ds(start, n), :]
-    return pltpu.roll(v, 1, 1), pltpu.roll(wz[x, pl.ds(start, n), :] * v, NZ - 1, 1)
-
-
-def neighbours(x, v_ref, wx, wy, wz, start, n, off, turn):
+def neighbours(x, v_ref, wx, wy, wz, start, n, off):
     rows, below, above = pl.ds(start, n), pl.ds(off + (start - 1), n), pl.ds(off + (start + 1), n)
+    v = v_ref[x, rows, :]
+    wzl = wz[x, rows, :]
     total = wx[x, rows, :] * v_ref[x - 1, rows, :] + wx[x + 1, rows, :] * v_ref[x + 1, rows, :]
     total = total + (wy[x, rows, :] * v_ref[x, below, :] + wy[x, above, :] * v_ref[x, above, :])
-    return v_ref[x, rows, :], total + (wz[x, rows, :] * turn[0] + turn[1])
-
-
-def sweep_rows(x, old, r2, wx, wy, wz, q, start, n, off, turn=None):
-    turn = turn or turned(x, old, wz, start, n)
-    v, total = neighbours(x, old, wx, wy, wz, start, n, off, turn)
+    return v, total + (wzl * pltpu.roll(v, 1, 1) + pltpu.roll(wzl * v, NZ - 1, 1))
+
+
+def sweep_rows(x, old, r2, wx, wy, wz, q, start, n, off):
+    v, total = neighbours(x, old, wx, wy, wz, start, n, off)
     rows = pl.ds(start, n)
     return (1.0 - DAMPING) * v + q[x, rows, :] * (r2[x, rows, :] + total)
 
 
-def residual_rows(x, old, r2, wx, wy, wz, q, start, n, off, turn=None):
-    turn = turn or turned(x, old, wz, start, n)
-    v, total = neighbours(x, old, wx, wy, wz, start, n, off, turn)
+def residual_rows(x, old, r2, wx, wy, wz, q, start, n, off):
+    v, total = neighbours(x, old, wx, wy, wz, start, n, off)
     rows = pl.ds(start, n)
     damped = q[x, rows, :]
     diagonal = DAMPING / jnp.where(damped == 0.0, 1.0, damped)
     return 0.5 * ((r2[x, rows, :] + total) - diagonal * v)
-
-
-def planes(first, last, old, wz, body):
-    def step(x, turn):
-        ahead = turned(x + 1, old, wz, TOP, CY)
-        body(x, turn)
-        return ahead
-
-    lax.fori_loop(first, last, step, turned(first, old, wz, TOP, CY))
 
 
 def fill(refs, fields, some, xl, xh):
@@ -185,38 +171,23 @@
     own = pl.ds(TOP, CY)
     field = (rx, wx, wy, wz, q, TOP, CY, off)
 
-    def prep(x, carry):
-        ok = ((x >= W) | xl) & ((x < W + CX) | xh)
-        prepare_rows(x, kx, wx, wy, wz, q, TOP, CY, None, ok, z)
-        return carry
-
-    def first(x, turn):
-        vb[x, own, :] = sweep_rows(x, va, *field, turn)
-
-    def second(x, turn):
-        vc[x, own, :] = sweep_rows(x, vb, *field, turn)
-
-    def third(x, turn):
-        rows = pl.ds(pl.multiple_of((x - W) * CY, CY), CY)
-        res[rows, :] = residual_rows(x, vc, *field, turn)
-
-    def put(x, carry):
-        for u in range(CY - 16):
-            r = (x - W) * CY + TOP + u
-            buf[pl.ds(slot[r], 1), :] = res[pl.ds(r, 1), :]
-        return carry
-
     for lo, hi in ranges[0]:
-        lax.fori_loop(lo, hi, prep, 0)
+        for x in range(lo, hi):
+            ok = plane_ok(x, xl, xh)
+            prepare_rows(x, kx, wx, wy, wz, q, TOP, CY, None, True if ok is None else ok, z)
         wx[hi, own, :] = kx[hi, own, :] + kx[hi - 1, own, :]
     for lo, hi in ranges[0]:
-        planes(lo, hi, va, wz, first)
+        for x in range(lo, hi):
+            vb[x, own, :] = sweep_rows(x, va, *field)
     for lo, hi in ranges[1]:
-        planes(lo, hi, vb, wz, second)
+        for x in range(lo, hi):
+            vc[x, own, :] = sweep_rows(x, vb, *field)
     for lo, hi in ranges[2]:
-        planes(lo, hi, vc, wz, third)
-    for lo, hi in ranges[2]:
-        lax.fori_loop(lo, hi, put, 0)
+        for x in range(lo, hi):
+            at = (x - W) * CY
+            res[at : at + CY, :] = residual_rows(x, vc, *field)
+            for r in range(at + TOP, at + CY - TOP):
+                buf[pl.ds(slot[r], 1), :] = res[r : r + 1, :]
 
 
 def core_kernel(slot, p_ref, k_ref, r_ref, buf_in, buf, kx, rx, va, vb, vc, wx, wy, wz, q, res, done):
@@ -293,11 +264,12 @@
     return a, b, (rest - b.astype(F32)).astype(BF16)
 
 
-def coarse_kernel(owners, data, leak_ref, link_ref, back, hot):
+def coarse_kernel(owners, data, leak_ref, link_ref, back, hot, parts):
     rows = owners * BLOCK
     groups = -(-owners // 3)
+    pairs = -(-groups // 2)
     number = (iota((CR, 128), 0) + 1).astype(F32)
-    total = jnp.zeros((CR, NZ), F32)
+    total = jnp.zeros((CR, 3 * NZ), F32)
     bases = []
     for g in range(groups):
         base = g * TRIO
@@ -309,10 +281,16 @@
             name = pltpu.roll(jnp.broadcast_to(name, (8, 128)), base - (rows - 128), 1)[0:1]
             base = rows - 128
         bases.append(base)
-        one_hot = jnp.where(number == name, 1.0, 0.0).astype(BF16)
-        hot[g] = one_hot
-        for part in parts_of(data[base : base + 128, :]):
-            total = total + jnp.dot(one_hot, part, preferred_element_type=F32)
+        at = g % 2 * 128
+        hot[g // 2, :, at : at + 128] = jnp.where(number == name, 1.0, 0.0).astype(BF16)
+        for i, part in enumerate(parts_of(data[base : base + 128, :])):
+            parts[g // 2, at : at + 128, i * NZ : (i + 1) * NZ] = part
+    if groups % 2:
+        hot[pairs - 1, :, 128:] = jnp.zeros((CR, 128), BF16)
+        parts[pairs - 1, 128:, :] = jnp.zeros((128, 3 * NZ), BF16)
+    for p in range(pairs):
+        total = total + jnp.dot(hot[p], parts[p], preferred_element_type=F32)
+    total = total[:, 0:NZ] + (total[:, NZ : 2 * NZ] + total[:, 2 * NZ :])
 
     z = iota((CR, NZ), 1)
     link = link_ref[...]
@@ -322,15 +300,15 @@
     u = w * total
     for _ in range(2):
         u = (1.0 - DAMPING) * u + w * (total + inner * pltpu.roll(u, NZ - 1, 1) + pltpu.roll(inner * u, 1, 1))
-    pieces = parts_of(u)
-    for g in range(groups - 1, -1, -1):
-        out = jnp.zeros((128, NZ), F32)
-        for part in pieces:
-            out = out + lax.dot_general(hot[g], part, (((0,), (0,)), ((), ())), preferred_element_type=F32)
-        if g == groups - 1:
-            back[bases[g] : bases[g] + 128, :] = out
-        else:
-            back[bases[g] : bases[g] + TRIO, :] = out[0:TRIO]
+    pieces = jnp.concatenate(parts_of(u), axis=1)
+    for p in range(pairs - 1, -1, -1):
+        out = lax.dot_general(hot[p], pieces, (((0,), (0,)), ((), ())), preferred_element_type=F32)
+        out = out[:, 0:NZ] + (out[:, NZ : 2 * NZ] + out[:, 2 * NZ :])
+        for g in (2 * p + 1, 2 * p):
+            if g < groups:
+                n = 128 if g == groups - 1 else TRIO
+                at = g % 2 * 128
+                back[bases[g] : bases[g] + n, :] = out[at : at + n]
 
 
 EDGE = (0, 1, CX - 2, CX - 1)
@@ -367,14 +345,10 @@
 
     field = (rx, wx, wy, wz, q, TOP, CY, off)
 
-    def first(x, turn):
-        ve[x, own, :] = sweep_rows(x, vd, *field, turn)
-
-    def second(x, turn):
-        out[x - W] = sweep_rows(x, ve, *field, turn)
-
-    planes(2, EX - 2, vd, wz, first)
-    planes(W, W + CX, ve, wz, second)
+    for x in range(2, EX - 2):
+        ve[x, own, :] = sweep_rows(x, vd, *field)
+    for x in range(CX):
+        out[x] = sweep_rows(x + W, ve, *field)
 
 
 def last_rim_kernel(sl, sh, vd_in, ve_in, inner, rx, wx, wy, wz, q, vd, ve, out):
@@ -392,20 +366,14 @@
             vd[e, TOP - 2 : TOP, :] = jnp.zeros((2, NZ), F32)
             vd[e, end : end + 2, :] = jnp.zeros((2, NZ), F32)
 
-    def first(x, carry):
+    field = (rx, wx, wy, wz, q)
+    for x in range(2, EX - 2):
         for start in (TOP - 1, end - 7):
-            ve[x, pl.ds(off + start, 8), :] = sweep_rows(x, vd, rx, wx, wy, wz, q, off + start, 8, 0)
-        return carry
-
-    lax.fori_loop(2, EX - 2, first, 0, unroll=3)
-
-    def second(x, carry):
+            ve[x, pl.ds(off + start, 8), :] = sweep_rows(x, vd, *field, off + start, 8, 0)
+    for x in range(CX):
         out[x, 8 : CY - 8, :] = inner[x, 8 : CY - 8, :]
         for start in (TOP, end - 8):
-            out[x, start - TOP : start - TOP + 8, :] = sweep_rows(x + W, ve, rx, wx, wy, wz, q, start, 8, off)
-        return carry
-
-    lax.fori_loop(0, CX, second, 0, unroll=4)
+            out[x, start - TOP : start - TOP + 8, :] = sweep_rows(x + W, ve, *field, start, 8, off)
 
 
 def ring(axis, step):
@@ -475,7 +443,7 @@
         lambda *refs: coarse_kernel(owners, *refs),
         [((slots, NZ), F32)],
         (got.reshape(slots, NZ), coarse_leak[0], coarse_link[0]),
-        scratch=[pltpu.VMEM((-(-owners // 3), CR, 128), BF16)],
+        scratch=[pltpu.VMEM((-(-owners // 6), CR, 256), BF16), pltpu.VMEM((-(-owners // 6), 256, 3 * NZ), BF16)],
     )
     back = lax.all_to_all(back.reshape(owners, BLOCK, 1, NZ), "bulk", 0, 0).reshape(slots, NZ)
     to_high, to_low = call(

time: 127 us -> 122 us (0.961)
  Pallas kernels: 23.1 us -> 13 us
  waiting for transfers between devices: 1.97 us -> 4.88 us
    pallas_call x11, Pallas kernels: 23.1 us -> 13 us  [call(): pl.pallas_call(kernel, out_shape=[jax.ShapeDtypeStruct(s, d) for s, d in...]
    ppermute x4, waiting for transfers between devices: 1.39 us -> 3.29 us  [from_both(): high = lax.ppermute(to_low, axis, ring(axis, -1))]
  transfers between devices with their start and end apart: 8 -> 8, of which waited for: 2 -> 6; matrix products, arithmetic and copies ran while one was open for 0% -> 0% of each run, Pallas kernels for 12% -> 6%
where the time goes in v4:
time: 122 us; the launch traced here: 121 us
  blocking collectives  83.7 us (69%)
  starting transfers between devices  18.4 us (15%)
  Pallas kernels  13 us (11%)
  waiting for transfers between devices  4.88 us (4%)
    all_to_all x1, blocking collectives, cycle(): got = lax.all_to_all(buf.reshape(owners, BLOCK, 1, NZ), 'bulk', 0, 0)  43.3 us
    all_to_all x1, blocking collectives, cycle(): lax.all_to_all(back.reshape(owners, BLOCK, 1, NZ), 'bulk', 0, 0)  40.4 us
    ppermute x4, starting transfers between devices, from_both(): high = lax.ppermute(to_low, axis, ring(axis, -1))  15 us
    pallas_call x11, Pallas kernels, call(): pl.pallas_call(kernel, out_shape=[jax.ShapeDtypeStruct(s, d) for s, d in...  13 us
    ppermute x4, starting transfers between devices, from_both(): low = lax.ppermute(to_high, axis, ring(axis, 1))  3.33 us
    ppermute x4, waiting for transfers between devices, from_both(): high = lax.ppermute(to_low, axis, ring(axis, -1))  3.29 us
  transfers between devices with their start and end apart: 8, of which 6 were waited for; matrix products, arithmetic and copies ran while one was open for 0% of the time, Pallas kernels for 6%

profile of v4, /device:TPU:24, one launch (start us, length us, event | category | flops | bytes accessed | tf_op | source)
XLA Modules:
  0.0 120.8 jit_solution(13544046220353322580)
XLA Ops:
  0.0 1.2 %shard_map.74 = (f32[8,64,128]{2,1,0:T(8,128)S(1)}, f32[8,64,128]{2,1,0:T(8,128)S(1)}) custom-call(f32[16,64,128]{2,1,0:T(8,128)} %p_ref.5, f32[16,64,128]{2,1,0:T(8,128)} %k_ref.5, f32[16,64,128]{2,1,0:T(8,128)} %r_ref.5), custom_call_target="tpu_custom_call" | custom-call | tf_op jit(solution)/shard_map/pallas_call | solution.py:29
  1.4 7.6 %collective-permute-start.1 = (f32[8,64,128]{2,1,0:T(8,128)S(1)}, f32[8,64,128]{2,1,0:T(8,128)S(1)}, u32[]{:S(2)}, u32[]{:S(2)}) collective-permute-start(f32[8,64,128]{2,1,0:T(8,128)S(1)} %get-tuple-element.49), channel_id=1, source_target_pairs={{0,252},{4,0},{8,4},{12,8},{16,12},{20,16},{24,20},{28,24},{32,28}... | collective-permute-start | bytes 786440 | tf_op jit(solution)/shard_map/ppermute | solution.py:386
  8.9 0.7 copy-done.6
  9.6 0.8 shard_map.73
  10.4 2.4 %shard_map.75 = (f32[2624,128]{1,0:T(8,128)S(1)}, f32[22,80,128]{2,1,0:T(8,128)S(1)}, f32[22,80,128]{2,1,0:T(8,128)S(1)}, f32[22,80,128]{2,1,0:T(8,128)S(1)}, f3...) custom-call(s32[1024]{0:T(1024)S(1)} %bitcast.14, ...), custom_call_target="tpu_custom_call", output_to_operand_aliasing={{0}: (4, {})} | custom-call | tf_op jit(solution)/shard_map/pallas_call | solution.py:29
  12.9 0.3 collective-permute-start.2
  13.2 1.8 %collective-permute-start.3 = (f32[20,8,128]{2,1,0:T(8,128)S(1)}, f32[20,8,128]{2,1,0:T(8,128)S(1)}, u32[]{:S(2)}, u32[]{:S(2)}) collective-permute-start(f32[20,8,128]{2,1,0:T(8,128)S(1)} %get-tuple-element.53), channel_id=1, source_target_pairs={{0,3},{1,0},{2,1},{3,2},{4,7},{5,4},{6,5},{7,6},{8,11},{9,8},{10,9... | collective-permute-start | bytes 245768 | tf_op jit(solution)/shard_map/ppermute | solution.py:386
  15.0 1.5 %shard_map.77 = (f32[2624,128]{1,0:T(8,128)S(1)}, f32[22,80,128]{2,1,0:T(8,128)S(1)}, f32[22,80,128]{2,1,0:T(8,128)S(1)}, f32[22,80,128]{2,1,0:T(8,128)S(1)}, f3...) custom-call(s32[1024]{0:T(1024)S(1)} %bitcast.15, ...), custom_call_target="tpu_custom_call", output_to_operand_aliasing={{0}: (3, {}), {1}: (4, {}), {2}: (5, {}), {3}: (6, {}), {4}... | custom-call | tf_op jit(solution)/shard_map/pallas_call | solution.py:29
  16.5 0.9 collective-permute-done.2.sl
  17.5 1.4 %collective-permute-done.3.sh = f32[20,8,128]{2,1,0:T(8,128)S(1)} collective-permute-done((f32[20,8,128]{2,1,0:T(8,128)S(1)}, f32[20,8,128]{2,1,0:T(8,128)S(1)}, u32[]{:S(2)}, u32[]{:S(2)}) %collective-permute-start.3) | collective-permute-done | bytes 81952 | tf_op jit(solution)/shard_map/ppermute | solution.py:386
  18.9 0.9 shard_map.78
  19.8 43.3 %all_to_all.10 = f32[64,41,1,128]{3,2,1,0:T(1,128)S(1)} all-to-all(f32[64,41,1,128]{3,2,1,0:T(1,128)S(1)} %bitcast.9), channel_id=1, replica_groups=mesh['bulk'=64,'slab'=4] {'bulk'}, dimensions={0} | all-to-all | bytes 2686976 | tf_op jit(solution)/shard_map/all_to_all | solution.py:441
  63.1 1.9 %shard_map.79 = f32[2624,128]{1,0:T(8,128)S(1)} custom-call(f32[2624,128]{1,0:T(8,128)S(1)} %bitcast.12, f32[128,128]{1,0:T(8,128)S(1)} %bitcast.19, f32[128,128]{1,0:T(8,128)S(1)} %bitcast.20), custom_call_target="tpu_custom_call" | custom-call | tf_op jit(solution)/shard_map/pallas_call | solution.py:29
  65.0 40.4 %all_to_all.11 = f32[64,41,1,128]{3,2,1,0:T(1,128)S(1)} all-to-all(f32[64,41,1,128]{3,2,1,0:T(1,128)S(1)} %bitcast.13), channel_id=1, replica_groups=mesh['bulk'=64,'slab'=4] {'bulk'}, dimensions={0} | all-to-all | bytes 2686976 | tf_op jit(solution)/shard_map/all_to_all | solution.py:448
  105.4 0.8 shard_map.80
  106.3 1.3 %shard_map.81.vd_in = f32[22,80,128]{2,1,0:T(8,128)S(1)} custom-call(s32[1024]{0:T(1024)S(1)} %bitcast.18, f32[2624,128]{1,0:T(8,128)S(1)} %bitcast.11, f32[22,80,128]{2,1,0:T(8,128)S(1)} %get-tuple-element.77.vc, f32[2,64,128]{2,1,0:T(8,128)S(1)} %get-tuple-element.78.to_high, f32[2,64,128]{2,1,0:T(8,128)S(1)} %get-tuple-element.79.to_low), custom_call_target="tpu_custom_call" | custom-call | tf_op jit(solution)/shard_map/pallas_call | solution.py:29
  107.5 5.1 %collective-permute-start.5 = (f32[2,64,128]{2,1,0:T(8,128)S(1)}, f32[2,64,128]{2,1,0:T(8,128)S(1)}, u32[]{:S(2)}, u32[]{:S(2)}) collective-permute-start(f32[2,64,128]{2,1,0:T(8,128)S(1)} %get-tuple-element.79.to_low), channel_id=1, source_target_pairs={{0,252},{4,0},{8,4},{12,8},{16,12},{20,16},{24,20},{28,24},{32,28}... | collective-permute-start | bytes 196616 | tf_op jit(solution)/shard_map/ppermute | solution.py:386
  112.7 0.6 collective-permute-done.4.bl
  113.3 1.3 %collective-permute-done.5.bh = f32[2,64,128]{2,1,0:T(8,128)S(1)} collective-permute-done((f32[2,64,128]{2,1,0:T(8,128)S(1)}, f32[2,64,128]{2,1,0:T(8,128)S(1)}, u32[]{:S(2)}, u32[]{:S(2)}) %collective-permute-start.5) | collective-permute-done | bytes 65568 | tf_op jit(solution)/shard_map/ppermute | solution.py:386
  114.6 0.5 collective-permute-start.7
  115.1 2.9 %collective-permute-start.6 = (f32[18,2,128]{2,1,0:T(2,128)S(1)}, f32[18,2,128]{2,1,0:T(2,128)S(1)}, u32[]{:S(2)}, u32[]{:S(2)}) collective-permute-start(f32[18,2,128]{2,1,0:T(2,128)S(1)} %pad_maximum_fusion), channel_id=1, source_target_pairs={{0,1},{1,2},{2,3},{3,0},{4,5},{5,6},{6,7},{7,4},{8,9},{9,10},{10,1... | collective-permute-start | bytes 55304 | tf_op jit(solution)/shard_map/ppermute | solution.py:385
  118.0 1.1 shard_map.82
  119.1 0.5 collective-permute-done.7.sh
  119.6 1.2 shard_map.83
  (24 shorter events, 0.4 us)
Async XLA Ops:
  0.0 10.4 %copy-start = (f32[16,64,128]{2,1,0:T(8,128)S(1)}, f32[16,64,128]{2,1,0:T(8,128)}, u32[]{:S(2)}) copy-start(f32[16,64,128]{2,1,0:T(8,128)} %p_ref.5) | copy-start | bytes 1572868
  0.0 10.4 %copy-start.2 = (f32[16,64,128]{2,1,0:T(8,128)S(1)}, f32[16,64,128]{2,1,0:T(8,128)}, u32[]{:S(2)}) copy-start(f32[16,64,128]{2,1,0:T(8,128)} %r_ref.5) | copy-start | bytes 1572868
  0.0 10.4 %copy-start.1 = (f32[16,64,128]{2,1,0:T(8,128)S(1)}, f32[16,64,128]{2,1,0:T(8,128)}, u32[]{:S(2)}) copy-start(f32[16,64,128]{2,1,0:T(8,128)} %k_ref.5) | copy-start | bytes 1572868
  0.0 8.9 %copy-start.5 = (s32[1,1,1024,1]{2,3,1,0:T(1,128)S(1)}, s32[1,1,1024,1]{2,3,1,0:T(1,128)}, u32[]{:S(2)}) copy-start(s32[1,1,1024,1]{2,3,1,0:T(1,128)} %param.10) | copy-start | bytes 12292
  1.3 11.6 %collective-permute-start = (f32[8,64,128]{2,1,0:T(8,128)S(1)}, f32[8,64,128]{2,1,0:T(8,128)S(1)}, u32[]{:S(2)}, u32[]{:S(2)}) collective-permute-start(f32[8,64,128]{2,1,0:T(8,128)S(1)} %get-tuple-element.48), channel_id=1, source_target_pairs={{0,4},{4,8},{8,12},{12,16},{16,20},{20,24},{24,28},{28,32},{32,36}... | collective-permute-start | bytes 786440 | tf_op jit(solution)/shard_map/ppermute | solution.py:385
  1.4 11.5 %collective-permute-start.1 = (f32[8,64,128]{2,1,0:T(8,128)S(1)}, f32[8,64,128]{2,1,0:T(8,128)S(1)}, u32[]{:S(2)}, u32[]{:S(2)}) collective-permute-start(f32[8,64,128]{2,1,0:T(8,128)S(1)} %get-tuple-element.49), channel_id=1, source_target_pairs={{0,252},{4,0},{8,4},{12,8},{16,12},{20,16},{24,20},{28,24},{32,28}... | collective-permute-start | bytes 786440 | tf_op jit(solution)/shard_map/ppermute | solution.py:386
  8.9 0.7 copy-start.6
  12.9 4.5 %collective-permute-start.2 = (f32[20,8,128]{2,1,0:T(8,128)S(1)}, f32[20,8,128]{2,1,0:T(8,128)S(1)}, u32[]{:S(2)}, u32[]{:S(2)}) collective-permute-start(f32[20,8,128]{2,1,0:T(8,128)S(1)} %get-tuple-element.52), channel_id=1, source_target_pairs={{0,1},{1,2},{2,3},{3,0},{4,5},{5,6},{6,7},{7,4},{8,9},{9,10},{10,1... | collective-permute-start | bytes 245768 | tf_op jit(solution)/shard_map/ppermute | solution.py:385
  13.2 5.7 %collective-permute-start.3 = (f32[20,8,128]{2,1,0:T(8,128)S(1)}, f32[20,8,128]{2,1,0:T(8,128)S(1)}, u32[]{:S(2)}, u32[]{:S(2)}) collective-permute-start(f32[20,8,128]{2,1,0:T(8,128)S(1)} %get-tuple-element.53), channel_id=1, source_target_pairs={{0,3},{1,0},{2,1},{3,2},{4,7},{5,4},{6,5},{7,6},{8,11},{9,8},{10,9... | collective-permute-start | bytes 245768 | tf_op jit(solution)/shard_map/ppermute | solution.py:386
  19.8 43.3 %copy-start.3 = (f32[1,128,128]{2,1,0:T(8,128)S(1)}, f32[1,128,128]{2,1,0:T(8,128)}, u32[]{:S(2)}) copy-start(f32[1,128,128]{2,1,0:T(8,128)} %param.12) | copy-start | bytes 196612
  19.8 43.3 %copy-start.4 = (f32[1,128,128]{2,1,0:T(8,128)S(1)}, f32[1,128,128]{2,1,0:T(8,128)}, u32[]{:S(2)}) copy-start(f32[1,128,128]{2,1,0:T(8,128)} %param.13) | copy-start | bytes 196612
  106.2 7.1 %collective-permute-start.4 = (f32[2,64,128]{2,1,0:T(8,128)S(1)}, f32[2,64,128]{2,1,0:T(8,128)S(1)}, u32[]{:S(2)}, u32[]{:S(2)}) collective-permute-start(f32[2,64,128]{2,1,0:T(8,128)S(1)} %get-tuple-element.78.to_high), channel_id=1, source_target_pairs={{0,4},{4,8},{8,12},{12,16},{16,20},{20,24},{24,28},{28,32},{32,36}... | collective-permute-start | bytes 196616 | tf_op jit(solution)/shard_map/ppermute | solution.py:385
  107.5 7.0 %collective-permute-start.5 = (f32[2,64,128]{2,1,0:T(8,128)S(1)}, f32[2,64,128]{2,1,0:T(8,128)S(1)}, u32[]{:S(2)}, u32[]{:S(2)}) collective-permute-start(f32[2,64,128]{2,1,0:T(8,128)S(1)} %get-tuple-element.79.to_low), channel_id=1, source_target_pairs={{0,252},{4,0},{8,4},{12,8},{16,12},{20,16},{24,20},{28,24},{32,28}... | collective-permute-start | bytes 196616 | tf_op jit(solution)/shard_map/ppermute | solution.py:386
  114.6 5.0 %collective-permute-start.7 = (f32[18,2,128]{2,1,0:T(2,128)S(1)}, f32[18,2,128]{2,1,0:T(2,128)S(1)}, u32[]{:S(2)}, u32[]{:S(2)}) collective-permute-start(f32[18,2,128]{2,1,0:T(2,128)S(1)} %pad_maximum_fusion.1), channel_id=1, source_target_pairs={{0,3},{1,0},{2,1},{3,2},{4,7},{5,4},{6,5},{7,6},{8,11},{9,8},{10,9... | collective-permute-start | bytes 55304 | tf_op jit(solution)/shard_map/ppermute | solution.py:386
  115.1 4.5 %collective-permute-start.6 = (f32[18,2,128]{2,1,0:T(2,128)S(1)}, f32[18,2,128]{2,1,0:T(2,128)S(1)}, u32[]{:S(2)}, u32[]{:S(2)}) collective-permute-start(f32[18,2,128]{2,1,0:T(2,128)S(1)} %pad_maximum_fusion), channel_id=1, source_target_pairs={{0,1},{1,2},{2,3},{3,0},{4,5},{5,6},{6,7},{7,4},{8,9},{9,10},{10,1... | collective-permute-start | bytes 55304 | tf_op jit(solution)/shard_map/ppermute | solution.py:385

commit v5 on v4

--- a/solution.py
+++ b/solution.py
@@ -78,12 +78,18 @@
     return xl if e < W else (None if e < W + CX else xh)
 
 
-def send_kernel(p_ref, k_ref, r_ref, to_high, to_low, sems):
+def is_odd():
+    return lax.rem(lax.axis_index("bulk"), 2) == 1
+
+
+def send_kernel(p_ref, k_ref, r_ref, to_o, to_e, sems):
+    odd = is_odd()
     copies = []
     at = 0
     for ref, n in ((p_ref, W), (k_ref, W), (r_ref, W - 1)):
-        for src, dst in ((ref.at[pl.ds(CX - n, n)], to_high.at[pl.ds(at, n)]), (ref.at[pl.ds(0, n)], to_low.at[pl.ds(at, n)])):
-            copies.append(pltpu.make_async_copy(src, dst, sems.at[len(copies)]))
+        for dst, high in ((to_o, odd), (to_e, jnp.logical_not(odd))):
+            src = ref.at[pl.ds(jnp.where(high, CX - n, 0), n)]
+            copies.append(pltpu.make_async_copy(src, dst.at[pl.ds(at, n)], sems.at[len(copies)]))
         at += n
     for copy in copies:
         copy.start()
@@ -91,25 +97,24 @@
         copy.wait()
 
 
-def halo_plane(refs, a, e):
-    own, bl, bh = refs[a], refs[3], refs[4]
+def halo_plane(refs, a, e, rows):
+    own, from_o, from_e, odd = refs[a], refs[3], refs[4], refs[5]
     if W <= e < W + CX:
-        return own, e - W
-    at = W * a
-    if e < W:
-        return bl, at + e - (1 if a == 2 else 0)
-    return bh, at + e - W - CX
-
-
-def side_kernel(p_ref, k_ref, r_ref, bl, bh, done, to_high, to_low):
+        return own[e - W, rows, :]
+    low = e < W
+    i = W * a + (e - (1 if a == 2 else 0) if low else e - W - CX)
+    of_o, of_e = from_o[i, rows, :], from_e[i, rows, :]
+    return jnp.where(odd, of_e, of_o) if low else jnp.where(odd, of_o, of_e)
+
+
+def side_kernel(p_ref, k_ref, r_ref, from_o, from_e, done, to_high, to_low):
     del done
-    refs = (p_ref, k_ref, r_ref, bl, bh)
+    refs = (p_ref, k_ref, r_ref, from_o, from_e, is_odd())
     for e in range(1, EX - 1):
         at = 0
         for a, n in ((0, W), (1, W), (2, W - 1)):
-            ref, i = halo_plane(refs, a, e)
-            to_high[e - 1, at : at + n, :] = ref[i, CY - n : CY, :]
-            to_low[e - 1, at : at + n, :] = ref[i, 0:n, :]
+            to_high[e - 1, at : at + n, :] = halo_plane(refs, a, e, slice(CY - n, CY))
+            to_low[e - 1, at : at + n, :] = halo_plane(refs, a, e, slice(0, n))
             at += n
 
 
@@ -160,8 +165,7 @@
         for e in some:
             if a == 2 and e in (0, EX - 1):
                 continue
-            ref, i = halo_plane(refs, a, e)
-            values = keep(plane_ok(e, xl, xh), ref[i])
+            values = keep(plane_ok(e, xl, xh), halo_plane(refs, a, e, slice(0, CY)))
             dst[e, TOP : TOP + CY, :] = values * 2.0 if a == 2 else values
 
 
@@ -192,18 +196,18 @@
 
 def core_kernel(slot, p_ref, k_ref, r_ref, buf_in, buf, kx, rx, va, vb, vc, wx, wy, wz, q, res, done):
     del buf_in
-    fill((p_ref, k_ref, r_ref, None, None), (va, kx, rx), range(W, W + CX), None, None)
+    fill((p_ref, k_ref, r_ref, None, None, None), (va, kx, rx), range(W, W + CX), None, None)
     a, b = W + 1, W + CX - 1
     ranges = (((a, b),), ((a + 1, b - 1),), ((a + 2, b - 2),))
     inner_steps(ranges, slot, buf, kx, rx, va, vb, vc, wx, wy, wz, q, res, True, True)
     done[...] = jnp.zeros_like(done)
 
 
-def mid_kernel(slot, bl, bh, *refs):
+def mid_kernel(slot, from_o, from_e, *refs):
     buf, kx, rx, va, vb, vc, wx, wy, wz, q, res = refs[11:]
     xl, xh, _, _ = edges()
     halo = [*range(W), *range(W + CX, EX)]
-    fill((None, None, None, bl, bh), (va, kx, rx), halo, xl, xh)
+    fill((None, None, None, from_o, from_e, is_odd()), (va, kx, rx), halo, xl, xh)
     a, b = W + 1, W + CX - 1
     ranges = tuple(((1 + i, a + i), (b - i, EX - 1 - i)) for i in range(3))
     inner_steps(ranges, slot, buf, kx, rx, va, vb, vc, wx, wy, wz, q, res, xl, xh)
@@ -314,16 +318,27 @@
 EDGE = (0, 1, CX - 2, CX - 1)
 
 
-def edge_kernel(slot, back, vc, to_high, to_low):
+def edge_kernel(slot, back, vc, to_o, to_e):
+    def fill_planes(low, high):
+        for i, x in enumerate(EDGE):
+            dst = low if i < 2 else high
+            for y in range(CY):
+                dst[i % 2, y : y + 1, :] = back[pl.ds(slot[x * CY + y], 1), :] + vc[x + W, TOP + y : TOP + y + 1, :]
+
+    @pl.when(is_odd())
+    def _():
+        fill_planes(to_e, to_o)
+
+    @pl.when(jnp.logical_not(is_odd()))
+    def _():
+        fill_planes(to_o, to_e)
+
+
+def body_kernel(slot, back, vc, to_o, to_e, vd):
+    odd = is_odd()
     for i, x in enumerate(EDGE):
-        dst = to_low if i < 2 else to_high
-        for y in range(CY):
-            dst[i % 2, y : y + 1, :] = back[pl.ds(slot[x * CY + y], 1), :] + vc[x + W, TOP + y : TOP + y + 1, :]
-
-
-def body_kernel(slot, back, vc, to_high, to_low, vd):
-    for i, x in enumerate(EDGE):
-        vd[x + W, TOP : TOP + CY, :] = (to_low if i < 2 else to_high)[i % 2]
+        of_o, of_e = to_o[i % 2], to_e[i % 2]
+        vd[x + W, TOP : TOP + CY, :] = jnp.where(odd, of_e, of_o) if i < 2 else jnp.where(odd, of_o, of_e)
 
     def plane(x, carry):
         for y in range(CY):
@@ -334,14 +349,25 @@
     lax.fori_loop(2, CX - 2, plane, 0)
 
 
-def last_inner_kernel(vd_in, bl, bh, rx, wx, wy, wz, q, vd, ve, out):
+def last_side_kernel(vd, from_o, from_e, to_high, to_low):
+    odd = is_odd()
+    for dst, rows in ((to_high, slice(CY - 2, CY)), (to_low, slice(0, 2))):
+        dst[0] = jnp.where(odd, from_e[1, rows, :], from_o[1, rows, :])
+        dst[CX + 1] = jnp.where(odd, from_o[0, rows, :], from_e[0, rows, :])
+        for x in range(CX):
+            dst[x + 1] = vd[x + W, TOP + rows.start : TOP + rows.stop, :]
+
+
+def last_inner_kernel(vd_in, from_o, from_e, rx, wx, wy, wz, q, vd, ve, out):
     del vd_in
     xl, xh, _, _ = edges()
     off = zero_index()
     own = pl.ds(TOP, CY)
+    odd = is_odd()
     for e in (1, 2):
-        vd[e, own, :] = keep(xl, bl[e - 1])
-        vd[e + CX + 2, own, :] = keep(xh, bh[e - 1])
+        of_o, of_e = from_o[e - 1], from_e[e - 1]
+        vd[e, own, :] = jnp.where(xl, jnp.where(odd, of_e, of_o), 0.0)
+        vd[e + CX + 2, own, :] = jnp.where(xh, jnp.where(odd, of_o, of_e), 0.0)
 
     field = (rx, wx, wy, wz, q, TOP, CY, off)
 
@@ -381,6 +407,15 @@
     return [(i, (i + step) % n) for i in range(n)]
 
 
+def swap_both(to_o, to_e):
+    n = lax.axis_size("bulk")
+    got = []
+    for first, values in ((1, to_o), (0, to_e)):
+        pairs = [(i, (i + 1) % n) for i in range(first, n, 2)]
+        got.append(lax.ppermute(values, "bulk", pairs + [(j, i) for i, j in pairs]))
+    return got
+
+
 def from_both(axis, to_high, to_low):
     low = lax.ppermute(to_high, axis, ring(axis, 1))
     high = lax.ppermute(to_low, axis, ring(axis, -1))
@@ -395,7 +430,7 @@
     slots = owners * BLOCK
     sent = ((2 * W + W - 1, CY, NZ), F32)
     side = ((EX - 2, 8, NZ), F32)
-    to_high, to_low = call(
+    to_o, to_e = call(
         send_kernel,
         [sent, sent],
         [pltpu.with_memory_space_constraint(f, pltpu.MemorySpace.HBM) for f in (pressure, kappa, rhs)],
@@ -403,7 +438,7 @@
         scratch=[pltpu.SemaphoreType.DMA((6,))],
         mib=2,
     )
-    bl, bh = from_both("bulk", to_high, to_low)
+    from_o, from_e = swap_both(to_o, to_e)
     slot, buf = call(
         lambda *refs: slot_kernel(owners, *refs),
         [((8, 128), I32), ((slots, NZ), F32)],
@@ -419,12 +454,12 @@
         aliases={4: 0},
         mib=20,
     )
-    to_high, to_low = call(side_kernel, [side, side], (pressure, kappa, rhs, bl, bh, done))
+    to_high, to_low = call(side_kernel, [side, side], (pressure, kappa, rhs, from_o, from_e, done))
     sl, sh = from_both("slab", to_high, to_low)
     buf, *ext, res = call(
         mid_kernel,
         work,
-        (table, bl, bh, *core),
+        (table, from_o, from_e, *core),
         in_specs=[SMEM] + [VMEM] * 13,
         aliases={3 + i: i for i in range(11)},
         mib=20,
@@ -446,20 +481,19 @@
         scratch=[pltpu.VMEM((-(-owners // 6), CR, 256), BF16), pltpu.VMEM((-(-owners // 6), 256, 3 * NZ), BF16)],
     )
     back = lax.all_to_all(back.reshape(owners, BLOCK, 1, NZ), "bulk", 0, 0).reshape(slots, NZ)
-    to_high, to_low = call(
+    to_o, to_e = call(
         edge_kernel, [((2, CY, NZ), F32)] * 2, (table, back, vc), in_specs=[SMEM, VMEM, VMEM]
     )
-    bl, bh = from_both("bulk", to_high, to_low)
-    (vd,) = call(body_kernel, [EXT], (table, back, vc, to_high, to_low), in_specs=[SMEM] + [VMEM] * 4)
-
-    def rim(lo, hi):
-        return jnp.concatenate([bl[1:, lo:hi], vd[W : W + CX, TOP + lo : TOP + hi], bh[:1, lo:hi]], axis=0)
-
-    sl, sh = from_both("slab", rim(CY - 2, CY), rim(0, 2))
+    from_o, from_e = swap_both(to_o, to_e)
+    (vd,) = call(body_kernel, [EXT], (table, back, vc, to_o, to_e), in_specs=[SMEM] + [VMEM] * 4)
+
+    last_side = ((CX + 2, 2, NZ), F32)
+    to_high, to_low = call(last_side_kernel, [last_side, last_side], (vd, from_o, from_e))
+    sl, sh = from_both("slab", to_high, to_low)
     vd, ve, inner = call(
         last_inner_kernel,
         [EXT, EXT, ((CX, CY, NZ), F32)],
-        (vd, bl, bh, rx, wx, wy, wz, q),
+        (vd, from_o, from_e, rx, wx, wy, wz, q),
         aliases={0: 0},
         mib=20,
     )

time: 122 us -> 119 us (0.975)
  starting transfers between devices: 18.4 us -> 13.5 us
  waiting for transfers between devices: 4.88 us -> 8.95 us
    ppermute x4 -> x2, starting transfers between devices: 15 us -> 3.46 us  [from_both(): high = lax.ppermute(to_low, axis, ring(axis, -1))]
    ppermute x0 -> x4, starting transfers between devices: none -> 9.26 us  [swap_both(): got.append(lax.ppermute(values, 'bulk', pairs + [(j, i) for i, j in pairs]))]
    ppermute x0 -> x4, waiting for transfers between devices: none -> 4.31 us  [swap_both(): got.append(lax.ppermute(values, 'bulk', pairs + [(j, i) for i, j in pairs]))]
    ppermute x4 -> x2, starting transfers between devices: 3.33 us -> 0.75 us  [from_both(): low = lax.ppermute(to_high, axis, ring(axis, 1))]
    all_to_all x1, blocking collectives: 43.3 us -> 42 us  [cycle(): got = lax.all_to_all(buf.reshape(owners, BLOCK, 1, NZ), 'bulk', 0, 0)]
    ppermute x4 -> x2, waiting for transfers between devices: 3.29 us -> 2.88 us  [from_both(): high = lax.ppermute(to_low, axis, ring(axis, -1))]
    pallas_call x11 -> x12, Pallas kernels: 13 us -> 13.1 us  [call(): pl.pallas_call(kernel, out_shape=[jax.ShapeDtypeStruct(s, d) for s, d in...]
where the time goes in v5:
time: 119 us
  blocking collectives  82.5 us (69%)
  starting transfers between devices  13.5 us (11%)
  Pallas kernels  13.1 us (11%)
  waiting for transfers between devices  8.95 us (8%)
    all_to_all x1, blocking collectives, cycle(): got = lax.all_to_all(buf.reshape(owners, BLOCK, 1, NZ), 'bulk', 0, 0)  42 us
    all_to_all x1, blocking collectives, cycle(): lax.all_to_all(back.reshape(owners, BLOCK, 1, NZ), 'bulk', 0, 0)  40.4 us
    pallas_call x12, Pallas kernels, call(): pl.pallas_call(kernel, out_shape=[jax.ShapeDtypeStruct(s, d) for s, d in...  13.1 us
    ppermute x4, starting transfers between devices, swap_both(): got.append(lax.ppermute(values, 'bulk', pairs + [(j, i) for i, j in pairs]))  9.26 us
    ppermute x4, waiting for transfers between devices, swap_both(): got.append(lax.ppermute(values, 'bulk', pairs + [(j, i) for i, j in pairs]))  4.31 us
    ppermute x2, starting transfers between devices, from_both(): high = lax.ppermute(to_low, axis, ring(axis, -1))  3.46 us
    ppermute x2, waiting for transfers between devices, from_both(): high = lax.ppermute(to_low, axis, ring(axis, -1))  2.88 us
  transfers between devices with their start and end apart: 8, of which 6 were waited for; matrix products, arithmetic and copies ran while one was open for 0% of the time, Pallas kernels for 6%

profile of v5, /device:TPU:24, one launch (start us, length us, event | category | flops | bytes accessed | tf_op | source)
XLA Modules:
  0.0 118.8 jit_solution(2508174309184520743)
XLA Ops:
  0.0 1.2 %shard_map.74 = (f32[8,64,128]{2,1,0:T(8,128)S(1)}, f32[8,64,128]{2,1,0:T(8,128)S(1)}) custom-call(f32[16,64,128]{2,1,0:T(8,128)} %p_ref.5, f32[16,64,128]{2,1,0:T(8,128)} %k_ref.5, f32[16,64,128]{2,1,0:T(8,128)} %r_ref.5), custom_call_target="tpu_custom_call" | custom-call | tf_op jit(solution)/shard_map/pallas_call | solution.py:29
  1.3 7.6 %collective-permute-start = (f32[8,64,128]{2,1,0:T(8,128)S(1)}, f32[8,64,128]{2,1,0:T(8,128)S(1)}, u32[]{:S(2)}, u32[]{:S(2)}) collective-permute-start(f32[8,64,128]{2,1,0:T(8,128)S(1)} %get-tuple-element.50), channel_id=1, source_target_pairs={{4,8},{12,16},{20,24},{28,32},{36,40},{44,48},{52,56},{60,64},{68,... | collective-permute-start | bytes 786440 | tf_op jit(solution)/shard_map/ppermute | solution.py:415
  8.9 0.7 copy-done.6
  9.5 0.8 shard_map.73
  10.3 2.4 %shard_map.75 = (f32[2624,128]{1,0:T(8,128)S(1)}, f32[22,80,128]{2,1,0:T(8,128)S(1)}, f32[22,80,128]{2,1,0:T(8,128)S(1)}, f32[22,80,128]{2,1,0:T(8,128)S(1)}, f3...) custom-call(s32[1024]{0:T(1024)S(1)} %bitcast.14, ...), custom_call_target="tpu_custom_call", output_to_operand_aliasing={{0}: (4, {})} | custom-call | tf_op jit(solution)/shard_map/pallas_call | solution.py:29
  13.3 1.8 %collective-permute-start.3 = (f32[20,8,128]{2,1,0:T(8,128)S(1)}, f32[20,8,128]{2,1,0:T(8,128)S(1)}, u32[]{:S(2)}, u32[]{:S(2)}) collective-permute-start(f32[20,8,128]{2,1,0:T(8,128)S(1)} %get-tuple-element.55), channel_id=1, source_target_pairs={{0,3},{1,0},{2,1},{3,2},{4,7},{5,4},{6,5},{7,6},{8,11},{9,8},{10,9... | collective-permute-start | bytes 245768 | tf_op jit(solution)/shard_map/ppermute | solution.py:421
  15.1 1.5 %shard_map.77 = (f32[2624,128]{1,0:T(8,128)S(1)}, f32[22,80,128]{2,1,0:T(8,128)S(1)}, f32[22,80,128]{2,1,0:T(8,128)S(1)}, f32[22,80,128]{2,1,0:T(8,128)S(1)}, f3...) custom-call(s32[1024]{0:T(1024)S(1)} %bitcast.15, ...), custom_call_target="tpu_custom_call", output_to_operand_aliasing={{0}: (3, {}), {1}: (4, {}), {2}: (5, {}), {3}: (6, {}), {4}... | custom-call | tf_op jit(solution)/shard_map/pallas_call | solution.py:29
  16.6 1.1 collective-permute-done.2.sl
  17.7 1.3 %collective-permute-done.3.sh = f32[20,8,128]{2,1,0:T(8,128)S(1)} collective-permute-done((f32[20,8,128]{2,1,0:T(8,128)S(1)}, f32[20,8,128]{2,1,0:T(8,128)S(1)}, u32[]{:S(2)}, u32[]{:S(2)}) %collective-permute-start.3) | collective-permute-done | bytes 81952 | tf_op jit(solution)/shard_map/ppermute | solution.py:421
  19.0 0.9 shard_map.78
  19.9 42.0 %all_to_all.10 = f32[64,41,1,128]{3,2,1,0:T(1,128)S(1)} all-to-all(f32[64,41,1,128]{3,2,1,0:T(1,128)S(1)} %bitcast.9), channel_id=1, replica_groups=mesh['bulk'=64,'slab'=4] {'bulk'}, dimensions={0} | all-to-all | bytes 2686976 | tf_op jit(solution)/shard_map/all_to_all | solution.py:476
  62.0 1.9 %shard_map.79 = f32[2624,128]{1,0:T(8,128)S(1)} custom-call(f32[2624,128]{1,0:T(8,128)S(1)} %bitcast.12, f32[128,128]{1,0:T(8,128)S(1)} %bitcast.19, f32[128,128]{1,0:T(8,128)S(1)} %bitcast.20), custom_call_target="tpu_custom_call" | custom-call | tf_op jit(solution)/shard_map/pallas_call | solution.py:29
  63.9 40.4 %all_to_all.11 = f32[64,41,1,128]{3,2,1,0:T(1,128)S(1)} all-to-all(f32[64,41,1,128]{3,2,1,0:T(1,128)S(1)} %bitcast.13), channel_id=1, replica_groups=mesh['bulk'=64,'slab'=4] {'bulk'}, dimensions={0} | all-to-all | bytes 2686976 | tf_op jit(solution)/shard_map/all_to_all | solution.py:483
  104.3 0.8 shard_map.80
  105.1 0.6 collective-permute-start.4
  105.7 1.1 collective-permute-start.5
  106.8 1.3 %shard_map.81.vd.vd_in = f32[22,80,128]{2,1,0:T(8,128)S(1)} custom-call(s32[1024]{0:T(1024)S(1)} %bitcast.18, f32[2624,128]{1,0:T(8,128)S(1)} %bitcast.11, f32[22,80,128]{2,1,0:T(8,128)S(1)} %get-tuple-element.79.vc, f32[2,64,128]{2,1,0:T(8,128)S(1)} %get-tuple-element.80.to_o, f32[2,64,128]{2,1,0:T(8,128)S(1)} %get-tuple-element.81.to_e), custom_call_target="tpu_custom_call" | custom-call | tf_op jit(solution)/shard_map/pallas_call | solution.py:29
  108.1 4.1 %collective-permute-done.4.from_o = f32[2,64,128]{2,1,0:T(8,128)S(1)} collective-permute-done((f32[2,64,128]{2,1,0:T(8,128)S(1)}, f32[2,64,128]{2,1,0:T(8,128)S(1)}, u32[]{:S(2)}, u32[]{:S(2)}) %collective-permute-start.4) | collective-permute-done | bytes 65568 | tf_op jit(solution)/shard_map/ppermute | solution.py:415
  112.2 0.4 collective-permute-start.6
  112.7 1.7 %collective-permute-start.7 = (f32[18,2,128]{2,1,0:T(2,128)S(1)}, f32[18,2,128]{2,1,0:T(2,128)S(1)}, u32[]{:S(2)}, u32[]{:S(2)}) collective-permute-start(f32[18,2,128]{2,1,0:T(2,128)S(1)} %get-tuple-element.83), channel_id=1, source_target_pairs={{0,3},{1,0},{2,1},{3,2},{4,7},{5,4},{6,5},{7,6},{8,11},{9,8},{10,9... | collective-permute-start | bytes 55304 | tf_op jit(solution)/shard_map/ppermute | solution.py:421
  114.3 1.1 shard_map.83
  115.4 0.6 collective-permute-done.6.sl
  116.1 1.6 %collective-permute-done.7.sh = f32[18,2,128]{2,1,0:T(2,128)S(1)} collective-permute-done((f32[18,2,128]{2,1,0:T(2,128)S(1)}, f32[18,2,128]{2,1,0:T(2,128)S(1)}, u32[]{:S(2)}, u32[]{:S(2)}) %collective-permute-start.7) | collective-permute-done | bytes 18464 | tf_op jit(solution)/shard_map/ppermute | solution.py:421
  117.6 1.2 shard_map.84
  (20 shorter events, 0.6 us)
Async XLA Ops:
  0.0 10.3 %copy-start = (f32[16,64,128]{2,1,0:T(8,128)S(1)}, f32[16,64,128]{2,1,0:T(8,128)}, u32[]{:S(2)}) copy-start(f32[16,64,128]{2,1,0:T(8,128)} %p_ref.5) | copy-start | bytes 1572868
  0.0 10.3 %copy-start.2 = (f32[16,64,128]{2,1,0:T(8,128)S(1)}, f32[16,64,128]{2,1,0:T(8,128)}, u32[]{:S(2)}) copy-start(f32[16,64,128]{2,1,0:T(8,128)} %r_ref.5) | copy-start | bytes 1572868
  0.0 10.3 %copy-start.1 = (f32[16,64,128]{2,1,0:T(8,128)S(1)}, f32[16,64,128]{2,1,0:T(8,128)}, u32[]{:S(2)}) copy-start(f32[16,64,128]{2,1,0:T(8,128)} %k_ref.5) | copy-start | bytes 1572868
  0.0 8.8 %copy-start.5 = (s32[1,1,1024,1]{2,3,1,0:T(1,128)S(1)}, s32[1,1,1024,1]{2,3,1,0:T(1,128)}, u32[]{:S(2)}) copy-start(s32[1,1,1024,1]{2,3,1,0:T(1,128)} %param.10) | copy-start | bytes 12292
  1.3 11.6 %collective-permute-start = (f32[8,64,128]{2,1,0:T(8,128)S(1)}, f32[8,64,128]{2,1,0:T(8,128)S(1)}, u32[]{:S(2)}, u32[]{:S(2)}) collective-permute-start(f32[8,64,128]{2,1,0:T(8,128)S(1)} %get-tuple-element.50), channel_id=1, source_target_pairs={{4,8},{12,16},{20,24},{28,32},{36,40},{44,48},{52,56},{60,64},{68,... | collective-permute-start | bytes 786440 | tf_op jit(solution)/shard_map/ppermute | solution.py:415
  8.8 4.1 %collective-permute-start.1 = (f32[8,64,128]{2,1,0:T(8,128)S(1)}, f32[8,64,128]{2,1,0:T(8,128)S(1)}, u32[]{:S(2)}, u32[]{:S(2)}) collective-permute-start(f32[8,64,128]{2,1,0:T(8,128)S(1)} %get-tuple-element.51), channel_id=1, source_target_pairs={{0,4},{8,12},{16,20},{24,28},{32,36},{40,44},{48,52},{56,60},{64,6... | collective-permute-start | bytes 786440 | tf_op jit(solution)/shard_map/ppermute | solution.py:415
  8.8 0.7 copy-start.6
  13.0 4.8 %collective-permute-start.2 = (f32[20,8,128]{2,1,0:T(8,128)S(1)}, f32[20,8,128]{2,1,0:T(8,128)S(1)}, u32[]{:S(2)}, u32[]{:S(2)}) collective-permute-start(f32[20,8,128]{2,1,0:T(8,128)S(1)} %get-tuple-element.54), channel_id=1, source_target_pairs={{0,1},{1,2},{2,3},{3,0},{4,5},{5,6},{6,7},{7,4},{8,9},{9,10},{10,1... | collective-permute-start | bytes 245768 | tf_op jit(solution)/shard_map/ppermute | solution.py:420
  13.3 5.8 %collective-permute-start.3 = (f32[20,8,128]{2,1,0:T(8,128)S(1)}, f32[20,8,128]{2,1,0:T(8,128)S(1)}, u32[]{:S(2)}, u32[]{:S(2)}) collective-permute-start(f32[20,8,128]{2,1,0:T(8,128)S(1)} %get-tuple-element.55), channel_id=1, source_target_pairs={{0,3},{1,0},{2,1},{3,2},{4,7},{5,4},{6,5},{7,6},{8,11},{9,8},{10,9... | collective-permute-start | bytes 245768 | tf_op jit(solution)/shard_map/ppermute | solution.py:421
  19.9 42.1 %copy-start.3 = (f32[1,128,128]{2,1,0:T(8,128)S(1)}, f32[1,128,128]{2,1,0:T(8,128)}, u32[]{:S(2)}) copy-start(f32[1,128,128]{2,1,0:T(8,128)} %param.12) | copy-start | bytes 196612
  19.9 42.1 %copy-start.4 = (f32[1,128,128]{2,1,0:T(8,128)S(1)}, f32[1,128,128]{2,1,0:T(8,128)}, u32[]{:S(2)}) copy-start(f32[1,128,128]{2,1,0:T(8,128)} %param.13) | copy-start | bytes 196612
  105.1 7.1 %collective-permute-start.4 = (f32[2,64,128]{2,1,0:T(8,128)S(1)}, f32[2,64,128]{2,1,0:T(8,128)S(1)}, u32[]{:S(2)}, u32[]{:S(2)}) collective-permute-start(f32[2,64,128]{2,1,0:T(8,128)S(1)} %get-tuple-element.80.to_o), channel_id=1, source_target_pairs={{4,8},{12,16},{20,24},{28,32},{36,40},{44,48},{52,56},{60,64},{68,... | collective-permute-start | bytes 196616 | tf_op jit(solution)/shard_map/ppermute | solution.py:415
  105.7 6.5 %collective-permute-start.5 = (f32[2,64,128]{2,1,0:T(8,128)S(1)}, f32[2,64,128]{2,1,0:T(8,128)S(1)}, u32[]{:S(2)}, u32[]{:S(2)}) collective-permute-start(f32[2,64,128]{2,1,0:T(8,128)S(1)} %get-tuple-element.81.to_e), channel_id=1, source_target_pairs={{0,4},{8,12},{16,20},{24,28},{32,36},{40,44},{48,52},{56,60},{64,6... | collective-permute-start | bytes 196616 | tf_op jit(solution)/shard_map/ppermute | solution.py:415
  112.2 3.8 %collective-permute-start.6 = (f32[18,2,128]{2,1,0:T(2,128)S(1)}, f32[18,2,128]{2,1,0:T(2,128)S(1)}, u32[]{:S(2)}, u32[]{:S(2)}) collective-permute-start(f32[18,2,128]{2,1,0:T(2,128)S(1)} %get-tuple-element.82), channel_id=1, source_target_pairs={{0,1},{1,2},{2,3},{3,0},{4,5},{5,6},{6,7},{7,4},{8,9},{9,10},{10,1... | collective-permute-start | bytes 55304 | tf_op jit(solution)/shard_map/ppermute | solution.py:420
  112.7 5.0 %collective-permute-start.7 = (f32[18,2,128]{2,1,0:T(2,128)S(1)}, f32[18,2,128]{2,1,0:T(2,128)S(1)}, u32[]{:S(2)}, u32[]{:S(2)}) collective-permute-start(f32[18,2,128]{2,1,0:T(2,128)S(1)} %get-tuple-element.83), channel_id=1, source_target_pairs={{0,3},{1,0},{2,1},{3,2},{4,7},{5,4},{6,5},{7,6},{8,11},{9,8},{10,9... | collective-permute-start | bytes 55304 | tf_op jit(solution)/shard_map/ppermute | solution.py:421

commit v6 on v5

--- a/solution.py
+++ b/solution.py
@@ -37,7 +37,7 @@
     )(*args)
 
 
-def slot_kernel(owners, own_ref, row_ref, slot_ref, buf_ref):
+def slot_kernel(owners, own_ref, row_ref, slot_ref, back_ref, buf_ref):
     shift = lax.rem(lax.axis_index("bulk"), 3) * BLOCK
     before = (iota((128, 128), 0) < iota((128, 128), 1)).astype(BF16)
     owner_of = iota((owners, 128), 0)
@@ -52,6 +52,7 @@
         rank = jnp.sum(jnp.where(mine, count, 0.0), axis=0, keepdims=True).astype(I32)
         seen = seen + jnp.sum(mine_f, axis=1, keepdims=True)
         slot_ref[b : b + 1, :] = own * BLOCK + rank
+        back_ref[b : b + 1, :] = own * CAP + rank
         named = jnp.where(lane_of == rank + shift, (row_ref[b : b + 1, :] + 1).astype(F32), 0.0)
         numbers = numbers + lax.dot_general(
             mine_f.astype(BF16), named.astype(BF16), (((1,), (1,)), ((), ())), preferred_element_type=F32
@@ -268,29 +269,30 @@
     return a, b, (rest - b.astype(F32)).astype(BF16)
 
 
-def coarse_kernel(owners, data, leak_ref, link_ref, back, hot, parts):
+def coarse_kernel(owners, data, leak_ref, link_ref, back, hot, hot_back, parts):
     rows = owners * BLOCK
     groups = -(-owners // 3)
     pairs = -(-groups // 2)
     number = (iota((CR, 128), 0) + 1).astype(F32)
     total = jnp.zeros((CR, 3 * NZ), F32)
-    bases = []
     for g in range(groups):
         base = g * TRIO
         names = [data[base + t * BLOCK + CAP : base + (t + 1) * BLOCK, :] for t in range(min(3, owners - 3 * g))]
-        name = names[0]
-        for more in names[1:]:
+        name = name_back = names[0]
+        for t, more in enumerate(names[1:], 1):
             name = name + more
+            name_back = name_back + pltpu.roll(jnp.broadcast_to(more, (8, 128)), 128 - t, 1)[0:1]
         if base + 128 > rows:
             name = pltpu.roll(jnp.broadcast_to(name, (8, 128)), base - (rows - 128), 1)[0:1]
             base = rows - 128
-        bases.append(base)
         at = g % 2 * 128
+        hot_back[g // 2, :, at : at + 128] = jnp.where(number == name_back, 1.0, 0.0).astype(BF16)
         hot[g // 2, :, at : at + 128] = jnp.where(number == name, 1.0, 0.0).astype(BF16)
         for i, part in enumerate(parts_of(data[base : base + 128, :])):
             parts[g // 2, at : at + 128, i * NZ : (i + 1) * NZ] = part
     if groups % 2:
         hot[pairs - 1, :, 128:] = jnp.zeros((CR, 128), BF16)
+        hot_back[pairs - 1, :, 128:] = jnp.zeros((CR, 128), BF16)
         parts[pairs - 1, 128:, :] = jnp.zeros((128, 3 * NZ), BF16)
     for p in range(pairs):
         total = total + jnp.dot(hot[p], parts[p], preferred_element_type=F32)
@@ -305,14 +307,14 @@
     for _ in range(2):
         u = (1.0 - DAMPING) * u + w * (total + inner * pltpu.roll(u, NZ - 1, 1) + pltpu.roll(inner * u, 1, 1))
     pieces = jnp.concatenate(parts_of(u), axis=1)
-    for p in range(pairs - 1, -1, -1):
-        out = lax.dot_general(hot[p], pieces, (((0,), (0,)), ((), ())), preferred_element_type=F32)
+    for p in range(pairs):
+        out = lax.dot_general(hot_back[p], pieces, (((0,), (0,)), ((), ())), preferred_element_type=F32)
         out = out[:, 0:NZ] + (out[:, NZ : 2 * NZ] + out[:, 2 * NZ :])
-        for g in (2 * p + 1, 2 * p):
+        for g in (2 * p, 2 * p + 1):
             if g < groups:
-                n = 128 if g == groups - 1 else TRIO
+                n = CAP * min(3, owners - 3 * g)
                 at = g % 2 * 128
-                back[bases[g] : bases[g] + n, :] = out[at : at + n]
+                back[3 * CAP * g : 3 * CAP * g + n, :] = out[at : at + n]
 
 
 EDGE = (0, 1, CX - 2, CX - 1)
@@ -411,8 +413,9 @@
     n = lax.axis_size("bulk")
     got = []
     for first, values in ((1, to_o), (0, to_e)):
-        pairs = [(i, (i + 1) % n) for i in range(first, n, 2)]
-        got.append(lax.ppermute(values, "bulk", pairs + [(j, i) for i, j in pairs]))
+        pairs = [(i, i + 1) for i in range(first, n - 1, 2)]
+        alone = [(i, i) for i in (0, n - 1)] if first else []
+        got.append(lax.ppermute(values, "bulk", pairs + [(j, i) for i, j in pairs] + alone))
     return got
 
 
@@ -439,12 +442,12 @@
         mib=2,
     )
     from_o, from_e = swap_both(to_o, to_e)
-    slot, buf = call(
+    slot, slot_back, buf = call(
         lambda *refs: slot_kernel(owners, *refs),
-        [((8, 128), I32), ((slots, NZ), F32)],
+        [((8, 128), I32), ((8, 128), I32), ((slots, NZ), F32)],
         (owner.reshape(8, 128), coarse_row.reshape(8, 128)),
     )
-    table = slot.reshape(CX * CY)
+    table, table_back = slot.reshape(CX * CY), slot_back.reshape(CX * CY)
     work = [((slots, NZ), F32)] + [EXT] * 9 + [((CX * CY, NZ), F32)]
     *core, done = call(
         core_kernel,
@@ -476,16 +479,16 @@
     got = lax.all_to_all(buf.reshape(owners, BLOCK, 1, NZ), "bulk", 0, 0)
     (back,) = call(
         lambda *refs: coarse_kernel(owners, *refs),
-        [((slots, NZ), F32)],
+        [((owners * CAP, NZ), F32)],
         (got.reshape(slots, NZ), coarse_leak[0], coarse_link[0]),
-        scratch=[pltpu.VMEM((-(-owners // 6), CR, 256), BF16), pltpu.VMEM((-(-owners // 6), 256, 3 * NZ), BF16)],
-    )
-    back = lax.all_to_all(back.reshape(owners, BLOCK, 1, NZ), "bulk", 0, 0).reshape(slots, NZ)
+        scratch=[pltpu.VMEM((-(-owners // 6), CR, 256), BF16), pltpu.VMEM((-(-owners // 6), CR, 256), BF16), pltpu.VMEM((-(-owners // 6), 256, 3 * NZ), BF16)],
+    )
+    back = lax.all_to_all(back.reshape(owners, CAP, 1, NZ), "bulk", 0, 0).reshape(owners * CAP, NZ)
     to_o, to_e = call(
-        edge_kernel, [((2, CY, NZ), F32)] * 2, (table, back, vc), in_specs=[SMEM, VMEM, VMEM]
+        edge_kernel, [((2, CY, NZ), F32)] * 2, (table_back, back, vc), in_specs=[SMEM, VMEM, VMEM]
     )
     from_o, from_e = swap_both(to_o, to_e)
-    (vd,) = call(body_kernel, [EXT], (table, back, vc, to_o, to_e), in_specs=[SMEM] + [VMEM] * 4)
+    (vd,) = call(body_kernel, [EXT], (table_back, back, vc, to_o, to_e), in_specs=[SMEM] + [VMEM] * 4)
 
     last_side = ((CX + 2, 2, NZ), F32)
     to_high, to_low = call(last_side_kernel, [last_side, last_side], (vd, from_o, from_e))

time: 119 us -> 120 us (level); the launches traced: 119 us -> 118 us
  blocking collectives: 82.5 us -> 87.8 us
  waiting for transfers between devices: 8.95 us -> 4.53 us
  starting transfers between devices: 13.5 us -> 11.4 us
    all_to_all x1, blocking collectives: 42 us -> 48.1 us  [cycle(): got = lax.all_to_all(buf.reshape(owners, BLOCK, 1, NZ), 'bulk', 0, 0)]
    ppermute x4, waiting for transfers between devices: 4.31 us -> 0.01 us  [swap_both(): lax.ppermute(values, 'bulk', pairs + [(j, i) for i, j in pairs] + alone)]
    ppermute x4, starting transfers between devices: 9.26 us -> 7.19 us  [swap_both(): lax.ppermute(values, 'bulk', pairs + [(j, i) for i, j in pairs] + alone)]
  transfers between devices with their start and end apart: 8 -> 8, of which waited for: 6 -> 4; matrix products, arithmetic and copies ran while one was open for 0% -> 0% of each run, Pallas kernels for 6% -> 6%
where the time goes in v6:
time: 120 us; the launch traced here: 118 us
  blocking collectives  87.8 us (73%)
  Pallas kernels  13.2 us (11%)
  starting transfers between devices  11.4 us (10%)
  waiting for transfers between devices  4.53 us (4%)
    all_to_all x1, blocking collectives, cycle(): got = lax.all_to_all(buf.reshape(owners, BLOCK, 1, NZ), 'bulk', 0, 0)  48.1 us
    all_to_all x1, blocking collectives, cycle(): lax.all_to_all(back.reshape(owners, CAP, 1, NZ), 'bulk', 0, 0)  39.7 us
    pallas_call x12, Pallas kernels, call(): pl.pallas_call(kernel, out_shape=[jax.ShapeDtypeStruct(s, d) for s, d in...  13.2 us
    ppermute x4, starting transfers between devices, swap_both(): lax.ppermute(values, 'bulk', pairs + [(j, i) for i, j in pairs] + alone)  7.19 us
    ppermute x2, starting transfers between devices, from_both(): high = lax.ppermute(to_low, axis, ring(axis, -1))  3.46 us
    ppermute x2, waiting for transfers between devices, from_both(): high = lax.ppermute(to_low, axis, ring(axis, -1))  3.01 us
  transfers between devices with their start and end apart: 8, of which 4 were waited for; matrix products, arithmetic and copies ran while one was open for 0% of the time, Pallas kernels for 6%

profile of v6, /device:TPU:24, one launch (start us, length us, event | category | flops | bytes accessed | tf_op | source)
XLA Modules:
  0.0 117.8 jit_solution(3482023089947625692)
XLA Ops:
  0.0 1.2 %shard_map.74 = (f32[8,64,128]{2,1,0:T(8,128)S(1)}, f32[8,64,128]{2,1,0:T(8,128)S(1)}) custom-call(f32[16,64,128]{2,1,0:T(8,128)} %p_ref.5, f32[16,64,128]{2,1,0:T(8,128)} %k_ref.5, f32[16,64,128]{2,1,0:T(8,128)} %r_ref.5), custom_call_target="tpu_custom_call" | custom-call | tf_op jit(solution)/shard_map/pallas_call | solution.py:29
  1.3 0.7 collective-permute-start
  2.0 2.9 %collective-permute-start.1 = (f32[8,64,128]{2,1,0:T(8,128)S(1)}, f32[8,64,128]{2,1,0:T(8,128)S(1)}, u32[]{:S(2)}, u32[]{:S(2)}) collective-permute-start(f32[8,64,128]{2,1,0:T(8,128)S(1)} %get-tuple-element.53), channel_id=1, source_target_pairs={{0,4},{8,12},{16,20},{24,28},{32,36},{40,44},{48,52},{56,60},{64,6... | collective-permute-start | bytes 786440 | tf_op jit(solution)/shard_map/ppermute | solution.py:418
  4.9 0.7 copy-done.6
  5.6 0.8 shard_map.73
  6.4 2.4 %shard_map.75 = (f32[2624,128]{1,0:T(8,128)S(1)}, f32[22,80,128]{2,1,0:T(8,128)S(1)}, f32[22,80,128]{2,1,0:T(8,128)S(1)}, f32[22,80,128]{2,1,0:T(8,128)S(1)}, f3...) custom-call(s32[1024]{0:T(1024)S(1)} %bitcast.19, ...), custom_call_target="tpu_custom_call", output_to_operand_aliasing={{0}: (4, {})} | custom-call | tf_op jit(solution)/shard_map/pallas_call | solution.py:29
  9.1 1.8 %collective-permute-start.3 = (f32[20,8,128]{2,1,0:T(8,128)S(1)}, f32[20,8,128]{2,1,0:T(8,128)S(1)}, u32[]{:S(2)}, u32[]{:S(2)}) collective-permute-start(f32[20,8,128]{2,1,0:T(8,128)S(1)} %get-tuple-element.57), channel_id=1, source_target_pairs={{0,3},{1,0},{2,1},{3,2},{4,7},{5,4},{6,5},{7,6},{8,11},{9,8},{10,9... | collective-permute-start | bytes 245768 | tf_op jit(solution)/shard_map/ppermute | solution.py:424
  10.9 1.5 %shard_map.77 = (f32[2624,128]{1,0:T(8,128)S(1)}, f32[22,80,128]{2,1,0:T(8,128)S(1)}, f32[22,80,128]{2,1,0:T(8,128)S(1)}, f32[22,80,128]{2,1,0:T(8,128)S(1)}, f3...) custom-call(s32[1024]{0:T(1024)S(1)} %bitcast.20, ...), custom_call_target="tpu_custom_call", output_to_operand_aliasing={{0}: (3, {}), {1}: (4, {}), {2}: (5, {}), {3}: (6, {}), {4}... | custom-call | tf_op jit(solution)/shard_map/pallas_call | solution.py:29
  12.5 0.9 collective-permute-done.2.sl
  13.3 1.4 %collective-permute-done.3.sh = f32[20,8,128]{2,1,0:T(8,128)S(1)} collective-permute-done((f32[20,8,128]{2,1,0:T(8,128)S(1)}, f32[20,8,128]{2,1,0:T(8,128)S(1)}, u32[]{:S(2)}, u32[]{:S(2)}) %collective-permute-start.3) | collective-permute-done | bytes 81952 | tf_op jit(solution)/shard_map/ppermute | solution.py:424
  14.8 0.9 shard_map.78
  15.7 48.1 %all_to_all.10 = f32[64,41,1,128]{3,2,1,0:T(1,128)S(1)} all-to-all(f32[64,41,1,128]{3,2,1,0:T(1,128)S(1)} %bitcast.12), channel_id=1, replica_groups=mesh['bulk'=64,'slab'=4] {'bulk'}, dimensions={0} | all-to-all | bytes 2686976 | tf_op jit(solution)/shard_map/all_to_all | solution.py:479
  63.8 2.0 %shard_map.79 = f32[2560,128]{1,0:T(8,128)S(1)} custom-call(f32[2624,128]{1,0:T(8,128)S(1)} %bitcast.15, f32[128,128]{1,0:T(8,128)S(1)} %bitcast.17, f32[128,128]{1,0:T(8,128)S(1)} %bitcast.18), custom_call_target="tpu_custom_call" | custom-call | tf_op jit(solution)/shard_map/pallas_call | solution.py:29
  65.8 39.7 %all_to_all.11 = f32[64,40,1,128]{3,1,2,0:T(8,128)S(1)} all-to-all(f32[64,40,1,128]{3,1,2,0:T(8,128)S(1)} %bitcast.16), channel_id=1, replica_groups=mesh['bulk'=64,'slab'=4] {'bulk'}, dimensions={0} | all-to-all | bytes 2621440 | tf_op jit(solution)/shard_map/all_to_all | solution.py:486
  105.5 0.8 shard_map.80
  106.3 0.7 collective-permute-start.4
  107.0 2.9 %collective-permute-start.5 = (f32[2,64,128]{2,1,0:T(8,128)S(1)}, f32[2,64,128]{2,1,0:T(8,128)S(1)}, u32[]{:S(2)}, u32[]{:S(2)}) collective-permute-start(f32[2,64,128]{2,1,0:T(8,128)S(1)} %get-tuple-element.83.to_e), channel_id=1, source_target_pairs={{0,4},{8,12},{16,20},{24,28},{32,36},{40,44},{48,52},{56,60},{64,6... | collective-permute-start | bytes 196616 | tf_op jit(solution)/shard_map/ppermute | solution.py:418
  109.9 1.3 %shard_map.81.vd.vd_in = f32[22,80,128]{2,1,0:T(8,128)S(1)} custom-call(s32[1024]{0:T(1024)S(1)} %bitcast.23, f32[2560,128]{1,0:T(8,128)S(1)} %bitcast.14, f32[22,80,128]{2,1,0:T(8,128)S(1)} %get-tuple-element.81.vc, f32[2,64,128]{2,1,0:T(8,128)S(1)} %get-tuple-element.82.to_o, f32[2,64,128]{2,1,0:T(8,128)S(1)} %get-tuple-element.83.to_e), custom_call_target="tpu_custom_call" | custom-call | tf_op jit(solution)/shard_map/pallas_call | solution.py:29
  111.2 0.4 collective-permute-start.6
  111.7 1.7 %collective-permute-start.7 = (f32[18,2,128]{2,1,0:T(2,128)S(1)}, f32[18,2,128]{2,1,0:T(2,128)S(1)}, u32[]{:S(2)}, u32[]{:S(2)}) collective-permute-start(f32[18,2,128]{2,1,0:T(2,128)S(1)} %get-tuple-element.85), channel_id=1, source_target_pairs={{0,3},{1,0},{2,1},{3,2},{4,7},{5,4},{6,5},{7,6},{8,11},{9,8},{10,9... | collective-permute-start | bytes 55304 | tf_op jit(solution)/shard_map/ppermute | solution.py:424
  113.3 1.1 shard_map.83
  114.5 0.6 collective-permute-done.6.sl
  115.1 1.6 %collective-permute-done.7.sh = f32[18,2,128]{2,1,0:T(2,128)S(1)} collective-permute-done((f32[18,2,128]{2,1,0:T(2,128)S(1)}, f32[18,2,128]{2,1,0:T(2,128)S(1)}, u32[]{:S(2)}, u32[]{:S(2)}) %collective-permute-start.7) | collective-permute-done | bytes 18464 | tf_op jit(solution)/shard_map/ppermute | solution.py:424
  116.7 1.2 shard_map.84
  (20 shorter events, 0.4 us)
Async XLA Ops:
  0.0 6.3 %copy-start = (f32[16,64,128]{2,1,0:T(8,128)S(1)}, f32[16,64,128]{2,1,0:T(8,128)}, u32[]{:S(2)}) copy-start(f32[16,64,128]{2,1,0:T(8,128)} %p_ref.5) | copy-start | bytes 1572868
  0.0 6.3 %copy-start.2 = (f32[16,64,128]{2,1,0:T(8,128)S(1)}, f32[16,64,128]{2,1,0:T(8,128)}, u32[]{:S(2)}) copy-start(f32[16,64,128]{2,1,0:T(8,128)} %r_ref.5) | copy-start | bytes 1572868
  0.0 6.4 %copy-start.1 = (f32[16,64,128]{2,1,0:T(8,128)S(1)}, f32[16,64,128]{2,1,0:T(8,128)}, u32[]{:S(2)}) copy-start(f32[16,64,128]{2,1,0:T(8,128)} %k_ref.5) | copy-start | bytes 1572868
  0.0 4.9 %copy-start.5 = (s32[1,1,1024,1]{2,3,1,0:T(1,128)S(1)}, s32[1,1,1024,1]{2,3,1,0:T(1,128)}, u32[]{:S(2)}) copy-start(s32[1,1,1024,1]{2,3,1,0:T(1,128)} %param.10) | copy-start | bytes 12292
  1.3 7.5 %collective-permute-start = (f32[8,64,128]{2,1,0:T(8,128)S(1)}, f32[8,64,128]{2,1,0:T(8,128)S(1)}, u32[]{:S(2)}, u32[]{:S(2)}) collective-permute-start(f32[8,64,128]{2,1,0:T(8,128)S(1)} %get-tuple-element.52), channel_id=1, source_target_pairs={{4,8},{12,16},{20,24},{28,32},{36,40},{44,48},{52,56},{60,64},{68,... | collective-permute-start | bytes 786440 | tf_op jit(solution)/shard_map/ppermute | solution.py:418
  2.0 6.8 %collective-permute-start.1 = (f32[8,64,128]{2,1,0:T(8,128)S(1)}, f32[8,64,128]{2,1,0:T(8,128)S(1)}, u32[]{:S(2)}, u32[]{:S(2)}) collective-permute-start(f32[8,64,128]{2,1,0:T(8,128)S(1)} %get-tuple-element.53), channel_id=1, source_target_pairs={{0,4},{8,12},{16,20},{24,28},{32,36},{40,44},{48,52},{56,60},{64,6... | collective-permute-start | bytes 786440 | tf_op jit(solution)/shard_map/ppermute | solution.py:418
  4.9 0.7 copy-start.6
  8.8 4.5 %collective-permute-start.2 = (f32[20,8,128]{2,1,0:T(8,128)S(1)}, f32[20,8,128]{2,1,0:T(8,128)S(1)}, u32[]{:S(2)}, u32[]{:S(2)}) collective-permute-start(f32[20,8,128]{2,1,0:T(8,128)S(1)} %get-tuple-element.56), channel_id=1, source_target_pairs={{0,1},{1,2},{2,3},{3,0},{4,5},{5,6},{6,7},{7,4},{8,9},{9,10},{10,1... | collective-permute-start | bytes 245768 | tf_op jit(solution)/shard_map/ppermute | solution.py:423
  9.1 5.7 %collective-permute-start.3 = (f32[20,8,128]{2,1,0:T(8,128)S(1)}, f32[20,8,128]{2,1,0:T(8,128)S(1)}, u32[]{:S(2)}, u32[]{:S(2)}) collective-permute-start(f32[20,8,128]{2,1,0:T(8,128)S(1)} %get-tuple-element.57), channel_id=1, source_target_pairs={{0,3},{1,0},{2,1},{3,2},{4,7},{5,4},{6,5},{7,6},{8,11},{9,8},{10,9... | collective-permute-start | bytes 245768 | tf_op jit(solution)/shard_map/ppermute | solution.py:424
  15.7 48.1 %copy-start.3 = (f32[1,128,128]{2,1,0:T(8,128)S(1)}, f32[1,128,128]{2,1,0:T(8,128)}, u32[]{:S(2)}) copy-start(f32[1,128,128]{2,1,0:T(8,128)} %param.12) | copy-start | bytes 196612
  15.7 48.1 %copy-start.4 = (f32[1,128,128]{2,1,0:T(8,128)S(1)}, f32[1,128,128]{2,1,0:T(8,128)}, u32[]{:S(2)}) copy-start(f32[1,128,128]{2,1,0:T(8,128)} %param.13) | copy-start | bytes 196612
  106.3 4.9 %collective-permute-start.4 = (f32[2,64,128]{2,1,0:T(8,128)S(1)}, f32[2,64,128]{2,1,0:T(8,128)S(1)}, u32[]{:S(2)}, u32[]{:S(2)}) collective-permute-start(f32[2,64,128]{2,1,0:T(8,128)S(1)} %get-tuple-element.82.to_o), channel_id=1, source_target_pairs={{4,8},{12,16},{20,24},{28,32},{36,40},{44,48},{52,56},{60,64},{68,... | collective-permute-start | bytes 196616 | tf_op jit(solution)/shard_map/ppermute | solution.py:418
  107.0 4.2 %collective-permute-start.5 = (f32[2,64,128]{2,1,0:T(8,128)S(1)}, f32[2,64,128]{2,1,0:T(8,128)S(1)}, u32[]{:S(2)}, u32[]{:S(2)}) collective-permute-start(f32[2,64,128]{2,1,0:T(8,128)S(1)} %get-tuple-element.83.to_e), channel_id=1, source_target_pairs={{0,4},{8,12},{16,20},{24,28},{32,36},{40,44},{48,52},{56,60},{64,6... | collective-permute-start | bytes 196616 | tf_op jit(solution)/shard_map/ppermute | solution.py:418
  111.2 3.8 %collective-permute-start.6 = (f32[18,2,128]{2,1,0:T(2,128)S(1)}, f32[18,2,128]{2,1,0:T(2,128)S(1)}, u32[]{:S(2)}, u32[]{:S(2)}) collective-permute-start(f32[18,2,128]{2,1,0:T(2,128)S(1)} %get-tuple-element.84), channel_id=1, source_target_pairs={{0,1},{1,2},{2,3},{3,0},{4,5},{5,6},{6,7},{7,4},{8,9},{9,10},{10,1... | collective-permute-start | bytes 55304 | tf_op jit(solution)/shard_map/ppermute | solution.py:423
  111.7 5.0 %collective-permute-start.7 = (f32[18,2,128]{2,1,0:T(2,128)S(1)}, f32[18,2,128]{2,1,0:T(2,128)S(1)}, u32[]{:S(2)}, u32[]{:S(2)}) collective-permute-start(f32[18,2,128]{2,1,0:T(2,128)S(1)} %get-tuple-element.85), channel_id=1, source_target_pairs={{0,3},{1,0},{2,1},{3,2},{4,7},{5,4},{6,5},{7,6},{8,11},{9,8},{10,9... | collective-permute-start | bytes 55304 | tf_op jit(solution)/shard_map/ppermute | solution.py:424

commit v7 on v6

--- a/solution.py
+++ b/solution.py
@@ -410,12 +410,13 @@
 
 
 def swap_both(to_o, to_e):
-    n = lax.axis_size("bulk")
+    n, m = lax.axis_size("bulk"), lax.axis_size("slab")
     got = []
     for first, values in ((1, to_o), (0, to_e)):
-        pairs = [(i, i + 1) for i in range(first, n - 1, 2)]
-        alone = [(i, i) for i in (0, n - 1)] if first else []
-        got.append(lax.ppermute(values, "bulk", pairs + [(j, i) for i, j in pairs] + alone))
+        pairs = [(i * m + s, (i + 1) * m + s) for i in range(first, n - 1, 2) for s in range(m)]
+        if first:
+            pairs += [(i * m + s, i * m + s + 1) for i in (0, n - 1) for s in range(0, m, 2)]
+        got.append(lax.ppermute(values, ("bulk", "slab"), pairs + [(j, i) for i, j in pairs]))
     return got
 
 

time: 120 us -> 116 us (0.967); the launches traced: 118 us -> 115 us
  waiting for transfers between devices: 4.53 us -> 8.49 us
  starting transfers between devices: 11.4 us -> 7.58 us
  blocking collectives: 87.8 us -> 85.4 us
    ppermute x4, starting transfers between devices: 7.19 us -> 3.37 us  [swap_both(): lax.ppermute(values, ('bulk', 'slab'), pairs + [(j, i) for i, j in pairs])]
    all_to_all x1, blocking collectives: 48.1 us -> 45.6 us  [cycle(): got = lax.all_to_all(buf.reshape(owners, BLOCK, 1, NZ), 'bulk', 0, 0)]
    ppermute x4, waiting for transfers between devices: 0.01 us -> 2.27 us  [swap_both(): lax.ppermute(values, ('bulk', 'slab'), pairs + [(j, i) for i, j in pairs])]
    ppermute x2, starting transfers between devices: 0.75 us -> 2.44 us  [from_both(): low = lax.ppermute(to_high, axis, ring(axis, 1))]
    ppermute x2, waiting for transfers between devices: 3.01 us -> 4.71 us  [from_both(): high = lax.ppermute(to_low, axis, ring(axis, -1))]
    ppermute x2, starting transfers between devices: 3.46 us -> 1.77 us  [from_both(): high = lax.ppermute(to_low, axis, ring(axis, -1))]
  transfers between devices with their start and end apart: 8 -> 8, of which waited for: 4 -> 6; matrix products, arithmetic and copies ran while one was open for 0% -> 0% of each run, Pallas kernels for 6% -> 6%
where the time goes in v7:
time: 116 us; the launch traced here: 115 us
  blocking collectives  85.4 us (74%)
  Pallas kernels  13.2 us (11%)
  waiting for transfers between devices  8.49 us (7%)
  starting transfers between devices  7.58 us (7%)
    all_to_all x1, blocking collectives, cycle(): got = lax.all_to_all(buf.reshape(owners, BLOCK, 1, NZ), 'bulk', 0, 0)  45.6 us
    all_to_all x1, blocking collectives, cycle(): lax.all_to_all(back.reshape(owners, CAP, 1, NZ), 'bulk', 0, 0)  39.7 us
    pallas_call x12, Pallas kernels, call(): pl.pallas_call(kernel, out_shape=[jax.ShapeDtypeStruct(s, d) for s, d in...  13.2 us
    ppermute x2, waiting for transfers between devices, from_both(): high = lax.ppermute(to_low, axis, ring(axis, -1))  4.71 us
    ppermute x4, starting transfers between devices, swap_both(): lax.ppermute(values, ('bulk', 'slab'), pairs + [(j, i) for i, j in pairs])  3.37 us
    ppermute x2, starting transfers between devices, from_both(): low = lax.ppermute(to_high, axis, ring(axis, 1))  2.44 us
  transfers between devices with their start and end apart: 8, of which 6 were waited for; matrix products, arithmetic and copies ran while one was open for 0% of the time, Pallas kernels for 6%

profile of v7, /device:TPU:24, one launch (start us, length us, event | category | flops | bytes accessed | tf_op | source)
XLA Modules:
  0.0 115.5 jit_solution(2271796642228200125)
XLA Ops:
  0.0 1.2 %shard_map.74 = (f32[8,64,128]{2,1,0:T(8,128)S(1)}, f32[8,64,128]{2,1,0:T(8,128)S(1)}) custom-call(f32[16,64,128]{2,1,0:T(8,128)} %p_ref.5, f32[16,64,128]{2,1,0:T(8,128)} %k_ref.5, f32[16,64,128]{2,1,0:T(8,128)} %r_ref.5), custom_call_target="tpu_custom_call" | custom-call | tf_op jit(solution)/shard_map/pallas_call | solution.py:29
  1.3 0.8 collective-permute-start
  2.1 0.9 collective-permute-start.1
  3.0 0.7 copy-done.6
  3.7 0.8 shard_map.73
  4.5 2.4 %shard_map.75 = (f32[2624,128]{1,0:T(8,128)S(1)}, f32[22,80,128]{2,1,0:T(8,128)S(1)}, f32[22,80,128]{2,1,0:T(8,128)S(1)}, f32[22,80,128]{2,1,0:T(8,128)S(1)}, f3...) custom-call(s32[1024]{0:T(1024)S(1)} %bitcast.19, ...), custom_call_target="tpu_custom_call", output_to_operand_aliasing={{0}: (4, {})} | custom-call | tf_op jit(solution)/shard_map/pallas_call | solution.py:29
  6.8 0.9 collective-permute-done.from_o
  7.8 2.0 %collective-permute-start.2 = (f32[20,8,128]{2,1,0:T(8,128)S(1)}, f32[20,8,128]{2,1,0:T(8,128)S(1)}, u32[]{:S(2)}, u32[]{:S(2)}) collective-permute-start(f32[20,8,128]{2,1,0:T(8,128)S(1)} %get-tuple-element.56), channel_id=1, source_target_pairs={{0,1},{1,2},{2,3},{3,0},{4,5},{5,6},{6,7},{7,4},{8,9},{9,10},{10,1... | collective-permute-start | bytes 245768 | tf_op jit(solution)/shard_map/ppermute | solution.py:424
  9.9 1.5 %shard_map.77 = (f32[2624,128]{1,0:T(8,128)S(1)}, f32[22,80,128]{2,1,0:T(8,128)S(1)}, f32[22,80,128]{2,1,0:T(8,128)S(1)}, f32[22,80,128]{2,1,0:T(8,128)S(1)}, f3...) custom-call(s32[1024]{0:T(1024)S(1)} %bitcast.20, ...), custom_call_target="tpu_custom_call", output_to_operand_aliasing={{0}: (3, {}), {1}: (4, {}), {2}: (5, {}), {3}: (6, {}), {4}... | custom-call | tf_op jit(solution)/shard_map/pallas_call | solution.py:29
  11.4 0.9 collective-permute-done.2.sl
  12.3 3.1 %collective-permute-done.3.sh = f32[20,8,128]{2,1,0:T(8,128)S(1)} collective-permute-done((f32[20,8,128]{2,1,0:T(8,128)S(1)}, f32[20,8,128]{2,1,0:T(8,128)S(1)}, u32[]{:S(2)}, u32[]{:S(2)}) %collective-permute-start.3) | collective-permute-done | bytes 81952 | tf_op jit(solution)/shard_map/ppermute | solution.py:425
  15.4 0.9 shard_map.78
  16.4 45.6 %all_to_all.10 = f32[64,41,1,128]{3,2,1,0:T(1,128)S(1)} all-to-all(f32[64,41,1,128]{3,2,1,0:T(1,128)S(1)} %bitcast.12), channel_id=1, replica_groups=mesh['bulk'=64,'slab'=4] {'bulk'}, dimensions={0} | all-to-all | bytes 2686976 | tf_op jit(solution)/shard_map/all_to_all | solution.py:480
  62.0 2.0 %shard_map.79 = f32[2560,128]{1,0:T(8,128)S(1)} custom-call(f32[2624,128]{1,0:T(8,128)S(1)} %bitcast.15, f32[128,128]{1,0:T(8,128)S(1)} %bitcast.17, f32[128,128]{1,0:T(8,128)S(1)} %bitcast.18), custom_call_target="tpu_custom_call" | custom-call | tf_op jit(solution)/shard_map/pallas_call | solution.py:29
  64.0 39.7 %all_to_all.11 = f32[64,40,1,128]{3,1,2,0:T(8,128)S(1)} all-to-all(f32[64,40,1,128]{3,1,2,0:T(8,128)S(1)} %bitcast.16), channel_id=1, replica_groups=mesh['bulk'=64,'slab'=4] {'bulk'}, dimensions={0} | all-to-all | bytes 2621440 | tf_op jit(solution)/shard_map/all_to_all | solution.py:487
  103.7 0.8 shard_map.80
  104.5 0.7 collective-permute-start.4
  105.2 1.0 collective-permute-start.5
  106.2 1.3 %shard_map.81.vd.vd_in = f32[22,80,128]{2,1,0:T(8,128)S(1)} custom-call(s32[1024]{0:T(1024)S(1)} %bitcast.23, f32[2560,128]{1,0:T(8,128)S(1)} %bitcast.14, f32[22,80,128]{2,1,0:T(8,128)S(1)} %get-tuple-element.81.vc, f32[2,64,128]{2,1,0:T(8,128)S(1)} %get-tuple-element.82.to_o, f32[2,64,128]{2,1,0:T(8,128)S(1)} %get-tuple-element.83.to_e), custom_call_target="tpu_custom_call" | custom-call | tf_op jit(solution)/shard_map/pallas_call | solution.py:29
  107.5 1.4 %collective-permute-done.4.from_o = f32[2,64,128]{2,1,0:T(8,128)S(1)} collective-permute-done((f32[2,64,128]{2,1,0:T(8,128)S(1)}, f32[2,64,128]{2,1,0:T(8,128)S(1)}, u32[]{:S(2)}, u32[]{:S(2)}) %collective-permute-start.4) | collective-permute-done | bytes 65568 | tf_op jit(solution)/shard_map/ppermute | solution.py:419
  109.3 1.7 %collective-permute-start.7 = (f32[18,2,128]{2,1,0:T(2,128)S(1)}, f32[18,2,128]{2,1,0:T(2,128)S(1)}, u32[]{:S(2)}, u32[]{:S(2)}) collective-permute-start(f32[18,2,128]{2,1,0:T(2,128)S(1)} %get-tuple-element.85), channel_id=1, source_target_pairs={{0,3},{1,0},{2,1},{3,2},{4,7},{5,4},{6,5},{7,6},{8,11},{9,8},{10,9... | collective-permute-start | bytes 55304 | tf_op jit(solution)/shard_map/ppermute | solution.py:425
  111.0 1.1 shard_map.83
  112.7 1.6 %collective-permute-done.7.sh = f32[18,2,128]{2,1,0:T(2,128)S(1)} collective-permute-done((f32[18,2,128]{2,1,0:T(2,128)S(1)}, f32[18,2,128]{2,1,0:T(2,128)S(1)}, u32[]{:S(2)}, u32[]{:S(2)}) %collective-permute-start.7) | collective-permute-done | bytes 18464 | tf_op jit(solution)/shard_map/ppermute | solution.py:425
  114.3 1.2 %shard_map.84 = (f32[22,80,128]{2,1,0:T(8,128)S(1)}, f32[22,80,128]{2,1,0:T(8,128)S(1)}, f32[16,64,128]{2,1,0:T(8,128)}) custom-call(f32[18,2,128]{2,1,0:T(2,128)S(1)} %collective-permute-done.6.sl, f32[18,2,128]{2,1,0:T(2,128)S(1)} %collective-permute-done.7.sh, ...), custom_call_target="tpu_custom_call", output_to_operand_aliasing={{0}: (2, {}), {1}: (3, {})} | custom-call | tf_op jit(solution)/shard_map/pallas_call | solution.py:29
  (20 shorter events, 1.3 us)
Async XLA Ops:
  0.0 4.4 %copy-start = (f32[16,64,128]{2,1,0:T(8,128)S(1)}, f32[16,64,128]{2,1,0:T(8,128)}, u32[]{:S(2)}) copy-start(f32[16,64,128]{2,1,0:T(8,128)} %p_ref.5) | copy-start | bytes 1572868
  0.0 4.4 %copy-start.2 = (f32[16,64,128]{2,1,0:T(8,128)S(1)}, f32[16,64,128]{2,1,0:T(8,128)}, u32[]{:S(2)}) copy-start(f32[16,64,128]{2,1,0:T(8,128)} %r_ref.5) | copy-start | bytes 1572868
  0.0 4.4 %copy-start.1 = (f32[16,64,128]{2,1,0:T(8,128)S(1)}, f32[16,64,128]{2,1,0:T(8,128)}, u32[]{:S(2)}) copy-start(f32[16,64,128]{2,1,0:T(8,128)} %k_ref.5) | copy-start | bytes 1572868
  0.0 3.0 %copy-start.5 = (s32[1,1,1024,1]{2,3,1,0:T(1,128)S(1)}, s32[1,1,1024,1]{2,3,1,0:T(1,128)}, u32[]{:S(2)}) copy-start(s32[1,1,1024,1]{2,3,1,0:T(1,128)} %param.10) | copy-start | bytes 12292
  1.3 6.5 %collective-permute-start = (f32[8,64,128]{2,1,0:T(8,128)S(1)}, f32[8,64,128]{2,1,0:T(8,128)S(1)}, u32[]{:S(2)}, u32[]{:S(2)}) collective-permute-start(f32[8,64,128]{2,1,0:T(8,128)S(1)} %get-tuple-element.52), channel_id=1, source_target_pairs={{4,8},{5,9},{6,10},{7,11},{12,16},{13,17},{14,18},{15,19},{20,24},... | collective-permute-start | bytes 786440 | tf_op jit(solution)/shard_map/ppermute | solution.py:419
  2.1 5.6 %collective-permute-start.1 = (f32[8,64,128]{2,1,0:T(8,128)S(1)}, f32[8,64,128]{2,1,0:T(8,128)S(1)}, u32[]{:S(2)}, u32[]{:S(2)}) collective-permute-start(f32[8,64,128]{2,1,0:T(8,128)S(1)} %get-tuple-element.53), channel_id=1, source_target_pairs={{0,4},{1,5},{2,6},{3,7},{8,12},{9,13},{10,14},{11,15},{16,20},{17,... | collective-permute-start | bytes 786440 | tf_op jit(solution)/shard_map/ppermute | solution.py:419
  3.0 0.7 copy-start.6
  7.8 4.5 %collective-permute-start.2 = (f32[20,8,128]{2,1,0:T(8,128)S(1)}, f32[20,8,128]{2,1,0:T(8,128)S(1)}, u32[]{:S(2)}, u32[]{:S(2)}) collective-permute-start(f32[20,8,128]{2,1,0:T(8,128)S(1)} %get-tuple-element.56), channel_id=1, source_target_pairs={{0,1},{1,2},{2,3},{3,0},{4,5},{5,6},{6,7},{7,4},{8,9},{9,10},{10,1... | collective-permute-start | bytes 245768 | tf_op jit(solution)/shard_map/ppermute | solution.py:424
  9.8 5.7 %collective-permute-start.3 = (f32[20,8,128]{2,1,0:T(8,128)S(1)}, f32[20,8,128]{2,1,0:T(8,128)S(1)}, u32[]{:S(2)}, u32[]{:S(2)}) collective-permute-start(f32[20,8,128]{2,1,0:T(8,128)S(1)} %get-tuple-element.57), channel_id=1, source_target_pairs={{0,3},{1,0},{2,1},{3,2},{4,7},{5,4},{6,5},{7,6},{8,11},{9,8},{10,9... | collective-permute-start | bytes 245768 | tf_op jit(solution)/shard_map/ppermute | solution.py:425
  16.3 45.7 %copy-start.3 = (f32[1,128,128]{2,1,0:T(8,128)S(1)}, f32[1,128,128]{2,1,0:T(8,128)}, u32[]{:S(2)}) copy-start(f32[1,128,128]{2,1,0:T(8,128)} %param.12) | copy-start | bytes 196612
  16.3 45.7 %copy-start.4 = (f32[1,128,128]{2,1,0:T(8,128)S(1)}, f32[1,128,128]{2,1,0:T(8,128)}, u32[]{:S(2)}) copy-start(f32[1,128,128]{2,1,0:T(8,128)} %param.13) | copy-start | bytes 196612
  104.5 4.4 %collective-permute-start.4 = (f32[2,64,128]{2,1,0:T(8,128)S(1)}, f32[2,64,128]{2,1,0:T(8,128)S(1)}, u32[]{:S(2)}, u32[]{:S(2)}) collective-permute-start(f32[2,64,128]{2,1,0:T(8,128)S(1)} %get-tuple-element.82.to_o), channel_id=1, source_target_pairs={{4,8},{5,9},{6,10},{7,11},{12,16},{13,17},{14,18},{15,19},{20,24},... | collective-permute-start | bytes 196616 | tf_op jit(solution)/shard_map/ppermute | solution.py:419
  105.2 3.7 %collective-permute-start.5 = (f32[2,64,128]{2,1,0:T(8,128)S(1)}, f32[2,64,128]{2,1,0:T(8,128)S(1)}, u32[]{:S(2)}, u32[]{:S(2)}) collective-permute-start(f32[2,64,128]{2,1,0:T(8,128)S(1)} %get-tuple-element.83.to_e), channel_id=1, source_target_pairs={{0,4},{1,5},{2,6},{3,7},{8,12},{9,13},{10,14},{11,15},{16,20},{17,... | collective-permute-start | bytes 196616 | tf_op jit(solution)/shard_map/ppermute | solution.py:419
  108.9 3.8 %collective-permute-start.6 = (f32[18,2,128]{2,1,0:T(2,128)S(1)}, f32[18,2,128]{2,1,0:T(2,128)S(1)}, u32[]{:S(2)}, u32[]{:S(2)}) collective-permute-start(f32[18,2,128]{2,1,0:T(2,128)S(1)} %get-tuple-element.84), channel_id=1, source_target_pairs={{0,1},{1,2},{2,3},{3,0},{4,5},{5,6},{6,7},{7,4},{8,9},{9,10},{10,1... | collective-permute-start | bytes 55304 | tf_op jit(solution)/shard_map/ppermute | solution.py:424
  109.3 5.0 %collective-permute-start.7 = (f32[18,2,128]{2,1,0:T(2,128)S(1)}, f32[18,2,128]{2,1,0:T(2,128)S(1)}, u32[]{:S(2)}, u32[]{:S(2)}) collective-permute-start(f32[18,2,128]{2,1,0:T(2,128)S(1)} %get-tuple-element.85), channel_id=1, source_target_pairs={{0,3},{1,0},{2,1},{3,2},{4,7},{5,4},{6,5},{7,6},{8,11},{9,8},{10,9... | collective-permute-start | bytes 55304 | tf_op jit(solution)/shard_map/ppermute | solution.py:425

commit v8 on v7

--- a/solution.py
+++ b/solution.py
@@ -274,7 +274,6 @@
     groups = -(-owners // 3)
     pairs = -(-groups // 2)
     number = (iota((CR, 128), 0) + 1).astype(F32)
-    total = jnp.zeros((CR, 3 * NZ), F32)
     for g in range(groups):
         base = g * TRIO
         names = [data[base + t * BLOCK + CAP : base + (t + 1) * BLOCK, :] for t in range(min(3, owners - 3 * g))]
@@ -287,15 +286,12 @@
             base = rows - 128
         at = g % 2 * 128
         hot_back[g // 2, :, at : at + 128] = jnp.where(number == name_back, 1.0, 0.0).astype(BF16)
-        hot[g // 2, :, at : at + 128] = jnp.where(number == name, 1.0, 0.0).astype(BF16)
+        hot[:, g * 128 : (g + 1) * 128] = jnp.where(number == name, 1.0, 0.0).astype(BF16)
         for i, part in enumerate(parts_of(data[base : base + 128, :])):
-            parts[g // 2, at : at + 128, i * NZ : (i + 1) * NZ] = part
+            parts[g * 128 : (g + 1) * 128, i * NZ : (i + 1) * NZ] = part
     if groups % 2:
-        hot[pairs - 1, :, 128:] = jnp.zeros((CR, 128), BF16)
         hot_back[pairs - 1, :, 128:] = jnp.zeros((CR, 128), BF16)
-        parts[pairs - 1, 128:, :] = jnp.zeros((128, 3 * NZ), BF16)
-    for p in range(pairs):
-        total = total + jnp.dot(hot[p], parts[p], preferred_element_type=F32)
+    total = jnp.dot(hot[...], parts[...], preferred_element_type=F32)
     total = total[:, 0:NZ] + (total[:, NZ : 2 * NZ] + total[:, 2 * NZ :])
 
     z = iota((CR, NZ), 1)
@@ -482,7 +478,11 @@
         lambda *refs: coarse_kernel(owners, *refs),
         [((owners * CAP, NZ), F32)],
         (got.reshape(slots, NZ), coarse_leak[0], coarse_link[0]),
-        scratch=[pltpu.VMEM((-(-owners // 6), CR, 256), BF16), pltpu.VMEM((-(-owners // 6), CR, 256), BF16), pltpu.VMEM((-(-owners // 6), 256, 3 * NZ), BF16)],
+        scratch=[
+            pltpu.VMEM((CR, -(-owners // 3) * 128), BF16),
+            pltpu.VMEM((-(-owners // 6), CR, 256), BF16),
+            pltpu.VMEM((-(-owners // 3) * 128, 3 * NZ), BF16),
+        ],
     )
     back = lax.all_to_all(back.reshape(owners, CAP, 1, NZ), "bulk", 0, 0).reshape(owners * CAP, NZ)
     to_o, to_e = call(

time: 116 us -> 116 us (level)
  no operation moved by 1% of the time
where the time goes in v8:
time: 116 us; the launch traced here: 115 us
  blocking collectives  85.4 us (74%)
  Pallas kernels  13.2 us (11%)
  waiting for transfers between devices  8.49 us (7%)
  starting transfers between devices  7.58 us (7%)
    all_to_all x1, blocking collectives, cycle(): got = lax.all_to_all(buf.reshape(owners, BLOCK, 1, NZ), 'bulk', 0, 0)  45.6 us
    all_to_all x1, blocking collectives, cycle(): lax.all_to_all(back.reshape(owners, CAP, 1, NZ), 'bulk', 0, 0)  39.7 us
    pallas_call x12, Pallas kernels, call(): pl.pallas_call(kernel, out_shape=[jax.ShapeDtypeStruct(s, d) for s, d in...  13.2 us
    ppermute x2, waiting for transfers between devices, from_both(): high = lax.ppermute(to_low, axis, ring(axis, -1))  4.71 us
    ppermute x4, starting transfers between devices, swap_both(): lax.ppermute(values, ('bulk', 'slab'), pairs + [(j, i) for i, j in pairs])  3.37 us
    ppermute x2, starting transfers between devices, from_both(): low = lax.ppermute(to_high, axis, ring(axis, 1))  2.44 us
  transfers between devices with their start and end apart: 8, of which 6 were waited for; matrix products, arithmetic and copies ran while one was open for 0% of the time, Pallas kernels for 6%

profile of v8, /device:TPU:24, one launch (start us, length us, event | category | flops | bytes accessed | tf_op | source)
XLA Modules:
  0.0 115.5 jit_solution(15885700052406985398)
XLA Ops:
  0.0 1.2 %shard_map.74 = (f32[8,64,128]{2,1,0:T(8,128)S(1)}, f32[8,64,128]{2,1,0:T(8,128)S(1)}) custom-call(f32[16,64,128]{2,1,0:T(8,128)} %p_ref.5, f32[16,64,128]{2,1,0:T(8,128)} %k_ref.5, f32[16,64,128]{2,1,0:T(8,128)} %r_ref.5), custom_call_target="tpu_custom_call" | custom-call | tf_op jit(solution)/shard_map/pallas_call | solution.py:29
  1.3 0.8 collective-permute-start
  2.1 0.9 collective-permute-start.1
  3.0 0.7 copy-done.6
  3.7 0.8 shard_map.73
  4.5 2.4 %shard_map.75 = (f32[2624,128]{1,0:T(8,128)S(1)}, f32[22,80,128]{2,1,0:T(8,128)S(1)}, f32[22,80,128]{2,1,0:T(8,128)S(1)}, f32[22,80,128]{2,1,0:T(8,128)S(1)}, f3...) custom-call(s32[1024]{0:T(1024)S(1)} %bitcast.19, ...), custom_call_target="tpu_custom_call", output_to_operand_aliasing={{0}: (4, {})} | custom-call | tf_op jit(solution)/shard_map/pallas_call | solution.py:29
  6.8 0.9 collective-permute-done.from_o
  7.8 2.0 %collective-permute-start.2 = (f32[20,8,128]{2,1,0:T(8,128)S(1)}, f32[20,8,128]{2,1,0:T(8,128)S(1)}, u32[]{:S(2)}, u32[]{:S(2)}) collective-permute-start(f32[20,8,128]{2,1,0:T(8,128)S(1)} %get-tuple-element.56), channel_id=1, source_target_pairs={{0,1},{1,2},{2,3},{3,0},{4,5},{5,6},{6,7},{7,4},{8,9},{9,10},{10,1... | collective-permute-start | bytes 245768 | tf_op jit(solution)/shard_map/ppermute | solution.py:420
  9.9 1.5 %shard_map.77 = (f32[2624,128]{1,0:T(8,128)S(1)}, f32[22,80,128]{2,1,0:T(8,128)S(1)}, f32[22,80,128]{2,1,0:T(8,128)S(1)}, f32[22,80,128]{2,1,0:T(8,128)S(1)}, f3...) custom-call(s32[1024]{0:T(1024)S(1)} %bitcast.20, ...), custom_call_target="tpu_custom_call", output_to_operand_aliasing={{0}: (3, {}), {1}: (4, {}), {2}: (5, {}), {3}: (6, {}), {4}... | custom-call | tf_op jit(solution)/shard_map/pallas_call | solution.py:29
  11.4 0.9 collective-permute-done.2.sl
  12.3 3.1 %collective-permute-done.3.sh = f32[20,8,128]{2,1,0:T(8,128)S(1)} collective-permute-done((f32[20,8,128]{2,1,0:T(8,128)S(1)}, f32[20,8,128]{2,1,0:T(8,128)S(1)}, u32[]{:S(2)}, u32[]{:S(2)}) %collective-permute-start.3) | collective-permute-done | bytes 81952 | tf_op jit(solution)/shard_map/ppermute | solution.py:421
  15.4 0.9 shard_map.78
  16.4 45.6 %all_to_all.10 = f32[64,41,1,128]{3,2,1,0:T(1,128)S(1)} all-to-all(f32[64,41,1,128]{3,2,1,0:T(1,128)S(1)} %bitcast.12), channel_id=1, replica_groups=mesh['bulk'=64,'slab'=4] {'bulk'}, dimensions={0} | all-to-all | bytes 2686976 | tf_op jit(solution)/shard_map/all_to_all | solution.py:476
  62.0 1.9 %shard_map.79 = f32[2560,128]{1,0:T(8,128)S(1)} custom-call(f32[2624,128]{1,0:T(8,128)S(1)} %bitcast.15, f32[128,128]{1,0:T(8,128)S(1)} %bitcast.17, f32[128,128]{1,0:T(8,128)S(1)} %bitcast.18), custom_call_target="tpu_custom_call" | custom-call | tf_op jit(solution)/shard_map/pallas_call | solution.py:29
  63.9 39.7 %all_to_all.11 = f32[64,40,1,128]{3,1,2,0:T(8,128)S(1)} all-to-all(f32[64,40,1,128]{3,1,2,0:T(8,128)S(1)} %bitcast.16), channel_id=1, replica_groups=mesh['bulk'=64,'slab'=4] {'bulk'}, dimensions={0} | all-to-all | bytes 2621440 | tf_op jit(solution)/shard_map/all_to_all | solution.py:487
  103.7 0.8 shard_map.80
  104.5 0.7 collective-permute-start.4
  105.2 1.0 collective-permute-start.5
  106.2 1.3 %shard_map.81.vd.vd_in = f32[22,80,128]{2,1,0:T(8,128)S(1)} custom-call(s32[1024]{0:T(1024)S(1)} %bitcast.23, f32[2560,128]{1,0:T(8,128)S(1)} %bitcast.14, f32[22,80,128]{2,1,0:T(8,128)S(1)} %get-tuple-element.81.vc, f32[2,64,128]{2,1,0:T(8,128)S(1)} %get-tuple-element.82.to_o, f32[2,64,128]{2,1,0:T(8,128)S(1)} %get-tuple-element.83.to_e), custom_call_target="tpu_custom_call" | custom-call | tf_op jit(solution)/shard_map/pallas_call | solution.py:29
  107.5 1.4 %collective-permute-done.4.from_o = f32[2,64,128]{2,1,0:T(8,128)S(1)} collective-permute-done((f32[2,64,128]{2,1,0:T(8,128)S(1)}, f32[2,64,128]{2,1,0:T(8,128)S(1)}, u32[]{:S(2)}, u32[]{:S(2)}) %collective-permute-start.4) | collective-permute-done | bytes 65568 | tf_op jit(solution)/shard_map/ppermute | solution.py:415
  109.3 1.7 %collective-permute-start.7 = (f32[18,2,128]{2,1,0:T(2,128)S(1)}, f32[18,2,128]{2,1,0:T(2,128)S(1)}, u32[]{:S(2)}, u32[]{:S(2)}) collective-permute-start(f32[18,2,128]{2,1,0:T(2,128)S(1)} %get-tuple-element.85), channel_id=1, source_target_pairs={{0,3},{1,0},{2,1},{3,2},{4,7},{5,4},{6,5},{7,6},{8,11},{9,8},{10,9... | collective-permute-start | bytes 55304 | tf_op jit(solution)/shard_map/ppermute | solution.py:421
  111.0 1.1 shard_map.83
  112.7 1.6 %collective-permute-done.7.sh = f32[18,2,128]{2,1,0:T(2,128)S(1)} collective-permute-done((f32[18,2,128]{2,1,0:T(2,128)S(1)}, f32[18,2,128]{2,1,0:T(2,128)S(1)}, u32[]{:S(2)}, u32[]{:S(2)}) %collective-permute-start.7) | collective-permute-done | bytes 18464 | tf_op jit(solution)/shard_map/ppermute | solution.py:421
  114.3 1.2 %shard_map.84 = (f32[22,80,128]{2,1,0:T(8,128)S(1)}, f32[22,80,128]{2,1,0:T(8,128)S(1)}, f32[16,64,128]{2,1,0:T(8,128)}) custom-call(f32[18,2,128]{2,1,0:T(2,128)S(1)} %collective-permute-done.6.sl, f32[18,2,128]{2,1,0:T(2,128)S(1)} %collective-permute-done.7.sh, ...), custom_call_target="tpu_custom_call", output_to_operand_aliasing={{0}: (2, {}), {1}: (3, {})} | custom-call | tf_op jit(solution)/shard_map/pallas_call | solution.py:29
  (20 shorter events, 1.3 us)
Async XLA Ops:
  0.0 4.4 %copy-start = (f32[16,64,128]{2,1,0:T(8,128)S(1)}, f32[16,64,128]{2,1,0:T(8,128)}, u32[]{:S(2)}) copy-start(f32[16,64,128]{2,1,0:T(8,128)} %p_ref.5) | copy-start | bytes 1572868
  0.0 4.4 %copy-start.2 = (f32[16,64,128]{2,1,0:T(8,128)S(1)}, f32[16,64,128]{2,1,0:T(8,128)}, u32[]{:S(2)}) copy-start(f32[16,64,128]{2,1,0:T(8,128)} %r_ref.5) | copy-start | bytes 1572868
  0.0 4.4 %copy-start.1 = (f32[16,64,128]{2,1,0:T(8,128)S(1)}, f32[16,64,128]{2,1,0:T(8,128)}, u32[]{:S(2)}) copy-start(f32[16,64,128]{2,1,0:T(8,128)} %k_ref.5) | copy-start | bytes 1572868
  0.0 3.0 %copy-start.5 = (s32[1,1,1024,1]{2,3,1,0:T(1,128)S(1)}, s32[1,1,1024,1]{2,3,1,0:T(1,128)}, u32[]{:S(2)}) copy-start(s32[1,1,1024,1]{2,3,1,0:T(1,128)} %param.10) | copy-start | bytes 12292
  1.3 6.5 %collective-permute-start = (f32[8,64,128]{2,1,0:T(8,128)S(1)}, f32[8,64,128]{2,1,0:T(8,128)S(1)}, u32[]{:S(2)}, u32[]{:S(2)}) collective-permute-start(f32[8,64,128]{2,1,0:T(8,128)S(1)} %get-tuple-element.52), channel_id=1, source_target_pairs={{4,8},{5,9},{6,10},{7,11},{12,16},{13,17},{14,18},{15,19},{20,24},... | collective-permute-start | bytes 786440 | tf_op jit(solution)/shard_map/ppermute | solution.py:415
  2.1 5.6 %collective-permute-start.1 = (f32[8,64,128]{2,1,0:T(8,128)S(1)}, f32[8,64,128]{2,1,0:T(8,128)S(1)}, u32[]{:S(2)}, u32[]{:S(2)}) collective-permute-start(f32[8,64,128]{2,1,0:T(8,128)S(1)} %get-tuple-element.53), channel_id=1, source_target_pairs={{0,4},{1,5},{2,6},{3,7},{8,12},{9,13},{10,14},{11,15},{16,20},{17,... | collective-permute-start | bytes 786440 | tf_op jit(solution)/shard_map/ppermute | solution.py:415
  3.0 0.7 copy-start.6
  7.8 4.5 %collective-permute-start.2 = (f32[20,8,128]{2,1,0:T(8,128)S(1)}, f32[20,8,128]{2,1,0:T(8,128)S(1)}, u32[]{:S(2)}, u32[]{:S(2)}) collective-permute-start(f32[20,8,128]{2,1,0:T(8,128)S(1)} %get-tuple-element.56), channel_id=1, source_target_pairs={{0,1},{1,2},{2,3},{3,0},{4,5},{5,6},{6,7},{7,4},{8,9},{9,10},{10,1... | collective-permute-start | bytes 245768 | tf_op jit(solution)/shard_map/ppermute | solution.py:420
  9.8 5.7 %collective-permute-start.3 = (f32[20,8,128]{2,1,0:T(8,128)S(1)}, f32[20,8,128]{2,1,0:T(8,128)S(1)}, u32[]{:S(2)}, u32[]{:S(2)}) collective-permute-start(f32[20,8,128]{2,1,0:T(8,128)S(1)} %get-tuple-element.57), channel_id=1, source_target_pairs={{0,3},{1,0},{2,1},{3,2},{4,7},{5,4},{6,5},{7,6},{8,11},{9,8},{10,9... | collective-permute-start | bytes 245768 | tf_op jit(solution)/shard_map/ppermute | solution.py:421
  16.3 45.7 %copy-start.3 = (f32[1,128,128]{2,1,0:T(8,128)S(1)}, f32[1,128,128]{2,1,0:T(8,128)}, u32[]{:S(2)}) copy-start(f32[1,128,128]{2,1,0:T(8,128)} %param.12) | copy-start | bytes 196612
  16.3 45.7 %copy-start.4 = (f32[1,128,128]{2,1,0:T(8,128)S(1)}, f32[1,128,128]{2,1,0:T(8,128)}, u32[]{:S(2)}) copy-start(f32[1,128,128]{2,1,0:T(8,128)} %param.13) | copy-start | bytes 196612
  104.5 4.4 %collective-permute-start.4 = (f32[2,64,128]{2,1,0:T(8,128)S(1)}, f32[2,64,128]{2,1,0:T(8,128)S(1)}, u32[]{:S(2)}, u32[]{:S(2)}) collective-permute-start(f32[2,64,128]{2,1,0:T(8,128)S(1)} %get-tuple-element.82.to_o), channel_id=1, source_target_pairs={{4,8},{5,9},{6,10},{7,11},{12,16},{13,17},{14,18},{15,19},{20,24},... | collective-permute-start | bytes 196616 | tf_op jit(solution)/shard_map/ppermute | solution.py:415
  105.2 3.7 %collective-permute-start.5 = (f32[2,64,128]{2,1,0:T(8,128)S(1)}, f32[2,64,128]{2,1,0:T(8,128)S(1)}, u32[]{:S(2)}, u32[]{:S(2)}) collective-permute-start(f32[2,64,128]{2,1,0:T(8,128)S(1)} %get-tuple-element.83.to_e), channel_id=1, source_target_pairs={{0,4},{1,5},{2,6},{3,7},{8,12},{9,13},{10,14},{11,15},{16,20},{17,... | collective-permute-start | bytes 196616 | tf_op jit(solution)/shard_map/ppermute | solution.py:415
  108.9 3.8 %collective-permute-start.6 = (f32[18,2,128]{2,1,0:T(2,128)S(1)}, f32[18,2,128]{2,1,0:T(2,128)S(1)}, u32[]{:S(2)}, u32[]{:S(2)}) collective-permute-start(f32[18,2,128]{2,1,0:T(2,128)S(1)} %get-tuple-element.84), channel_id=1, source_target_pairs={{0,1},{1,2},{2,3},{3,0},{4,5},{5,6},{6,7},{7,4},{8,9},{9,10},{10,1... | collective-permute-start | bytes 55304 | tf_op jit(solution)/shard_map/ppermute | solution.py:420
  109.3 5.0 %collective-permute-start.7 = (f32[18,2,128]{2,1,0:T(2,128)S(1)}, f32[18,2,128]{2,1,0:T(2,128)S(1)}, u32[]{:S(2)}, u32[]{:S(2)}) collective-permute-start(f32[18,2,128]{2,1,0:T(2,128)S(1)} %get-tuple-element.85), channel_id=1, source_target_pairs={{0,3},{1,0},{2,1},{3,2},{4,7},{5,4},{6,5},{7,6},{8,11},{9,8},{10,9... | collective-permute-start | bytes 55304 | tf_op jit(solution)/shard_map/ppermute | solution.py:421
